TPU v7x, 512 devices: a whole 4x4x16 slice. The times are simulated.
512 devices in a mesh: gx: 8 (over z_lo), gy: 8 (over y, core), gz: 8 (over x, z_hi).
Axes of the slice: x: 4, y: 4, z: 16 (z_hi: 2, z_lo: 8; z = z_hi * 8 + z_lo), core: 2. Of those that a mesh axis runs over, the one named last changes fastest.
Arguments:
- positions_now: float32 [64, 32, 8, 4, 128], P('gx', 'gy', 'gz'), may hold values from 0 to 1
- velocities: float32 [64, 32, 8, 3, 128], P('gx', 'gy', 'gz'), may hold values from -6 to 6
- positions_next: float32 [64, 32, 8, 3, 128], P('gx', 'gy', 'gz'), may hold values from 0 to 1
- halo_counts: int32 [64, 32, 8], P('gx', 'gy', 'gz'), may hold values from 1 to 128, as said below
- neighbour_lists: int32 [64, 32, 8, 14], P('gx', 'gy', 'gz'), may hold values from 0 to 26, as said below
- descendants: int32 [64, 32, 8, 2, 128], P('gx', 'gy', 'gz'), may hold values from 0 to 127, as said below
Outputs:
- drift: float32 [64, 32, 8, 3, 128], P('gx', 'gy', 'gz')
- tension: float32 [64, 32, 8, 128], P('gx', 'gy', 'gz')
Inputs may be any that keep to these rules, and one draw needn't show every extreme that they name: `halo_counts`: every cell holds 1 to 128 live halos; some cell holds exactly 128. `neighbour_lists`: each cell's list begins with code 13 (the cell itself) and holds distinct codes. `descendants`: row 0 is a code 0 to 26; row 1 is a live slot of the descendant's cell.
All inputs are finite; a program needn't handle non-finite values.
Results may differ from a plain program's by a relative error of at most 0.0003.
Values sent between devices are 32-bit elements; how exact they have to be, the bound alone decides.
No kernel may reach another device: no remote copies, remote signals or barrier semaphores. Data moves between devices by JAX's collectives and lax.ppermute only.
A program may use at most 64 MiB of HBM per device.

v0:
```python
import functools

import jax
import jax.numpy as jnp
from jax import lax
from jax.sharding import Mesh
from jax.sharding import PartitionSpec as P

GX_GY_GZ = ("gx", "gy_0", "gy_1", "gz_0", "gz_1")
GY = ("gy_0", "gy_1")
GZ = ("gz_0", "gz_1")


EPS_SQ = 0.01
STEP_DT = 0.3
HALF_KICK = 0.045


def padded_2(block, sides, width):
    for axis, dim in sides:
        count = lax.axis_size(axis)
        forward = [(i, i + 1) for i in range(count - 1)]
        forward.append((count - 1, 0))
        backward = [(target, source) for source, target in forward]
        low = lax.ppermute(
            lax.slice_in_dim(block, block.shape[dim] - width, None, axis=dim), axis, forward
        )
        high = lax.ppermute(lax.slice_in_dim(block, 0, width, axis=dim), axis, backward)
        block = jnp.concatenate([low, block, high], axis=dim)
    return block


def by_axis(shard, axes):
    return functools.reduce(lax.psum, axes, shard)


def offsets_of(code):
    return (code // 9 - 1, code // 3 % 3 - 1, code % 3 - 1)


def stack_state(positions_now, positions_next, halo_counts):
    slots = positions_now.shape[-1]
    live = (
        jnp.arange(slots, dtype=jnp.int32)[None, None, None, :] < halo_counts[..., None]
    ).astype(jnp.float32)
    masses = positions_now[:, :, :, 3:4, :] * live[:, :, :, None, :]
    return (jnp.concatenate([positions_now[:, :, :, :3, :], masses, positions_next], axis=3), live)


def predict(padded, neighbour_lists, velocities, descendants, halo_counts):
    cx, cy, cz = neighbour_lists.shape[:3]
    width = neighbour_lists.shape[3]
    px, py, pz = (cx + 2, cy + 2, cz + 2)
    slots = padded.shape[-1]
    cells = cx * cy * cz
    flat = padded.reshape(px * py * pz, 7, slots)
    next_rows = jnp.transpose(flat[:, 4:7, :], (0, 2, 1)).reshape(px * py * pz * slots, 3)
    grid = jnp.indices((cx, cy, cz), dtype=jnp.int32).reshape(3, cells)
    base = ((grid[0] + 1) * py + grid[1] + 1) * pz + grid[2] + 1
    group = 32
    blocks = cells // group
    lists = neighbour_lists.reshape(blocks, group, width)
    vel = velocities.reshape(blocks, group, 3, slots)
    desc = descendants.reshape(blocks, group, 2, slots)
    counts = halo_counts.reshape(blocks, group)
    bases = base.reshape(blocks, group)

    def one_group(items):
        base_g, list_g, vel_g, desc_g, count_g = items
        own = flat[base_g]
        pos = own[:, :3, :]

        def step(accel, code):
            dx, dy, dz = offsets_of(code)
            source = flat[base_g + dx * py * pz + dy * pz + dz]
            offset = jnp.stack([dx, dy, dz], 1).astype(jnp.float32)
            spot = offset[:, :, None] + source[:, :3, :]
            diff = spot[:, :, None, :] - pos[:, :, :, None]
            dist_sq = jnp.sum(diff * diff, axis=1) + EPS_SQ
            weight = source[:, 3, None, :] / (dist_sq * jnp.sqrt(dist_sq))
            return (accel + jnp.sum(diff * weight[:, None, :, :], axis=3), None)

        accel, _ = lax.scan(step, jnp.zeros(pos.shape, jnp.float32), jnp.transpose(list_g))
        predicted = pos + STEP_DT * vel_g + HALF_KICK * accel
        dcode = desc_g[:, 0, :]
        dslot = desc_g[:, 1, :]
        ddx, ddy, ddz = offsets_of(dcode)
        target = base_g[:, None] + ddx * py * pz + ddy * pz + ddz
        found = jnp.transpose(next_rows[target * slots + dslot], (0, 2, 1))
        offset = jnp.stack([ddx, ddy, ddz], 1).astype(jnp.float32)
        error = offset + found - predicted
        live = (jnp.arange(slots, dtype=jnp.int32)[None, :] < count_g[:, None]).astype(jnp.float32)
        drift = error * live[:, None, :]
        squared = jnp.sum(error * error, axis=1) * live
        return (drift, squared)

    drift, squared = lax.map(one_group, (bases, lists, vel, desc, counts))
    return (drift.reshape(cx, cy, cz, 3, slots), squared.reshape(cx, cy, cz, slots))


def shards(positions_now, velocities, positions_next, halo_counts, neighbour_lists, descendants):
    state, live = stack_state(positions_now, positions_next, halo_counts)
    padded = padded_2(state, (("gx", 0), (GY, 1), (GZ, 2)), 1)
    drift, squared = predict(padded, neighbour_lists, velocities, descendants, halo_counts)
    total_sq, total_live = (by_axis(jnp.sum(squared), GX_GY_GZ), by_axis(jnp.sum(live), GX_GY_GZ))
    mean_sq = total_sq / total_live
    return (drift, squared / (mean_sq + 1e-06))


def solution(mesh):
    finer = Mesh(
        mesh.devices.reshape(mesh.shape["gx"], 4, 2, 4, 2), ("gx", "gy_0", "gy_1", "gz_0", "gz_1")
    )
    return jax.shard_map(
        shards,
        mesh=finer,
        in_specs=(
            P("gx", GY, GZ, None, None),
            P("gx", GY, GZ, None, None),
            P("gx", GY, GZ, None, None),
            P("gx", GY, GZ),
            P("gx", GY, GZ, None),
            P("gx", GY, GZ, None, None),
        ),
        out_specs=(P("gx", GY, GZ, None, None), P("gx", GY, GZ, None)),
        check_vma=False,
    )
```

profile of v0, /device:TPU:1, one launch (start us, length us, event | category | flops | bytes accessed | tf_op | source)
XLA Modules:
  0.0 281.4 jit_solution(17403782360344154359)
XLA Ops:
  1.4 0.8 slice.74
  2.2 0.8 compare_select_fusion.1
  3.8 13.7 %collective-permute-start.1 = (f32[1,4,1,7,128]{4,2,3,1,0:T(1,128)S(1)}, f32[1,4,1,7,128]{4,2,3,1,0:T(1,128)S(1)}, u32[]{:S(2)}, u32[]{:S(2)}) collective-permute-start(f32[1,4,1,7,128]{4,2,3,1,0:T(1,128)S(1)} %get-tuple-element.226), channel_id=1, source_target_pairs={{64,0},{128,64},{192,128},{256,192},{320,256},{384,320},{448,384},... | collective-permute-start | bytes 43016 | tf_op jit(solution)/shard_map/ppermute | solution.py:28
  17.5 1.9 collective-permute-start
  19.7 0.9 broadcast_multiply_fusion.1
  20.6 0.8 copy.104
  21.5 0.8 fusion.30
  22.2 6.3 %collective-permute-done = f32[1,4,1,7,128]{4,2,3,1,0:T(1,128)S(1)} collective-permute-done((f32[1,4,1,7,128]{4,2,3,1,0:T(1,128)S(1)}, f32[1,4,1,7,128]{4,2,3,1,0:T(1,128)S(1)}, u32[]{:S(2)}, u32[]{:S(2)}) %collective-permute-start) | collective-permute-done | bytes 14368 | tf_op jit(solution)/shard_map/ppermute | solution.py:25
  28.6 0.8 pad_maximum_fusion.6
  29.4 2.1 collective-permute-start.3
  31.5 1.2 collective-permute-start.2
  33.4 0.8 copy.113
  34.4 1.0 pad_maximum_fusion.1
  35.4 10.1 %collective-permute-start.5 = (f32[10,6,1,7,128]{4,2,3,1,0:T(1,128)S(1)}, f32[10,6,1,7,128]{4,2,3,1,0:T(1,128)S(1)}, u32[]{:S(2)}, u32[]{:S(2)}) collective-permute-start(f32[10,6,1,7,128]{4,2,3,1,0:T(1,128)S(1)} %pad_maximum_fusion.1), channel_id=1, source_target_pairs={{1,0},{2,1},{3,2},{4,3},{5,4},{6,5},{7,6},{0,7},{9,8},{10,9},{11,1... | collective-permute-start | bytes 645128 | tf_op jit(solution)/shard_map/ppermute | solution.py:28
  45.5 3.9 %collective-permute-start.4 = (f32[10,6,1,7,128]{4,2,3,1,0:T(1,128)S(1)}, f32[10,6,1,7,128]{4,2,3,1,0:T(1,128)S(1)}, u32[]{:S(2)}, u32[]{:S(2)}) collective-permute-start(f32[10,6,1,7,128]{4,2,3,1,0:T(1,128)S(1)} %pad_maximum_fusion.1), channel_id=1, source_target_pairs={{0,1},{1,2},{2,3},{3,4},{4,5},{5,6},{6,7},{7,0},{8,9},{9,10},{10,1... | collective-permute-start | bytes 645128 | tf_op jit(solution)/shard_map/ppermute | solution.py:25
  49.4 24.7 %collective-permute-done.5 = f32[10,6,1,7,128]{4,2,3,1,0:T(1,128)S(1)} collective-permute-done((f32[10,6,1,7,128]{4,2,3,1,0:T(1,128)S(1)}, f32[10,6,1,7,128]{4,2,3,1,0:T(1,128)S(1)}, u32[]{:S(2)}, u32[]{:S(2)}) %collective-permute-start.5) | collective-permute-done | bytes 215072 | tf_op jit(solution)/shard_map/ppermute | solution.py:28
  74.2 6.7 %collective-permute-done.4 = f32[10,6,1,7,128]{4,2,3,1,0:T(1,128)S(1)} collective-permute-done((f32[10,6,1,7,128]{4,2,3,1,0:T(1,128)S(1)}, f32[10,6,1,7,128]{4,2,3,1,0:T(1,128)S(1)}, u32[]{:S(2)}, u32[]{:S(2)}) %collective-permute-start.4) | collective-permute-done | bytes 215072 | tf_op jit(solution)/shard_map/ppermute | solution.py:25
  80.8 1.4 pad_maximum_fusion
  83.0 106.7 %while.22 = (s32[]{:T(128)}, f32[32,3,128]{2,1,0:T(4,128)S(1)}, s32[14,32]{1,0:T(8,128)S(1)}, f32[180,7,128]{2,1,0:T(8,128)S(1)}, f32[32,3,128]{2,1,0:T(4,128)S(1)}, /*index=5*/s32[]{:T(128)}, s32[]{:T(128)}) while((s32[]{:T(128)}, f32[32,3,128]{2,1,0:T(4,128)S(1)}, s32[14,32]{1,0:T(8,128)S(1)}, f32[180,7,128]{2,1,0:T(8,128)S(1)}, ...), condition=%wide.region_3.4_spmd.clone, body=%wide.region_0.3_spmd.clone.sunk | while | flops 10512963 | bytes 9166179 | solution.py:83
  84.0 2.1 fusion.45
  86.1 0.8 fusion.46
  86.9 3.7 %fusion.47 = f32[32,3,128]{2,1,0:T(4,128)S(1)} fusion(f32[32,128,128]{2,1,0:T(8,128)S(1)} %fusion.46, f32[32,3,128]{2,1,0:T(4,128)S(1)} %get-tuple-element.287, f32[32,3,128]{2,1,0:T(4,128)S(1)} %slice_add_fusion.2), kind=kLoop, calls=%fused_computation.7.clone.1 | loop fusion | flops 4706304 | bytes 2244608 | tf_op jit(solution)/shard_map/while/body/eval_jaxpr/while/body/eval_jaxpr/reduce_sum | solution.py:81
  91.6 2.1 fusion.45
  93.7 0.8 fusion.46
  94.5 3.7 %fusion.47 = f32[32,3,128]{2,1,0:T(4,128)S(1)} fusion(f32[32,128,128]{2,1,0:T(8,128)S(1)} %fusion.46, f32[32,3,128]{2,1,0:T(4,128)S(1)} %get-tuple-element.287, f32[32,3,128]{2,1,0:T(4,128)S(1)} %slice_add_fusion.2), kind=kLoop, calls=%fused_computation.7.clone.1 | loop fusion | flops 4706304 | bytes 2244608 | tf_op jit(solution)/shard_map/while/body/eval_jaxpr/while/body/eval_jaxpr/reduce_sum | solution.py:81
  99.2 2.1 fusion.45
  101.3 0.8 fusion.46
  102.1 3.7 %fusion.47 = f32[32,3,128]{2,1,0:T(4,128)S(1)} fusion(f32[32,128,128]{2,1,0:T(8,128)S(1)} %fusion.46, f32[32,3,128]{2,1,0:T(4,128)S(1)} %get-tuple-element.287, f32[32,3,128]{2,1,0:T(4,128)S(1)} %slice_add_fusion.2), kind=kLoop, calls=%fused_computation.7.clone.1 | loop fusion | flops 4706304 | bytes 2244608 | tf_op jit(solution)/shard_map/while/body/eval_jaxpr/while/body/eval_jaxpr/reduce_sum | solution.py:81
  106.9 2.1 fusion.45
  109.0 0.8 fusion.46
  109.7 3.7 %fusion.47 = f32[32,3,128]{2,1,0:T(4,128)S(1)} fusion(f32[32,128,128]{2,1,0:T(8,128)S(1)} %fusion.46, f32[32,3,128]{2,1,0:T(4,128)S(1)} %get-tuple-element.287, f32[32,3,128]{2,1,0:T(4,128)S(1)} %slice_add_fusion.2), kind=kLoop, calls=%fused_computation.7.clone.1 | loop fusion | flops 4706304 | bytes 2244608 | tf_op jit(solution)/shard_map/while/body/eval_jaxpr/while/body/eval_jaxpr/reduce_sum | solution.py:81
  114.5 2.1 fusion.45
  116.6 0.8 fusion.46
  117.3 3.7 %fusion.47 = f32[32,3,128]{2,1,0:T(4,128)S(1)} fusion(f32[32,128,128]{2,1,0:T(8,128)S(1)} %fusion.46, f32[32,3,128]{2,1,0:T(4,128)S(1)} %get-tuple-element.287, f32[32,3,128]{2,1,0:T(4,128)S(1)} %slice_add_fusion.2), kind=kLoop, calls=%fused_computation.7.clone.1 | loop fusion | flops 4706304 | bytes 2244608 | tf_op jit(solution)/shard_map/while/body/eval_jaxpr/while/body/eval_jaxpr/reduce_sum | solution.py:81
  122.1 2.1 fusion.45
  124.2 0.8 fusion.46
  125.0 3.7 %fusion.47 = f32[32,3,128]{2,1,0:T(4,128)S(1)} fusion(f32[32,128,128]{2,1,0:T(8,128)S(1)} %fusion.46, f32[32,3,128]{2,1,0:T(4,128)S(1)} %get-tuple-element.287, f32[32,3,128]{2,1,0:T(4,128)S(1)} %slice_add_fusion.2), kind=kLoop, calls=%fused_computation.7.clone.1 | loop fusion | flops 4706304 | bytes 2244608 | tf_op jit(solution)/shard_map/while/body/eval_jaxpr/while/body/eval_jaxpr/reduce_sum | solution.py:81
  129.7 2.1 fusion.45
  132.6 3.7 %fusion.47 = f32[32,3,128]{2,1,0:T(4,128)S(1)} fusion(f32[32,128,128]{2,1,0:T(8,128)S(1)} %fusion.46, f32[32,3,128]{2,1,0:T(4,128)S(1)} %get-tuple-element.287, f32[32,3,128]{2,1,0:T(4,128)S(1)} %slice_add_fusion.2), kind=kLoop, calls=%fused_computation.7.clone.1 | loop fusion | flops 4706304 | bytes 2244608 | tf_op jit(solution)/shard_map/while/body/eval_jaxpr/while/body/eval_jaxpr/reduce_sum | solution.py:81
  137.3 2.1 fusion.45
  140.2 3.7 %fusion.47 = f32[32,3,128]{2,1,0:T(4,128)S(1)} fusion(f32[32,128,128]{2,1,0:T(8,128)S(1)} %fusion.46, f32[32,3,128]{2,1,0:T(4,128)S(1)} %get-tuple-element.287, f32[32,3,128]{2,1,0:T(4,128)S(1)} %slice_add_fusion.2), kind=kLoop, calls=%fused_computation.7.clone.1 | loop fusion | flops 4706304 | bytes 2244608 | tf_op jit(solution)/shard_map/while/body/eval_jaxpr/while/body/eval_jaxpr/reduce_sum | solution.py:81
  145.0 2.1 fusion.45
  147.1 0.8 fusion.46
  147.8 3.7 %fusion.47 = f32[32,3,128]{2,1,0:T(4,128)S(1)} fusion(f32[32,128,128]{2,1,0:T(8,128)S(1)} %fusion.46, f32[32,3,128]{2,1,0:T(4,128)S(1)} %get-tuple-element.287, f32[32,3,128]{2,1,0:T(4,128)S(1)} %slice_add_fusion.2), kind=kLoop, calls=%fused_computation.7.clone.1 | loop fusion | flops 4706304 | bytes 2244608 | tf_op jit(solution)/shard_map/while/body/eval_jaxpr/while/body/eval_jaxpr/reduce_sum | solution.py:81
  152.6 2.1 fusion.45
  154.7 0.8 fusion.46
  155.5 3.7 %fusion.47 = f32[32,3,128]{2,1,0:T(4,128)S(1)} fusion(f32[32,128,128]{2,1,0:T(8,128)S(1)} %fusion.46, f32[32,3,128]{2,1,0:T(4,128)S(1)} %get-tuple-element.287, f32[32,3,128]{2,1,0:T(4,128)S(1)} %slice_add_fusion.2), kind=kLoop, calls=%fused_computation.7.clone.1 | loop fusion | flops 4706304 | bytes 2244608 | tf_op jit(solution)/shard_map/while/body/eval_jaxpr/while/body/eval_jaxpr/reduce_sum | solution.py:81
  160.2 2.1 fusion.45
  162.3 0.8 fusion.46
  163.1 3.7 %fusion.47 = f32[32,3,128]{2,1,0:T(4,128)S(1)} fusion(f32[32,128,128]{2,1,0:T(8,128)S(1)} %fusion.46, f32[32,3,128]{2,1,0:T(4,128)S(1)} %get-tuple-element.287, f32[32,3,128]{2,1,0:T(4,128)S(1)} %slice_add_fusion.2), kind=kLoop, calls=%fused_computation.7.clone.1 | loop fusion | flops 4706304 | bytes 2244608 | tf_op jit(solution)/shard_map/while/body/eval_jaxpr/while/body/eval_jaxpr/reduce_sum | solution.py:81
  167.8 2.1 fusion.45
  169.9 0.8 fusion.46
  170.7 3.7 %fusion.47 = f32[32,3,128]{2,1,0:T(4,128)S(1)} fusion(f32[32,128,128]{2,1,0:T(8,128)S(1)} %fusion.46, f32[32,3,128]{2,1,0:T(4,128)S(1)} %get-tuple-element.287, f32[32,3,128]{2,1,0:T(4,128)S(1)} %slice_add_fusion.2), kind=kLoop, calls=%fused_computation.7.clone.1 | loop fusion | flops 4706304 | bytes 2244608 | tf_op jit(solution)/shard_map/while/body/eval_jaxpr/while/body/eval_jaxpr/reduce_sum | solution.py:81
  175.5 2.1 fusion.45
  178.3 3.7 %fusion.47 = f32[32,3,128]{2,1,0:T(4,128)S(1)} fusion(f32[32,128,128]{2,1,0:T(8,128)S(1)} %fusion.46, f32[32,3,128]{2,1,0:T(4,128)S(1)} %get-tuple-element.287, f32[32,3,128]{2,1,0:T(4,128)S(1)} %slice_add_fusion.2), kind=kLoop, calls=%fused_computation.7.clone.1 | loop fusion | flops 4706304 | bytes 2244608 | tf_op jit(solution)/shard_map/while/body/eval_jaxpr/while/body/eval_jaxpr/reduce_sum | solution.py:81
  183.1 2.1 fusion.45
  185.9 3.7 %fusion.47 = f32[32,3,128]{2,1,0:T(4,128)S(1)} fusion(f32[32,128,128]{2,1,0:T(8,128)S(1)} %fusion.46, f32[32,3,128]{2,1,0:T(4,128)S(1)} %get-tuple-element.287, f32[32,3,128]{2,1,0:T(4,128)S(1)} %slice_add_fusion.2), kind=kLoop, calls=%fused_computation.7.clone.1 | loop fusion | flops 4706304 | bytes 2244608 | tf_op jit(solution)/shard_map/while/body/eval_jaxpr/while/body/eval_jaxpr/reduce_sum | solution.py:81
  189.7 5.9 %copy.109 = f32[180,128,3]{2,1,0:T(8,128)} copy(f32[180,128,3]{1,2,0:T(4,128)S(1)} %slice_bitcast_fusion) | data formatting | bytes 552960 | tf_op jit(solution)/shard_map/transpose | solution.py:57
  195.7 15.1 %gather_fusion.1 = f32[4096,3]{1,0:T(8,128)S(1)} fusion(f32[23040,3]{1,0:T(8,128)} %bitcast.118, s32[4096]{0:T(1024)S(1)} %get-tuple-element.220), kind=kCustom, calls=%fused_computation.1 | custom fusion | bytes 114688 | tf_op jit(solution)/shard_map/while/body/eval_jaxpr/gather | solution.py:89
  212.8 27.8 %all-reduce = (f32[]{:T(128)}, f32[]{:T(128)}) all-reduce(f32[]{:T(128)} %select_reduce_fusion, f32[]{:T(128)} %fusion.30), channel_id=1, replica_groups=mesh['gx'=8,'gy_0'=4,'gy_1'=2,'gz_0'=4,'gz_1'=2] {'gx'}, use_global_device_ids=true, to_apply=%region_6.7 | all-reduce | flops 2 | bytes 16 | tf_op jit(solution)/shard_map/psum | solution.py:34
  240.6 9.4 %all-reduce.2 = (f32[]{:T(128)}, f32[]{:T(128)}) all-reduce(f32[]{:T(128)} %get-tuple-element.204, f32[]{:T(128)} %get-tuple-element.205), channel_id=1, replica_groups=mesh['gx'=8,'gy_0'=4,'gy_1'=2,'gz_0'=4,'gz_1'=2] {'gy_0'}, use_global_device_ids=true, to_apply=%region_7.8 | all-reduce | flops 2 | bytes 16 | tf_op jit(solution)/shard_map/psum | solution.py:34
  250.0 9.0 %all-reduce.4 = (f32[]{:T(128)}, f32[]{:T(128)}) all-reduce(f32[]{:T(128)} %get-tuple-element.208, f32[]{:T(128)} %get-tuple-element.209), channel_id=1, replica_groups=mesh['gx'=8,'gy_0'=4,'gy_1'=2,'gz_0'=4,'gz_1'=2] {'gy_1'}, use_global_device_ids=true, to_apply=%region_8.9 | all-reduce | flops 2 | bytes 16 | tf_op jit(solution)/shard_map/psum | solution.py:34
  259.0 7.3 %all-reduce.1 = (f32[]{:T(128)}, f32[]{:T(128)}) all-reduce(f32[]{:T(128)} %get-tuple-element.212, f32[]{:T(128)} %get-tuple-element.213), channel_id=1, replica_groups=mesh['gx'=8,'gy_0'=4,'gy_1'=2,'gz_0'=4,'gz_1'=2] {'gz_0'}, use_global_device_ids=true, to_apply=%region_9.10 | all-reduce | flops 2 | bytes 16 | tf_op jit(solution)/shard_map/psum | solution.py:34
  266.3 13.1 %all-reduce.3 = (f32[]{:T(128)}, f32[]{:T(128)}) all-reduce(f32[]{:T(128)} %get-tuple-element.206, f32[]{:T(128)} %get-tuple-element.207), channel_id=1, replica_groups=mesh['gx'=8,'gy_0'=4,'gy_1'=2,'gz_0'=4,'gz_1'=2] {'gz_1'}, use_global_device_ids=true, to_apply=%region_10.11 | all-reduce | flops 2 | bytes 16 | tf_op jit(solution)/shard_map/psum | solution.py:34
  (173 shorter events, 23.5 us)
Async XLA Ops:
  3.8 18.5 %collective-permute-start.1 = (f32[1,4,1,7,128]{4,2,3,1,0:T(1,128)S(1)}, f32[1,4,1,7,128]{4,2,3,1,0:T(1,128)S(1)}, u32[]{:S(2)}, u32[]{:S(2)}) collective-permute-start(f32[1,4,1,7,128]{4,2,3,1,0:T(1,128)S(1)} %get-tuple-element.226), channel_id=1, source_target_pairs={{64,0},{128,64},{192,128},{256,192},{320,256},{384,320},{448,384},... | collective-permute-start | bytes 43016 | tf_op jit(solution)/shard_map/ppermute | solution.py:28
  17.5 11.1 %collective-permute-start = (f32[1,4,1,7,128]{4,2,3,1,0:T(1,128)S(1)}, f32[1,4,1,7,128]{4,2,3,1,0:T(1,128)S(1)}, u32[]{:S(2)}, u32[]{:S(2)}) collective-permute-start(f32[1,4,1,7,128]{4,2,3,1,0:T(1,128)S(1)} %get-tuple-element.225), channel_id=1, source_target_pairs={{0,64},{64,128},{128,192},{192,256},{256,320},{320,384},{384,448},... | collective-permute-start | bytes 43016 | tf_op jit(solution)/shard_map/ppermute | solution.py:25
  29.4 5.0 %collective-permute-start.3 = (f32[10,1,1,7,128]{4,2,3,1,0:T(1,128)S(1)}, f32[10,1,1,7,128]{4,2,3,1,0:T(1,128)S(1)}, u32[]{:S(2)}, u32[]{:S(2)}) collective-permute-start(f32[10,1,1,7,128]{4,2,3,1,0:T(1,128)S(1)} %get-tuple-element.224), channel_id=1, source_target_pairs={{8,0},{16,8},{24,16},{32,24},{40,32},{48,40},{56,48},{0,56},{9,1},... | collective-permute-start | bytes 107528 | tf_op jit(solution)/shard_map/ppermute | solution.py:28
  31.5 2.9 %collective-permute-start.2 = (f32[10,1,1,7,128]{4,2,3,1,0:T(1,128)S(1)}, f32[10,1,1,7,128]{4,2,3,1,0:T(1,128)S(1)}, u32[]{:S(2)}, u32[]{:S(2)}) collective-permute-start(f32[10,1,1,7,128]{4,2,3,1,0:T(1,128)S(1)} %get-tuple-element.223), channel_id=1, source_target_pairs={{0,8},{8,16},{16,24},{24,32},{32,40},{40,48},{48,56},{56,0},{1,9},... | collective-permute-start | bytes 107528 | tf_op jit(solution)/shard_map/ppermute | solution.py:25
  35.4 38.8 %collective-permute-start.5 = (f32[10,6,1,7,128]{4,2,3,1,0:T(1,128)S(1)}, f32[10,6,1,7,128]{4,2,3,1,0:T(1,128)S(1)}, u32[]{:S(2)}, u32[]{:S(2)}) collective-permute-start(f32[10,6,1,7,128]{4,2,3,1,0:T(1,128)S(1)} %pad_maximum_fusion.1), channel_id=1, source_target_pairs={{1,0},{2,1},{3,2},{4,3},{5,4},{6,5},{7,6},{0,7},{9,8},{10,9},{11,1... | collective-permute-start | bytes 645128 | tf_op jit(solution)/shard_map/ppermute | solution.py:28
  45.5 35.3 %collective-permute-start.4 = (f32[10,6,1,7,128]{4,2,3,1,0:T(1,128)S(1)}, f32[10,6,1,7,128]{4,2,3,1,0:T(1,128)S(1)}, u32[]{:S(2)}, u32[]{:S(2)}) collective-permute-start(f32[10,6,1,7,128]{4,2,3,1,0:T(1,128)S(1)} %pad_maximum_fusion.1), channel_id=1, source_target_pairs={{0,1},{1,2},{2,3},{3,4},{4,5},{5,6},{6,7},{7,0},{8,9},{9,10},{10,1... | collective-permute-start | bytes 645128 | tf_op jit(solution)/shard_map/ppermute | solution.py:25
where the time goes:
time: 284 us; the launch traced here: 281 us
  other arithmetic  103 us (36%)
  blocking collectives  66.6 us (23%)
  local copies, waits for them, and re-layouts  38.2 us (13%)
  waiting for transfers between devices  37.7 us (13%)
  starting transfers between devices  32.9 us (12%)
    psum x5, blocking collectives, by_axis(): return functools.reduce(lax.psum, axes, shard)  66.6 us
    reduce_sum x14, other arithmetic, step(): return (accel + jnp.sum(diff * weight[:, None, :, :], axis=3), None)  52.1 us
    reduce_sum x14, other arithmetic, step(): dist_sq = jnp.sum(diff * diff, axis=1) + EPS_SQ  28.9 us
    ppermute x3, starting transfers between devices, padded_2(): lax.ppermute(lax.slice_in_dim(block, 0, width, axis=dim), axis, backward)  26 us
    ppermute x3, waiting for transfers between devices, padded_2(): lax.ppermute(lax.slice_in_dim(block, 0, width, axis=dim), axis, backward)  24.7 us
    gather x2, local copies, waits for them, and re-layouts, one_group(): found = jnp.transpose(next_rows[target * slots + dslot], (0, 2, 1))  15.7 us
    ppermute x3, waiting for transfers between devices, padded_2(): lax.ppermute(lax.slice_in_dim(block, block.shape[dim] - width, None, axis...  13 us
    div x14, other arithmetic, step(): weight = source[:, 3, None, :] / (dist_sq * jnp.sqrt(dist_sq))  10.7 us
  transfers between devices with their start and end apart: 6, of which 3 were waited for; matrix products, arithmetic and copies ran while one was open for 2% of the time, Pallas kernels for 0%

commit v1 on v0

v1 whole, which is shorter than its diff:
```python
import functools

import jax
import jax.numpy as jnp
from jax import lax
from jax.experimental import pallas as pl
from jax.experimental.pallas import tpu as pltpu
from jax.sharding import Mesh
from jax.sharding import PartitionSpec as P

AXES = ("gx", "gy_0", "gy_1", "gz_0", "gz_1")
GY = ("gy_0", "gy_1")
GZ = ("gz_0", "gz_1")
ZRING = ("gx", "gz_1")
XYC = ("gz_0", "gy_0", "gy_1")

EPS_SQ = 0.01
STEP_DT = 0.3
HALF_KICK = 0.045


def ring(count, step):
    return [(i, (i + step) % count) for i in range(count)]


def xhop_pairs(count):
    pairs = []
    for x in range(count):
        pairs.append((2 * x, 2 * ((x + 1) % count)))
        pairs.append((2 * x + 1, 2 * ((x - 1) % count) + 1))
    return pairs


def zring_pairs(low, step):
    total = 2 * low

    def flat(z):
        return (z % low) * 2 + z // low

    return [(flat(z), flat((z + step) % total)) for z in range(total)]


def split3(v):
    high = v.astype(jnp.bfloat16).astype(jnp.float32)
    rest = v - high
    mid = rest.astype(jnp.bfloat16).astype(jnp.float32)
    return high, mid, rest - mid


def kernel(half_ref, nbr_ref, cnt_ref, off_ref, st_ref, vel_ref, desc_ref, drift_ref, sq_ref, part_ref):
    cx, cy = vel_ref.shape[0], vel_ref.shape[1]
    width = nbr_ref.shape[3]
    half = half_ref[0]
    sub = lax.broadcasted_iota(jnp.int32, (8, 128), 0)
    lane = lax.broadcasted_iota(jnp.int32, (1, 128), 1)
    zero8 = jnp.zeros((8, 128), jnp.float32)

    def plane_of(dz):
        z = half + dz - 1
        return jnp.where(z < 0, 2, z)

    def one_cell(c, carry):
        total, count = carry
        x = c // cy
        y = c % cy
        own = st_ref[half, x + 1, y + 1]
        centred = jnp.where(sub < 3, own - 0.5, 0.0)
        norm = jnp.sum(centred * centred, axis=0, keepdims=True) + EPS_SQ
        p8 = jnp.where(sub < 3, -2.0 * centred, jnp.where(sub == 3, 1.0, jnp.where(sub == 4, norm, 0.0)))
        ph, pm, pll = split3(p8)
        pcat = jnp.concatenate([ph, ph, ph, pm, pm, pll] + [zero8] * 10, axis=0)
        pt = jnp.transpose(pcat).astype(jnp.bfloat16)
        acc = zero8
        for k in range(width):
            code = nbr_ref[x, y, 0, k]
            dx = code // 9
            dy = (code // 3) % 3
            dz = code % 3
            src = st_ref[plane_of(dz), x + dx, y + dy]
            spot = src + off_ref[code]
            inner = jnp.where(sub < 3, spot, 0.0)
            far = jnp.sum(inner * inner, axis=0, keepdims=True)
            s8 = jnp.where(sub < 3, spot, jnp.where(sub == 3, far, jnp.where(sub == 4, 1.0, 0.0)))
            m8 = jnp.where(sub < 3, spot, jnp.where(sub == 3, 1.0, 0.0)) * src[3:4]
            sh, sm, sl = split3(s8)
            scat = jnp.concatenate([sh, sm, sl, sh, sm, sh] + [zero8] * 10, axis=0).astype(jnp.bfloat16)
            dist = lax.dot_general(pt, scat, (((1,), (0,)), ((), ())), preferred_element_type=jnp.float32)
            inv = lax.rsqrt(dist)
            weight = inv * inv * inv
            wh = weight.astype(jnp.bfloat16)
            wl = (weight - wh.astype(jnp.float32)).astype(jnp.bfloat16)
            mh, mm, ml = split3(m8)
            mcat = jnp.concatenate([mh, mm, ml, zero8], axis=0).astype(jnp.bfloat16)
            nt = (((1,), (1,)), ((), ()))
            a1 = lax.dot_general(mcat, wh, nt, preferred_element_type=jnp.float32)
            a2 = lax.dot_general(mcat[:16], wl, nt, preferred_element_type=jnp.float32)
            acc = acc + ((a1[16:24] + a2[8:16]) + (a1[8:16] + a2[:8])) + a1[:8]
        accel = acc - centred * acc[3:4]
        dcode = desc_ref[x, y, 0, 0:1, :]
        dslot = jnp.broadcast_to(desc_ref[x, y, 0, 1:2, :], (8, 128))
        found = zero8
        for code in range(27):
            dx, dy, dz = code // 9, code // 3 % 3, code % 3
            src = st_ref[plane_of(dz), x + dx, y + dy]
            got = jnp.take_along_axis(src, dslot, axis=1)
            found = jnp.where(dcode == code, got, found)
        ox = (dcode >= 9).astype(jnp.int32) + (dcode >= 18).astype(jnp.int32)
        rest = dcode - 9 * ox
        oy = (rest >= 3).astype(jnp.int32) + (rest >= 6).astype(jnp.int32)
        oz = rest - 3 * oy
        offset = jnp.concatenate([ox, oy, oz], axis=0).astype(jnp.float32) - 1.0
        predicted = own[:3] + STEP_DT * vel_ref[x, y, 0] + HALF_KICK * accel[:3]
        error = offset + found[4:7] - predicted
        alive = lane < cnt_ref[x, y, 0]
        drift_ref[x, y, 0] = jnp.where(alive, error, 0.0)
        squared = jnp.where(alive, jnp.sum(error * error, axis=0, keepdims=True), 0.0)
        sq_ref[x, y] = squared
        return total + squared, count + cnt_ref[x, y, 0]

    total, count = lax.fori_loop(0, cx * cy, one_cell, (jnp.zeros((1, 128), jnp.float32), jnp.int32(0)))
    folded = total + pltpu.roll(jnp.broadcast_to(total, (8, 128)), 64, 1)[:1]
    live = jnp.where(lane == 64, count.astype(jnp.float32), 0.0)
    part_ref[...] = jnp.where(lane < 64, folded, live)


def shards(positions_now, velocities, positions_next, halo_counts, neighbour_lists, descendants):
    cx, cy, cz, _, slots = positions_now.shape
    half = lax.axis_index("gz_1")
    xs = lax.axis_size("gz_0")
    low = lax.axis_size("gx")
    live = (jnp.arange(slots, dtype=jnp.int32) < halo_counts[..., None]).astype(jnp.float32)
    mass = positions_now[..., 3:4, :] * live[..., None, :]
    own = jnp.concatenate(
        [positions_now[..., :3, :], mass, positions_next, jnp.zeros_like(mass)], axis=3
    )[:, :, 0]
    other = lax.ppermute(own, "gz_1", [(0, 1), (1, 0)])
    pair = jnp.where(half == 0, jnp.stack([own, other]), jnp.stack([other, own]))
    below = lax.ppermute(pair[:, cx - 1 :], ZRING, zring_pairs(low, 1))
    above = lax.ppermute(pair[:, :1], ZRING, zring_pairs(low, -1))
    pair = jnp.concatenate([below, pair, above], axis=1)
    sent = jnp.where(half == 0, pair[1], pair[0])
    far = lax.ppermute(sent, GZ, xhop_pairs(xs))
    cube = jnp.concatenate([pair, far[None]], axis=0)
    ny = lax.axis_size(GY)
    below = lax.ppermute(cube[:, :, cy - 1 :], GY, ring(ny, 1))
    above = lax.ppermute(cube[:, :, :1], GY, ring(ny, -1))
    cube = jnp.concatenate([below, cube, above], axis=2)
    codes = jnp.arange(27, dtype=jnp.int32)
    table = jnp.stack([codes // 9, codes // 3 % 3, codes % 3], 1).astype(jnp.float32) - 1.5
    table = jnp.broadcast_to(jnp.pad(table, ((0, 0), (0, 5)))[:, :, None], (27, 8, 128))
    smem = pl.BlockSpec(memory_space=pltpu.SMEM)
    vmem = pl.BlockSpec(memory_space=pltpu.VMEM)
    drift, squared, part = pl.pallas_call(
        kernel,
        in_specs=[smem, smem, smem, vmem, vmem, vmem, vmem],
        out_specs=[vmem, vmem, vmem],
        out_shape=[
            jax.ShapeDtypeStruct((cx, cy, cz, 3, slots), jnp.float32),
            jax.ShapeDtypeStruct((cx, cy, cz, slots), jnp.float32),
            jax.ShapeDtypeStruct((1, slots), jnp.float32),
        ],
        compiler_params=pltpu.CompilerParams(vmem_limit_bytes=32 << 20),
    )(half[None], neighbour_lists, halo_counts, table, cube, velocities, descendants)

    def gathered(row, axes):
        count = lax.axis_size(axes)
        rows = jnp.broadcast_to(row, (count, slots))
        return jnp.sum(lax.all_to_all(rows, axes, 0, 0, tiled=True), axis=0, keepdims=True)

    sums = gathered(gathered(part, XYC), ZRING)
    mean_sq = jnp.sum(sums[:, :64]) / jnp.sum(sums[:, 64:])
    return drift, squared / (mean_sq + 1e-06)


def solution(mesh):
    finer = Mesh(mesh.devices.reshape(mesh.shape["gx"], 4, 2, 4, 2), AXES)
    return jax.shard_map(
        shards,
        mesh=finer,
        in_specs=(
            P("gx", GY, GZ, None, None),
            P("gx", GY, GZ, None, None),
            P("gx", GY, GZ, None, None),
            P("gx", GY, GZ),
            P("gx", GY, GZ, None),
            P("gx", GY, GZ, None, None),
        ),
        out_specs=(P("gx", GY, GZ, None, None), P("gx", GY, GZ, None)),
        check_vma=False,
    )
```

time: 284 us -> 178 us (0.63)
  other arithmetic: 103 us -> 1.67 us
  Pallas kernels: 0 us -> 83.5 us
  blocking collectives: 66.6 us -> 12.4 us
  local copies, waits for them, and re-layouts: 38.2 us -> 3.89 us
  starting transfers between devices: 32.9 us -> 51.8 us
  waiting for transfers between devices: 37.7 us -> 22.6 us
    pallas_call x0 -> x1, Pallas kernels: none -> 83.5 us  [shards(): pl.pallas_call(kernel, in_specs=[smem, smem, smem, vmem, vmem, vmem, vmem...]
    reduce_sum x31 -> x3, other arithmetic: 82.4 us -> 0.71 us  [the longest x1 0.67 us: shards(): mean_sq = jnp.sum(sums[:, :64]) / jnp.sum(sums[:, 64:])]
    psum x5 -> x0, blocking collectives: 66.6 us -> none  [by_axis(): return functools.reduce(lax.psum, axes, shard)]
    ppermute x6, waiting for transfers between devices: 37.7 us -> 12.1 us  [the longest x1 4.12 us: shards(): far = lax.ppermute(sent, GZ, xhop_pairs(xs))]
    gather x17 -> x0, local copies, waits for them, and re-layouts: 24.5 us -> none  [the longest x2 15.7 us: one_group(): found = jnp.transpose(next_rows[target * slots + dslot], (0, 2, 1))]
    all_to_all x0 -> x1, blocking collectives: none -> 12.4 us  [gathered(): lax.all_to_all(rows, axes, 0, 0, tiled=True)]
    all_to_all x0 -> x1, starting transfers between devices: none -> 12.3 us  [gathered(): lax.all_to_all(rows, axes, 0, 0, tiled=True)]
    div x14 -> x0, other arithmetic: 10.7 us -> none  [step(): weight = source[:, 3, None, :] / (dist_sq * jnp.sqrt(dist_sq))]
  transfers between devices with their start and end apart: 6 -> 7, of which waited for: 3 -> 6; matrix products, arithmetic and copies ran while one was open for 2% -> 1% of each run, Pallas kernels for 0% -> 0%
where the time goes in v1:
time: 178 us
  Pallas kernels  83.5 us (47%)
  starting transfers between devices  51.8 us (29%)
  waiting for transfers between devices  22.6 us (13%)
  blocking collectives  12.4 us (7%)
  local copies, waits for them, and re-layouts  3.89 us (2%)
  between operations  2.07 us (1%)
    pallas_call x1, Pallas kernels, shards(): pl.pallas_call(kernel, in_specs=[smem, smem, smem, vmem, vmem, vmem, vmem...  83.5 us
    ppermute x1, starting transfers between devices, shards(): other = lax.ppermute(own, 'gz_1', [(0, 1), (1, 0)])  16.3 us
    all_to_all x1, blocking collectives, gathered(): lax.all_to_all(rows, axes, 0, 0, tiled=True)  12.4 us
    all_to_all x1, starting transfers between devices, gathered(): lax.all_to_all(rows, axes, 0, 0, tiled=True)  12.3 us
    ppermute x1, starting transfers between devices, shards(): below = lax.ppermute(pair[:, cx - 1:], ZRING, zring_pairs(low, 1))  11.6 us
    all_to_all x1, waiting for transfers between devices, gathered(): lax.all_to_all(rows, axes, 0, 0, tiled=True)  10.5 us
    ppermute x1, starting transfers between devices, shards(): below = lax.ppermute(cube[:, :, cy - 1:], GY, ring(ny, 1))  5.15 us
    ppermute x1, waiting for transfers between devices, shards(): far = lax.ppermute(sent, GZ, xhop_pairs(xs))  4.12 us
  transfers between devices with their start and end apart: 7, of which 6 were waited for; matrix products, arithmetic and copies ran while one was open for 1% of the time, Pallas kernels for 0%

profile of v1, /device:TPU:1, one launch (start us, length us, event | category | flops | bytes accessed | tf_op | source)
XLA Modules:
  0.0 178.0 jit_solution(9352948259804643913)
XLA Ops:
  0.6 0.0 copy-start.2
  0.6 0.8 copy.33
  1.4 0.8 copy.35
  2.2 0.0 copy-done.2
  2.3 0.1 compare_select_fusion
  2.4 0.1 fusion.2
  2.5 16.3 %collective-permute-start = (f32[8,4,8,128]{3,2,1,0:T(8,128)S(1)}, f32[8,4,8,128]{3,2,1,0:T(8,128)S(1)}, u32[]{:S(2)}, u32[]{:S(2)}) collective-permute-start(f32[8,4,8,128]{3,2,1,0:T(8,128)S(1)} %get-tuple-element.23), channel_id=1, source_target_pairs={{0,1},{1,0},{2,3},{3,2},{4,5},{5,4},{6,7},{7,6},{8,9},{9,8},{10,11... | collective-permute-start | bytes 393224 | tf_op jit(solution)/shard_map/ppermute | solution.py:136
  18.7 2.6 %collective-permute-done = f32[8,4,8,128]{3,2,1,0:T(8,128)S(1)} collective-permute-done((f32[8,4,8,128]{3,2,1,0:T(8,128)S(1)}, f32[8,4,8,128]{3,2,1,0:T(8,128)S(1)}, u32[]{:S(2)}, u32[]{:S(2)}) %collective-permute-start) | collective-permute-done | bytes 131104 | tf_op jit(solution)/shard_map/ppermute | solution.py:136
  21.4 11.6 %collective-permute-start.1 = (f32[2,1,4,8,128]{4,3,2,1,0:T(8,128)S(1)}, f32[2,1,4,8,128]{4,3,2,1,0:T(8,128)S(1)}, u32[]{:S(2)}, u32[]{:S(2)}) collective-permute-start(f32[2,1,4,8,128]{4,3,2,1,0:T(8,128)S(1)} %get-tuple-element.20), channel_id=1, source_target_pairs={{0,64},{64,128},{128,192},{192,256},{256,320},{320,384},{384,448},... | collective-permute-start | bytes 98312 | tf_op jit(solution)/shard_map/ppermute | solution.py:138
  33.1 3.3 %collective-permute-start.2 = (f32[2,1,4,8,128]{4,3,2,1,0:T(8,128)S(1)}, f32[2,1,4,8,128]{4,3,2,1,0:T(8,128)S(1)}, u32[]{:S(2)}, u32[]{:S(2)}) collective-permute-start(f32[2,1,4,8,128]{4,3,2,1,0:T(8,128)S(1)} %get-tuple-element.21), channel_id=1, source_target_pairs={{0,449},{64,0},{128,64},{192,128},{256,192},{320,256},{384,320},{4... | collective-permute-start | bytes 98312 | tf_op jit(solution)/shard_map/ppermute | solution.py:139
  36.4 0.0 collective-permute-done.1
  36.4 1.3 collective-permute-done.2
  37.8 3.1 %collective-permute-start.3 = (f32[10,4,8,128]{3,2,1,0:T(8,128)S(1)}, f32[10,4,8,128]{3,2,1,0:T(8,128)S(1)}, u32[]{:S(2)}, u32[]{:S(2)}) collective-permute-start(f32[10,4,8,128]{3,2,1,0:T(8,128)S(1)} %fusion), channel_id=1, source_target_pairs={{0,2},{1,7},{2,4},{3,1},{4,6},{5,3},{6,0},{7,5},{8,10},{9,15},{10,... | collective-permute-start | bytes 491528 | tf_op jit(solution)/shard_map/ppermute | solution.py:142
  40.9 4.1 %collective-permute-done.3 = f32[10,4,8,128]{3,2,1,0:T(8,128)S(1)} collective-permute-done((f32[10,4,8,128]{3,2,1,0:T(8,128)S(1)}, f32[10,4,8,128]{3,2,1,0:T(8,128)S(1)}, u32[]{:S(2)}, u32[]{:S(2)}) %collective-permute-start.3) | collective-permute-done | bytes 163872 | tf_op jit(solution)/shard_map/ppermute | solution.py:142
  45.1 0.0 copy-start.4
  45.1 0.0 copy-start.3
  45.1 5.1 %collective-permute-start.4 = (f32[3,10,1,8,128]{4,3,2,1,0:T(8,128)S(1)}, f32[3,10,1,8,128]{4,3,2,1,0:T(8,128)S(1)}, u32[]{:S(2)}, u32[]{:S(2)}) collective-permute-start(f32[3,10,1,8,128]{4,3,2,1,0:T(8,128)S(1)} %get-tuple-element.18), channel_id=1, source_target_pairs={{0,8},{8,16},{16,24},{24,32},{32,40},{40,48},{48,56},{56,0},{1,9},... | collective-permute-start | bytes 368648 | tf_op jit(solution)/shard_map/ppermute | solution.py:145
  50.2 0.0 collective-permute-start.5
  50.2 0.0 copy-done.4
  50.3 0.1 copy.36.cnt_ref
  50.4 0.1 copy.41
  50.5 0.0 copy-done.3
  50.5 1.6 collective-permute-done.4
  52.1 2.4 %collective-permute-done.5 = f32[3,10,1,8,128]{4,3,2,1,0:T(8,128)S(1)} collective-permute-done((f32[3,10,1,8,128]{4,3,2,1,0:T(8,128)S(1)}, f32[3,10,1,8,128]{4,3,2,1,0:T(8,128)S(1)}, u32[]{:S(2)}, u32[]{:S(2)}) %collective-permute-start.5) | collective-permute-done | bytes 122912 | tf_op jit(solution)/shard_map/ppermute | solution.py:146
  54.6 0.0 copy-start
  54.6 0.0 copy-start.1
  54.6 0.1 broadcast_in_dim.13.off_ref
  54.7 0.6 copy-done
  55.4 0.0 copy-done.1
  55.4 83.5 %shard_map.77 = (f32[8,4,1,3,128]{4,3,2,1,0:T(4,128)S(1)}, f32[8,4,1,128]{3,2,1,0:T(1,128)S(1)}, f32[1,128]{1,0:T(1,128)S(1)}) custom-call(s32[1]{0:T(128)} %bitcast.half_ref, s32[8,4,1,14]{3,2,1,0:T(1,128)S(1)} %copy-done.1, s32[8,4,1]{2,1,0:T(4,128)S(1)} %copy.36.cnt_ref, f32[27,8,128]{2,1,0:T(8,128)S(1)} %broadcast_in_dim.13.off_ref, ...), custom_call_target="tpu_custom_call" | custom-call | tf_op jit(solution)/shard_map/pallas_call | solution.py:153
  138.9 12.4 %all_to_all.12 = f32[32,1,128]{2,1,0:T(1,128)S(1)} all-to-all(f32[32,1,128]{2,1,0:T(1,128)S(1)} %broadcast_in_dim.15), channel_id=1, replica_groups=mesh['gx'=8,'gy_0'=4,'gy_1'=2,'gz_0'=4,'gz_1'=2] {'gz_0','gy_0','gy_1'}, dimensions={0} | all-to-all | bytes 32768 | tf_op jit(solution)/shard_map/all_to_all | solution.py:168
  151.3 0.6 broadcast_in_dim.16
  151.9 12.3 %all-to-all-start.1 = ((f32[16,1,128]{2,1,0:T(1,128)}), f32[16,1,128]{2,1,0:T(1,128)S(1)}, u32[]{:S(2)}, u32[]{:S(2)}) async-start(f32[16,1,128]{2,1,0:T(1,128)} %broadcast_in_dim.16), calls=%async_computation.1 | async-start | bytes 16384 | tf_op jit(solution)/shard_map/all_to_all | solution.py:168
  164.2 0.7 copy.40
  164.9 10.5 %all-to-all-done.1 = f32[16,1,128]{2,1,0:T(1,128)S(1)} async-done(((f32[16,1,128]{2,1,0:T(1,128)}), f32[16,1,128]{2,1,0:T(1,128)S(1)}, u32[]{:S(2)}, u32[]{:S(2)}) %all-to-all-start.1) | async-done | bytes 8224 | tf_op jit(solution)/shard_map/all_to_all | solution.py:168
  175.4 0.7 slice_reduce_fusion
  177.4 0.6 broadcast_divide_fusion
  (15 shorter events, 0.3 us)
Async XLA Ops:
  0.6 1.6 copy-start.2
  2.5 18.9 %collective-permute-start = (f32[8,4,8,128]{3,2,1,0:T(8,128)S(1)}, f32[8,4,8,128]{3,2,1,0:T(8,128)S(1)}, u32[]{:S(2)}, u32[]{:S(2)}) collective-permute-start(f32[8,4,8,128]{3,2,1,0:T(8,128)S(1)} %get-tuple-element.23), channel_id=1, source_target_pairs={{0,1},{1,0},{2,3},{3,2},{4,5},{5,4},{6,7},{7,6},{8,9},{9,8},{10,11... | collective-permute-start | bytes 393224 | tf_op jit(solution)/shard_map/ppermute | solution.py:136
  21.4 15.0 %collective-permute-start.1 = (f32[2,1,4,8,128]{4,3,2,1,0:T(8,128)S(1)}, f32[2,1,4,8,128]{4,3,2,1,0:T(8,128)S(1)}, u32[]{:S(2)}, u32[]{:S(2)}) collective-permute-start(f32[2,1,4,8,128]{4,3,2,1,0:T(8,128)S(1)} %get-tuple-element.20), channel_id=1, source_target_pairs={{0,64},{64,128},{128,192},{192,256},{256,320},{320,384},{384,448},... | collective-permute-start | bytes 98312 | tf_op jit(solution)/shard_map/ppermute | solution.py:138
  33.1 4.7 %collective-permute-start.2 = (f32[2,1,4,8,128]{4,3,2,1,0:T(8,128)S(1)}, f32[2,1,4,8,128]{4,3,2,1,0:T(8,128)S(1)}, u32[]{:S(2)}, u32[]{:S(2)}) collective-permute-start(f32[2,1,4,8,128]{4,3,2,1,0:T(8,128)S(1)} %get-tuple-element.21), channel_id=1, source_target_pairs={{0,449},{64,0},{128,64},{192,128},{256,192},{320,256},{384,320},{4... | collective-permute-start | bytes 98312 | tf_op jit(solution)/shard_map/ppermute | solution.py:139
  37.8 7.3 %collective-permute-start.3 = (f32[10,4,8,128]{3,2,1,0:T(8,128)S(1)}, f32[10,4,8,128]{3,2,1,0:T(8,128)S(1)}, u32[]{:S(2)}, u32[]{:S(2)}) collective-permute-start(f32[10,4,8,128]{3,2,1,0:T(8,128)S(1)} %fusion), channel_id=1, source_target_pairs={{0,2},{1,7},{2,4},{3,1},{4,6},{5,3},{6,0},{7,5},{8,10},{9,15},{10,... | collective-permute-start | bytes 491528 | tf_op jit(solution)/shard_map/ppermute | solution.py:142
  45.1 5.2 %copy-start.4 = (s32[8,4,1]{0,2,1:T(1,128)S(1)}, s32[8,4,1]{0,2,1:T(1,128)}, u32[]{:S(2)}) copy-start(s32[8,4,1]{0,2,1:T(1,128)} %param.9) | copy-start | bytes 388
  45.1 5.4 %copy-start.3 = (f32[8,4,1,3,128]{4,2,3,1,0:T(1,128)S(1)}, f32[8,4,1,3,128]{4,2,3,1,0:T(1,128)}, u32[]{:S(2)}) copy-start(f32[8,4,1,3,128]{4,2,3,1,0:T(1,128)} %param.7) | copy-start | bytes 147460
  45.1 7.0 %collective-permute-start.4 = (f32[3,10,1,8,128]{4,3,2,1,0:T(8,128)S(1)}, f32[3,10,1,8,128]{4,3,2,1,0:T(8,128)S(1)}, u32[]{:S(2)}, u32[]{:S(2)}) collective-permute-start(f32[3,10,1,8,128]{4,3,2,1,0:T(8,128)S(1)} %get-tuple-element.18), channel_id=1, source_target_pairs={{0,8},{8,16},{16,24},{24,32},{32,40},{40,48},{48,56},{56,0},{1,9},... | collective-permute-start | bytes 368648 | tf_op jit(solution)/shard_map/ppermute | solution.py:145
  50.2 4.3 %collective-permute-start.5 = (f32[3,10,1,8,128]{4,3,2,1,0:T(8,128)S(1)}, f32[3,10,1,8,128]{4,3,2,1,0:T(8,128)S(1)}, u32[]{:S(2)}, u32[]{:S(2)}) collective-permute-start(f32[3,10,1,8,128]{4,3,2,1,0:T(8,128)S(1)} %get-tuple-element.19), channel_id=1, source_target_pairs={{0,56},{8,0},{16,8},{24,16},{32,24},{40,32},{48,40},{56,48},{1,57}... | collective-permute-start | bytes 368648 | tf_op jit(solution)/shard_map/ppermute | solution.py:146
  54.6 0.8 copy-start
  54.6 0.8 copy-start.1
  151.9 23.5 %all-to-all-start.1 = ((f32[16,1,128]{2,1,0:T(1,128)}), f32[16,1,128]{2,1,0:T(1,128)S(1)}, u32[]{:S(2)}, u32[]{:S(2)}) async-start(f32[16,1,128]{2,1,0:T(1,128)} %broadcast_in_dim.16), calls=%async_computation.1 | async-start | bytes 16384 | tf_op jit(solution)/shard_map/all_to_all | solution.py:168

commit v2 on v1

v2 whole, which is shorter than its diff:
```python
import functools

import jax
import jax.numpy as jnp
from jax import lax
from jax.experimental import pallas as pl
from jax.experimental.pallas import tpu as pltpu
from jax.sharding import Mesh
from jax.sharding import PartitionSpec as P

AXES = ("gx", "gy_0", "gy_1", "gz_0", "gz_1")
GY = ("gy_0", "gy_1")
GZ = ("gz_0", "gz_1")
ZRING = ("gx", "gz_1")
XYC = ("gz_0", "gy_0", "gy_1")

EPS_SQ = 0.01
STEP_DT = 0.3
HALF_KICK = 0.045


def ring(count, step):
    return [(i, (i + step) % count) for i in range(count)]


def xhop_pairs(count):
    pairs = []
    for x in range(count):
        pairs.append((2 * x, 2 * ((x + 1) % count)))
        pairs.append((2 * x + 1, 2 * ((x - 1) % count) + 1))
    return pairs


def zring_pairs(low, step):
    total = 2 * low

    def flat(z):
        return (z % low) * 2 + z // low

    return [(flat(z), flat((z + step) % total)) for z in range(total)]


def split3(v):
    high = v.astype(jnp.bfloat16).astype(jnp.float32)
    rest = v - high
    mid = rest.astype(jnp.bfloat16).astype(jnp.float32)
    return high, mid, rest - mid


def assemble(cnt_ref, now_ref, next_ref, own_ref):
    lane = lax.broadcasted_iota(jnp.int32, (1, 128), 1)
    for x in range(now_ref.shape[0]):
        for y in range(now_ref.shape[1]):
            own_ref[x, y, :3] = now_ref[x, y, 0, :3]
            own_ref[x, y, 3:4] = jnp.where(lane < cnt_ref[y, 0, x], now_ref[x, y, 0, 3:4], 0.0)
            own_ref[x, y, 4:7] = next_ref[x, y, :, 0]
            own_ref[x, y, 7:] = jnp.zeros((1, 128), jnp.float32)


def kernel(
    half_ref, nbr_ref, cnt_ref, off_ref, st_ref, vel_ref, desc_ref, drift_ref, sq_ref, part_ref, out_ref, sems
):
    cx, cy = vel_ref.shape[0], vel_ref.shape[1]
    width = nbr_ref.shape[3]
    half = half_ref[0]
    sub = lax.broadcasted_iota(jnp.int32, (8, 128), 0)
    wide = lax.broadcasted_iota(jnp.int32, (8, width * 128), 0)
    lane = lax.broadcasted_iota(jnp.int32, (1, 128), 1)
    f32, bf16 = jnp.float32, jnp.bfloat16

    def plane_of(dz):
        z = half + dz - 1
        return jnp.where(z < 0, 2, z)

    def acceleration(x, y, own):
        centred = jnp.where(sub < 3, own - 0.5, 0.0)
        norm = jnp.sum(centred * centred, axis=0, keepdims=True) + EPS_SQ
        p8 = jnp.where(sub < 3, -2.0 * centred, jnp.where(sub == 3, 1.0, jnp.where(sub == 4, norm, 0.0)))
        ph, pm, pl3 = split3(p8)
        pcat = jnp.concatenate([ph, ph, ph, pm, pm, pl3], axis=0).astype(bf16)
        spots, masses = [], []
        for k in range(width):
            code = nbr_ref[x, y, 0, k]
            dx = code // 9
            dy = (code // 3) % 3
            dz = code % 3
            src = st_ref[plane_of(dz), x + dx, y + dy]
            spots.append(src + off_ref[code])
            masses.append(src[3:4])
        spot = jnp.concatenate(spots, axis=1)
        mass = jnp.concatenate(masses, axis=1)
        inner = jnp.where(wide < 3, spot, 0.0)
        far = jnp.sum(inner * inner, axis=0, keepdims=True)
        s8 = jnp.where(wide < 3, spot, jnp.where(wide == 3, far, jnp.where(wide == 4, 1.0, 0.0)))
        m8 = jnp.where(wide < 3, spot, jnp.where(wide == 3, 1.0, 0.0)) * mass
        sh, sm, sl = split3(s8)
        mh, mm, ml = split3(m8)
        scat = jnp.transpose(jnp.concatenate([sh, sm, sl, sh, sm, sh], axis=0)).astype(bf16)
        mcat = jnp.concatenate([mh, mm, ml, jnp.zeros_like(ml)], axis=0).astype(bf16)
        dist = jnp.dot(scat, pcat, preferred_element_type=f32)
        inv = lax.rsqrt(dist)
        weight = inv * inv * inv
        wh = weight.astype(bf16)
        wl = (weight - wh.astype(f32)).astype(bf16)
        a1 = jnp.dot(mcat, wh, preferred_element_type=f32)
        a2 = jnp.dot(mcat[:16], wl, preferred_element_type=f32)
        acc = ((a1[16:24] + a2[8:16]) + (a1[8:16] + a2[:8])) + a1[:8]
        return acc - centred * acc[3:4]

    def one_cell(x, y):
        own = st_ref[half, x + 1, y + 1]
        accel = acceleration(x, y, own)
        dcode = desc_ref[x, y, 0, 0:1, :]
        dslot = jnp.broadcast_to(desc_ref[x, y, 0, 1:2, :], (8, 128))
        found = jnp.zeros((8, 128), f32)
        for code in range(27):
            dx, dy, dz = code // 9, code // 3 % 3, code % 3
            src = st_ref[plane_of(dz), x + dx, y + dy]
            got = jnp.take_along_axis(src, dslot, axis=1)
            found = jnp.where(dcode == code, got, found)
        ox = (dcode >= 9).astype(jnp.int32) + (dcode >= 18).astype(jnp.int32)
        rest = dcode - 9 * ox
        oy = (rest >= 3).astype(jnp.int32) + (rest >= 6).astype(jnp.int32)
        oz = rest - 3 * oy
        offset = jnp.concatenate([ox, oy, oz], axis=0).astype(f32) - 1.0
        predicted = own[:3] + STEP_DT * vel_ref[x, y, :, 0] + HALF_KICK * accel[:3]
        error = offset + found[4:7] - predicted
        alive = lane < cnt_ref[y, 0, x]
        out_ref[x, y, :, 0] = jnp.where(alive, error, 0.0)
        squared = jnp.where(alive, jnp.sum(error * error, axis=0, keepdims=True), 0.0)
        sq_ref[x, y] = squared
        return squared

    def one_row(x, carry):
        total, count = carry
        for y in range(cy):
            total = total + one_cell(x, y)
            count = count + cnt_ref[y, 0, x]
        pltpu.make_async_copy(out_ref.at[x], drift_ref.at[x], sems.at[x]).start()
        return total, count

    total, count = lax.fori_loop(0, cx, one_row, (jnp.zeros((1, 128), f32), jnp.int32(0)))
    folded = total + pltpu.roll(jnp.broadcast_to(total, (8, 128)), 64, 1)[:1]
    live = jnp.where(lane == 64, count.astype(f32), 0.0)
    part_ref[...] = jnp.where(lane < 64, folded, live)
    for x in range(cx):
        pltpu.make_async_copy(out_ref.at[x], drift_ref.at[x], sems.at[x]).wait()


def shards(positions_now, velocities, positions_next, halo_counts, neighbour_lists, descendants):
    cx, cy, cz, _, slots = positions_now.shape
    half = lax.axis_index("gz_1")
    xs = lax.axis_size("gz_0")
    low = lax.axis_size("gx")
    smem = pl.BlockSpec(memory_space=pltpu.SMEM)
    vmem = pl.BlockSpec(memory_space=pltpu.VMEM)
    nxt = jnp.transpose(positions_next, (0, 1, 3, 2, 4))
    vel = jnp.transpose(velocities, (0, 1, 3, 2, 4))
    counts = jnp.transpose(halo_counts, (1, 2, 0))
    own = pl.pallas_call(
        assemble,
        in_specs=[smem, vmem, vmem],
        out_specs=vmem,
        out_shape=jax.ShapeDtypeStruct((cx, cy, 8, slots), jnp.float32),
    )(counts, positions_now, nxt)
    other = lax.ppermute(own, "gz_1", [(0, 1), (1, 0)])
    pair = jnp.where(half == 0, jnp.stack([own, other]), jnp.stack([other, own]))
    below = lax.ppermute(pair[:, cx - 1 :], ZRING, zring_pairs(low, 1))
    above = lax.ppermute(pair[:, :1], ZRING, zring_pairs(low, -1))
    pair = jnp.concatenate([below, pair, above], axis=1)
    sent = jnp.where(half == 0, pair[1], pair[0])
    far = lax.ppermute(sent, GZ, xhop_pairs(xs))
    cube = jnp.concatenate([pair, far[None]], axis=0)
    ny = lax.axis_size(GY)
    below = lax.ppermute(cube[:, :, cy - 1 :], GY, ring(ny, 1))
    above = lax.ppermute(cube[:, :, :1], GY, ring(ny, -1))
    cube = jnp.concatenate([below, cube, above], axis=2)
    codes = jnp.arange(27, dtype=jnp.int32)
    table = jnp.stack([codes // 9, codes // 3 % 3, codes % 3], 1).astype(jnp.float32) - 1.5
    table = jnp.broadcast_to(jnp.pad(table, ((0, 0), (0, 5)))[:, :, None], (27, 8, 128))
    drift, squared, part = pl.pallas_call(
        kernel,
        in_specs=[smem, smem, smem, vmem, vmem, vmem, vmem],
        out_specs=[pl.BlockSpec(memory_space=pl.ANY), vmem, vmem],
        out_shape=[
            jax.ShapeDtypeStruct((cx, cy, 3, cz, slots), jnp.float32),
            jax.ShapeDtypeStruct((cx, cy, cz, slots), jnp.float32),
            jax.ShapeDtypeStruct((1, slots), jnp.float32),
        ],
        scratch_shapes=[
            pltpu.VMEM((cx, cy, 3, cz, slots), jnp.float32),
            pltpu.SemaphoreType.DMA((cx,)),
        ],
        compiler_params=pltpu.CompilerParams(vmem_limit_bytes=48 << 20),
    )(half[None], neighbour_lists, counts, table, cube, vel, descendants)

    def gathered(row, axes):
        count = lax.axis_size(axes)
        rows = jnp.broadcast_to(row, (count, slots))
        return jnp.sum(lax.all_to_all(rows, axes, 0, 0, tiled=True), axis=0, keepdims=True)

    sums = gathered(gathered(part, XYC), ZRING)
    mean_sq = jnp.sum(sums[:, :64]) / jnp.sum(sums[:, 64:])
    return jnp.transpose(drift, (0, 1, 3, 2, 4)), squared / (mean_sq + 1e-06)


def solution(mesh):
    finer = Mesh(mesh.devices.reshape(mesh.shape["gx"], 4, 2, 4, 2), AXES)
    return jax.shard_map(
        shards,
        mesh=finer,
        in_specs=(
            P("gx", GY, GZ, None, None),
            P("gx", GY, GZ, None, None),
            P("gx", GY, GZ, None, None),
            P("gx", GY, GZ),
            P("gx", GY, GZ, None),
            P("gx", GY, GZ, None, None),
        ),
        out_specs=(P("gx", GY, GZ, None, None), P("gx", GY, GZ, None)),
        check_vma=False,
    )
```

time: 178 us -> 110 us (0.62)
  Pallas kernels: 83.5 us -> 16.4 us
  blocking collectives: 12.4 us -> 35.8 us
  starting transfers between devices: 51.8 us -> 39.5 us
  waiting for transfers between devices: 22.6 us -> 12.5 us
  local copies, waits for them, and re-layouts: 3.89 us -> 0.92 us
    pallas_call x1, Pallas kernels: 83.5 us -> 14.8 us  [shards(): pl.pallas_call(kernel, in_specs=[smem, smem, smem, vmem, vmem, vmem, vmem...]
    all_to_all x1 -> x2, blocking collectives: 12.4 us -> 35.8 us  [gathered(): lax.all_to_all(rows, axes, 0, 0, tiled=True)]
    all_to_all x1 -> x0, starting transfers between devices: 12.3 us -> none  [gathered(): lax.all_to_all(rows, axes, 0, 0, tiled=True)]
    all_to_all x1 -> x0, waiting for transfers between devices: 10.5 us -> none  [gathered(): lax.all_to_all(rows, axes, 0, 0, tiled=True)]
  transfers between devices with their start and end apart: 7 -> 6, of which waited for: 6 -> 5; matrix products, arithmetic and copies ran while one was open for 1% -> 0% of each run, Pallas kernels for 0% -> 0%
where the time goes in v2:
time: 110 us
  starting transfers between devices  39.5 us (36%)
  blocking collectives  35.8 us (33%)
  Pallas kernels  16.4 us (15%)
  waiting for transfers between devices  12.5 us (11%)
  other arithmetic  2.53 us (2%)
  between operations  2.08 us (2%)
    all_to_all x2, blocking collectives, gathered(): lax.all_to_all(rows, axes, 0, 0, tiled=True)  35.8 us
    ppermute x1, starting transfers between devices, shards(): other = lax.ppermute(own, 'gz_1', [(0, 1), (1, 0)])  16.3 us
    pallas_call x1, Pallas kernels, shards(): pl.pallas_call(kernel, in_specs=[smem, smem, smem, vmem, vmem, vmem, vmem...  14.8 us
    ppermute x1, starting transfers between devices, shards(): below = lax.ppermute(pair[:, cx - 1:], ZRING, zring_pairs(low, 1))  11.6 us
    ppermute x1, starting transfers between devices, shards(): below = lax.ppermute(cube[:, :, cy - 1:], GY, ring(ny, 1))  5.15 us
    ppermute x1, waiting for transfers between devices, shards(): far = lax.ppermute(sent, GZ, xhop_pairs(xs))  4.12 us
    ppermute x1, starting transfers between devices, shards(): above = lax.ppermute(pair[:, :1], ZRING, zring_pairs(low, -1))  3.31 us
    ppermute x1, starting transfers between devices, shards(): far = lax.ppermute(sent, GZ, xhop_pairs(xs))  3.12 us
  transfers between devices with their start and end apart: 6, of which 5 were waited for; matrix products, arithmetic and copies ran while one was open for 0% of the time, Pallas kernels for 0%

profile of v2, /device:TPU:1, one launch (start us, length us, event | category | flops | bytes accessed | tf_op | source)
XLA Modules:
  0.0 109.6 jit_solution(14620042707383821068)
XLA Ops:
  0.6 1.6 %shard_map.77 = f32[8,4,8,128]{3,2,1,0:T(8,128)} custom-call(s32[4,1,8]{2,1,0:T(1,128)} %bitcast.15, f32[8,4,1,4,128]{4,3,2,1,0:T(4,128)} %now_ref.1, f32[8,4,3,1,128]{4,3,2,1,0:T(1,128)} %bitcast.23), custom_call_target="tpu_custom_call" | custom-call | tf_op jit(solution)/shard_map/pallas_call | solution.py:160
  2.2 16.3 %collective-permute-start = (f32[8,4,8,128]{3,2,1,0:T(8,128)}, f32[8,4,8,128]{3,2,1,0:T(8,128)S(1)}, u32[]{:S(2)}, u32[]{:S(2)}) collective-permute-start(f32[8,4,8,128]{3,2,1,0:T(8,128)} %shard_map.77), channel_id=1, source_target_pairs={{0,1},{1,0},{2,3},{3,2},{4,5},{5,4},{6,7},{7,6},{8,9},{9,8},{10,11... | collective-permute-start | bytes 393224 | tf_op jit(solution)/shard_map/ppermute | solution.py:166
  18.5 2.8 %collective-permute-done = f32[8,4,8,128]{3,2,1,0:T(8,128)S(1)} collective-permute-done((f32[8,4,8,128]{3,2,1,0:T(8,128)}, f32[8,4,8,128]{3,2,1,0:T(8,128)S(1)}, u32[]{:S(2)}, u32[]{:S(2)}) %collective-permute-start) | collective-permute-done | bytes 131104 | tf_op jit(solution)/shard_map/ppermute | solution.py:166
  21.3 1.0 maximum_select_fusion
  22.3 11.6 %collective-permute-start.1 = (f32[2,1,4,8,128]{4,3,2,1,0:T(8,128)S(1)}, f32[2,1,4,8,128]{4,3,2,1,0:T(8,128)S(1)}, u32[]{:S(2)}, u32[]{:S(2)}) collective-permute-start(f32[2,1,4,8,128]{4,3,2,1,0:T(8,128)S(1)} %get-tuple-element.12), channel_id=1, source_target_pairs={{0,64},{64,128},{128,192},{192,256},{256,320},{320,384},{384,448},... | collective-permute-start | bytes 98312 | tf_op jit(solution)/shard_map/ppermute | solution.py:168
  34.0 3.3 %collective-permute-start.2 = (f32[2,1,4,8,128]{4,3,2,1,0:T(8,128)S(1)}, f32[2,1,4,8,128]{4,3,2,1,0:T(8,128)S(1)}, u32[]{:S(2)}, u32[]{:S(2)}) collective-permute-start(f32[2,1,4,8,128]{4,3,2,1,0:T(8,128)S(1)} %get-tuple-element.13), channel_id=1, source_target_pairs={{0,449},{64,0},{128,64},{192,128},{256,192},{320,256},{384,320},{4... | collective-permute-start | bytes 98312 | tf_op jit(solution)/shard_map/ppermute | solution.py:169
  37.3 0.0 collective-permute-done.1
  37.3 1.3 %collective-permute-done.2 = f32[2,1,4,8,128]{4,3,2,1,0:T(8,128)S(1)} collective-permute-done((f32[2,1,4,8,128]{4,3,2,1,0:T(8,128)S(1)}, f32[2,1,4,8,128]{4,3,2,1,0:T(8,128)S(1)}, u32[]{:S(2)}, u32[]{:S(2)}) %collective-permute-start.2) | collective-permute-done | bytes 32800 | tf_op jit(solution)/shard_map/ppermute | solution.py:169
  38.7 3.1 %collective-permute-start.3 = (f32[10,4,8,128]{3,2,1,0:T(8,128)S(1)}, f32[10,4,8,128]{3,2,1,0:T(8,128)S(1)}, u32[]{:S(2)}, u32[]{:S(2)}) collective-permute-start(f32[10,4,8,128]{3,2,1,0:T(8,128)S(1)} %fusion), channel_id=1, source_target_pairs={{0,2},{1,7},{2,4},{3,1},{4,6},{5,3},{6,0},{7,5},{8,10},{9,15},{10,... | collective-permute-start | bytes 491528 | tf_op jit(solution)/shard_map/ppermute | solution.py:172
  41.9 4.1 %collective-permute-done.3 = f32[10,4,8,128]{3,2,1,0:T(8,128)S(1)} collective-permute-done((f32[10,4,8,128]{3,2,1,0:T(8,128)S(1)}, f32[10,4,8,128]{3,2,1,0:T(8,128)S(1)}, u32[]{:S(2)}, u32[]{:S(2)}) %collective-permute-start.3) | collective-permute-done | bytes 163872 | tf_op jit(solution)/shard_map/ppermute | solution.py:172
  46.0 5.1 %collective-permute-start.4 = (f32[3,10,1,8,128]{4,3,2,1,0:T(8,128)S(1)}, f32[3,10,1,8,128]{4,3,2,1,0:T(8,128)S(1)}, u32[]{:S(2)}, u32[]{:S(2)}) collective-permute-start(f32[3,10,1,8,128]{4,3,2,1,0:T(8,128)S(1)} %get-tuple-element.10), channel_id=1, source_target_pairs={{0,8},{8,16},{16,24},{24,32},{32,40},{40,48},{48,56},{56,0},{1,9},... | collective-permute-start | bytes 368648 | tf_op jit(solution)/shard_map/ppermute | solution.py:175
  51.1 0.0 collective-permute-start.5
  51.2 0.1 copy.13
  51.3 1.7 %collective-permute-done.4 = f32[3,10,1,8,128]{4,3,2,1,0:T(8,128)S(1)} collective-permute-done((f32[3,10,1,8,128]{4,3,2,1,0:T(8,128)S(1)}, f32[3,10,1,8,128]{4,3,2,1,0:T(8,128)S(1)}, u32[]{:S(2)}, u32[]{:S(2)}) %collective-permute-start.4) | collective-permute-done | bytes 122912 | tf_op jit(solution)/shard_map/ppermute | solution.py:175
  53.0 2.4 %collective-permute-done.5 = f32[3,10,1,8,128]{4,3,2,1,0:T(8,128)S(1)} collective-permute-done((f32[3,10,1,8,128]{4,3,2,1,0:T(8,128)S(1)}, f32[3,10,1,8,128]{4,3,2,1,0:T(8,128)S(1)}, u32[]{:S(2)}, u32[]{:S(2)}) %collective-permute-start.5) | collective-permute-done | bytes 122912 | tf_op jit(solution)/shard_map/ppermute | solution.py:176
  55.5 0.0 copy-start
  55.5 0.0 copy-start.1
  55.5 0.0 copy-start.2
  55.5 0.1 broadcast_in_dim.13.off_ref
  55.6 0.0 copy-start.3
  55.6 0.7 copy-done
  56.3 0.0 copy-done.1
  56.3 0.0 copy-done.2
  56.3 0.0 copy-done.3
  56.3 14.8 %shard_map.78 = (f32[8,4,3,1,128]{4,3,2,1,0:T(1,128)}, f32[8,4,1,128]{3,2,1,0:T(1,128)S(1)}, f32[1,128]{1,0:T(1,128)S(1)}) custom-call(s32[1]{0:T(128)} %bitcast.half_ref, s32[8,4,1,14]{3,2,1,0:T(1,128)S(1)} %copy-done.2, s32[4,1,8]{2,1,0:T(1,128)S(1)} %bitcast.16, f32[27,8,128]{2,1,0:T(8,128)S(1)} %broadcast_in_dim.13.off_ref, ...), custom_call_target="tpu_custom_call" | custom-call | tf_op jit(solution)/shard_map/pallas_call | solution.py:181
  71.1 12.4 %all_to_all.12 = f32[32,1,128]{2,1,0:T(1,128)S(1)} all-to-all(f32[32,1,128]{2,1,0:T(1,128)S(1)} %broadcast_in_dim.29), channel_id=1, replica_groups=mesh['gx'=8,'gy_0'=4,'gy_1'=2,'gz_0'=4,'gz_1'=2] {'gz_0','gy_0','gy_1'}, dimensions={0} | all-to-all | bytes 32768 | tf_op jit(solution)/shard_map/all_to_all | solution.py:200
  83.6 23.3 %all_to_all.13 = f32[16,1,128]{2,1,0:T(1,128)S(1)} all-to-all(f32[16,1,128]{2,1,0:T(1,128)S(1)} %broadcast_in_dim.30), channel_id=1, replica_groups=mesh['gx'=8,'gy_0'=4,'gy_1'=2,'gz_0'=4,'gz_1'=2] {'gx','gz_1'}, dimensions={0} | all-to-all | bytes 16384 | tf_op jit(solution)/shard_map/all_to_all | solution.py:200
  107.0 0.7 slice_reduce_fusion
  109.0 0.6 broadcast_divide_fusion
  (13 shorter events, 0.2 us)
Async XLA Ops:
  2.2 19.1 %collective-permute-start = (f32[8,4,8,128]{3,2,1,0:T(8,128)}, f32[8,4,8,128]{3,2,1,0:T(8,128)S(1)}, u32[]{:S(2)}, u32[]{:S(2)}) collective-permute-start(f32[8,4,8,128]{3,2,1,0:T(8,128)} %shard_map.77), channel_id=1, source_target_pairs={{0,1},{1,0},{2,3},{3,2},{4,5},{5,4},{6,7},{7,6},{8,9},{9,8},{10,11... | collective-permute-start | bytes 393224 | tf_op jit(solution)/shard_map/ppermute | solution.py:166
  22.3 15.0 %collective-permute-start.1 = (f32[2,1,4,8,128]{4,3,2,1,0:T(8,128)S(1)}, f32[2,1,4,8,128]{4,3,2,1,0:T(8,128)S(1)}, u32[]{:S(2)}, u32[]{:S(2)}) collective-permute-start(f32[2,1,4,8,128]{4,3,2,1,0:T(8,128)S(1)} %get-tuple-element.12), channel_id=1, source_target_pairs={{0,64},{64,128},{128,192},{192,256},{256,320},{320,384},{384,448},... | collective-permute-start | bytes 98312 | tf_op jit(solution)/shard_map/ppermute | solution.py:168
  34.0 4.7 %collective-permute-start.2 = (f32[2,1,4,8,128]{4,3,2,1,0:T(8,128)S(1)}, f32[2,1,4,8,128]{4,3,2,1,0:T(8,128)S(1)}, u32[]{:S(2)}, u32[]{:S(2)}) collective-permute-start(f32[2,1,4,8,128]{4,3,2,1,0:T(8,128)S(1)} %get-tuple-element.13), channel_id=1, source_target_pairs={{0,449},{64,0},{128,64},{192,128},{256,192},{320,256},{384,320},{4... | collective-permute-start | bytes 98312 | tf_op jit(solution)/shard_map/ppermute | solution.py:169
  38.7 7.3 %collective-permute-start.3 = (f32[10,4,8,128]{3,2,1,0:T(8,128)S(1)}, f32[10,4,8,128]{3,2,1,0:T(8,128)S(1)}, u32[]{:S(2)}, u32[]{:S(2)}) collective-permute-start(f32[10,4,8,128]{3,2,1,0:T(8,128)S(1)} %fusion), channel_id=1, source_target_pairs={{0,2},{1,7},{2,4},{3,1},{4,6},{5,3},{6,0},{7,5},{8,10},{9,15},{10,... | collective-permute-start | bytes 491528 | tf_op jit(solution)/shard_map/ppermute | solution.py:172
  46.0 7.0 %collective-permute-start.4 = (f32[3,10,1,8,128]{4,3,2,1,0:T(8,128)S(1)}, f32[3,10,1,8,128]{4,3,2,1,0:T(8,128)S(1)}, u32[]{:S(2)}, u32[]{:S(2)}) collective-permute-start(f32[3,10,1,8,128]{4,3,2,1,0:T(8,128)S(1)} %get-tuple-element.10), channel_id=1, source_target_pairs={{0,8},{8,16},{16,24},{24,32},{32,40},{40,48},{48,56},{56,0},{1,9},... | collective-permute-start | bytes 368648 | tf_op jit(solution)/shard_map/ppermute | solution.py:175
  51.1 4.3 %collective-permute-start.5 = (f32[3,10,1,8,128]{4,3,2,1,0:T(8,128)S(1)}, f32[3,10,1,8,128]{4,3,2,1,0:T(8,128)S(1)}, u32[]{:S(2)}, u32[]{:S(2)}) collective-permute-start(f32[3,10,1,8,128]{4,3,2,1,0:T(8,128)S(1)} %get-tuple-element.11), channel_id=1, source_target_pairs={{0,56},{8,0},{16,8},{24,16},{32,24},{40,32},{48,40},{56,48},{1,57}... | collective-permute-start | bytes 368648 | tf_op jit(solution)/shard_map/ppermute | solution.py:176
  55.5 0.8 copy-start
  55.5 0.8 copy-start.1
  55.5 0.8 copy-start.2
  55.6 0.7 copy-start.3

commit v3 on v2

v3 whole, which is shorter than its diff:
```python
import functools

import jax
import jax.numpy as jnp
import numpy as np
from jax import lax
from jax.experimental import pallas as pl
from jax.experimental.pallas import tpu as pltpu
from jax.sharding import Mesh
from jax.sharding import PartitionSpec as P

AXES = ("gx", "gy_0", "gy_1", "gz_0", "gz_1")
GY = ("gy_0", "gy_1")
GZ = ("gz_0", "gz_1")
ZRING = ("gx", "gz_1")
XYC = ("gz_0", "gy_0", "gy_1")

EPS_SQ = 0.01
STEP_DT = 0.3
HALF_KICK = 0.045


def ring(count, step):
    return [(i, (i + step) % count) for i in range(count)]


def xhop_pairs(count):
    pairs = []
    for x in range(count):
        pairs.append((2 * x, 2 * ((x + 1) % count)))
        pairs.append((2 * x + 1, 2 * ((x - 1) % count) + 1))
    return pairs


def zring_pairs(low, step):
    total = 2 * low

    def flat(z):
        return (z % low) * 2 + z // low

    return [(flat(z), flat((z + step) % total)) for z in range(total)]


def split3(v):
    high = v.astype(jnp.bfloat16).astype(jnp.float32)
    rest = v - high
    mid = rest.astype(jnp.bfloat16).astype(jnp.float32)
    return high, mid, rest - mid


def assemble(cnt_ref, now_ref, next_ref, own_ref):
    lane = lax.broadcasted_iota(jnp.int32, (1, 128), 1)
    for x in range(now_ref.shape[0]):
        for y in range(now_ref.shape[1]):
            own_ref[x, y, :3] = now_ref[x, y, 0, :3]
            own_ref[x, y, 3:4] = jnp.where(lane < cnt_ref[y, 0, x], now_ref[x, y, 0, 3:4], 0.0)
            own_ref[x, y, 4:7] = next_ref[x, y, :, 0]
            own_ref[x, y, 7:] = jnp.zeros((1, 128), jnp.float32)


CLASSES = 4
BATCH = 36
F32, BF16, I32 = jnp.float32, jnp.bfloat16, jnp.int32


def item_table(cx, cy):
    px = cx + 2
    table = np.zeros((2, 3, 3, 27), np.int32)
    for half in range(2):
        for xe in range(3):
            for ye in range(3):
                for code in range(27):
                    dx, dy, dz = code // 9, code // 3 % 3, code % 3
                    plane = 0 if dz == 1 else (1 if (dz == 2) == (half == 0) else 2)
                    x_in = not (xe == 0 and dx == 0 or xe == 2 and dx == 2)
                    if ye == 0 and dy == 0 or ye == 2 and dy == 2:
                        kind, step = 3, (3 * px if dy == 2 else 0) + plane * px + dx
                    elif plane == 2:
                        kind, step = 2, dx * cy + dy - 1
                    elif plane == 1:
                        kind, step = 1, dx * cy + dy - 1
                    elif x_in:
                        kind, step = 0, (dx - 1) * cy + dy - 1
                    else:
                        kind = 1
                        step = px * cy + dy - 1 if dx == 0 else (px + 1 - (cx - 1)) * cy + dy - 1
                    table[half, xe, ye, code] = 4 * (1024 * step + 32 * code) + kind
    return table.reshape(-1)


def offset_table():
    codes = np.arange(27)
    rows = np.stack([codes // 9, codes // 3 % 3, codes % 3], 1).astype(np.float32) - 0.5
    return np.broadcast_to(np.pad(rows, ((0, 0), (0, 5)))[:, :, None], (27, 8, 128)).copy()


def sublanes():
    return lax.broadcasted_iota(I32, (8, 128), 0)


def source_features(src, index, st_ref, mc_ref):
    sub = sublanes()
    q = jnp.where(sub < 3, src - 0.5, 0.0)
    norm = jnp.sum(q * q, axis=0, keepdims=True)
    s8 = jnp.where(sub < 3, -2.0 * q, jnp.where(sub == 3, norm, jnp.where(sub == 4, 1.0, 0.0)))
    m8 = jnp.where(sub == 3, 1.0, q) * src[3:4]
    sh, sm, sl = split3(s8)
    mh, mm, ml = split3(m8)
    st_ref[index] = jnp.transpose(jnp.concatenate([sh, sm, sl, sh, sm, sh], axis=0)).astype(BF16)
    mc_ref[index] = jnp.concatenate([mh, mm, ml, jnp.zeros_like(ml)], axis=0).astype(BF16)


def run_items(kind, cap, list_ref, count_ref, st_ref, mc_ref, own_of, off_ref, acc_ref):
    sub = sublanes()
    count = count_ref[kind]

    def batch(b, carry):
        sums = []
        for t in range(BATCH):
            place = b * BATCH + t
            valid = place < count
            item = jnp.where(valid, list_ref[kind * cap + place], 0)
            src, code, cell = item >> 10, (item >> 5) & 31, item & 31
            p = jnp.where(sub < 3, own_of(cell) - off_ref[code], 0.0)
            norm = jnp.sum(p * p, axis=0, keepdims=True) + EPS_SQ
            p8 = jnp.where(sub == 3, 1.0, jnp.where(sub == 4, norm, p))
            ph, pm, pr = split3(p8)
            pcat = jnp.concatenate([ph, ph, ph, pm, pm, pr], axis=0).astype(BF16)
            dist = jnp.dot(st_ref[src], pcat, preferred_element_type=F32)
            inv = lax.rsqrt(dist)
            weight = inv * inv * inv
            wh = weight.astype(BF16)
            wl = (weight - wh.astype(F32)).astype(BF16)
            mc = mc_ref[src]
            a = jnp.dot(
                jnp.concatenate([mc, mc], axis=1), jnp.concatenate([wh, wl], axis=0), preferred_element_type=F32
            )
            a8 = (a[16:24] + a[8:16]) + a[:8]
            sums.append((cell, (a8 - p * a8[3:4]) * valid.astype(F32)))
        for cell, add in sums:
            acc_ref[cell] = acc_ref[cell] + add
        return carry

    lax.fori_loop(0, (count + BATCH - 1) // BATCH, batch, 0)


def own_pass(half_ref, table_ref, nbr_ref, off_ref, own_ref, list_ref, count_ref, acc_ref, st_ref, mc_ref, *, cap):
    cx, cy = own_ref.shape[0], own_ref.shape[1]
    width = nbr_ref.shape[3]
    half = half_ref[0]
    for kind in range(CLASSES):
        count_ref[kind] = 0
    acc_ref[...] = jnp.zeros(acc_ref.shape, F32)

    def one_row(x, carry):
        xe = jnp.where(x == 0, 0, jnp.where(x == cx - 1, 2, 1))
        for y in range(cy):
            cell = x * cy + y
            ye = (0 if y == 0 else 1) if y < cy - 1 else 2
            row = ((half * 3 + xe) * 3 + ye) * 27
            for k in range(width):
                entry = table_ref[row + nbr_ref[x, y, 0, k]]
                kind = entry & 3
                item = (entry >> 2) + jnp.where(kind == 3, cell + 1024 * x, 1025 * cell)
                place = count_ref[kind]
                list_ref[kind * cap + place] = item
                count_ref[kind] = place + 1
            source_features(own_ref[x, y], cell, st_ref, mc_ref)
        return carry

    lax.fori_loop(0, cx, one_row, 0)
    run_items(0, cap, list_ref, count_ref, st_ref, mc_ref, lambda c: own_ref[c // cy, c % cy], off_ref, acc_ref)


def other_pass(list_ref, count_ref, off_ref, own_ref, other_ref, acc_ref, st_ref, mc_ref, *, cap):
    px, cy = own_ref.shape[0], own_ref.shape[1]
    acc_ref[...] = jnp.zeros(acc_ref.shape, F32)

    rows = px // 2

    def some_rows(part, carry):
        for step in range(rows):
            x = part * rows + step
            for y in range(cy):
                source_features(other_ref[x, y], x * cy + y, st_ref, mc_ref)
        return carry

    lax.fori_loop(0, 2, some_rows, 0)
    for y in range(cy):
        source_features(own_ref[0, y], px * cy + y, st_ref, mc_ref)
        source_features(own_ref[px - 1, y], (px + 1) * cy + y, st_ref, mc_ref)
    run_items(1, cap, list_ref, count_ref, st_ref, mc_ref, lambda c: own_ref[c // cy + 1, c % cy], off_ref, acc_ref)


def far_pass(list_ref, count_ref, off_ref, own_ref, far_ref, acc_ref, st_ref, mc_ref, *, cap):
    px, cy = own_ref.shape[0], own_ref.shape[1]
    acc_ref[...] = jnp.zeros(acc_ref.shape, F32)

    rows = px // 2

    def some_rows(part, carry):
        for step in range(rows):
            x = part * rows + step
            for y in range(cy):
                source_features(far_ref[x, y], x * cy + y, st_ref, mc_ref)
        return carry

    lax.fori_loop(0, 2, some_rows, 0)
    run_items(2, cap, list_ref, count_ref, st_ref, mc_ref, lambda c: own_ref[c // cy + 1, c % cy], off_ref, acc_ref)


def last_pass(
    half_ref, list_ref, count_ref, cnt_ref, off_ref, own_ref, other_ref, far_ref, low_ref, high_ref,
    acc0_ref, acc1_ref, acc2_ref, vel_ref, desc_ref,
    drift_ref, sq_ref, part_ref,
    acc_ref, st_ref, mc_ref, cube_ref, out_ref, sems, *, cap
):
    px, cy = own_ref.shape[0], own_ref.shape[1]
    cx = px - 2
    half = half_ref[0]
    lane = lax.broadcasted_iota(I32, (1, 128), 1)
    acc_ref[...] = acc0_ref[...] + acc1_ref[...] + acc2_ref[...]

    rows = px // 2

    def strips(part, carry):
        for step in range(rows):
            x = part * rows + step
            for plane in range(3):
                source_features(low_ref[plane, x], plane * px + x, st_ref, mc_ref)
                source_features(high_ref[plane, x], (3 + plane) * px + x, st_ref, mc_ref)
        return carry

    lax.fori_loop(0, 2, strips, 0)
    run_items(3, cap, list_ref, count_ref, st_ref, mc_ref, lambda c: own_ref[c // cy + 1, c % cy], off_ref, acc_ref)

    def fill(z, ref, plane):
        cube_ref[z, :, 0] = low_ref[plane]
        cube_ref[z, :, 1 : cy + 1] = ref[...]
        cube_ref[z, :, cy + 1] = high_ref[plane]

    fill(1, own_ref, 0)

    @pl.when(half == 0)
    def _():
        fill(0, far_ref, 2)
        fill(2, other_ref, 1)

    @pl.when(half != 0)
    def _():
        fill(0, other_ref, 1)
        fill(2, far_ref, 2)

    def one_cell(x, y):
        own = own_ref[x + 1, y]
        accel = acc_ref[x * cy + y]
        dcode = desc_ref[x, y, 0, 0:1, :]
        dslot = jnp.broadcast_to(desc_ref[x, y, 0, 1:2, :], (8, 128))
        found = jnp.zeros((8, 128), F32)
        for code in range(27):
            dx, dy, dz = code // 9, code // 3 % 3, code % 3
            got = jnp.take_along_axis(cube_ref[dz, x + dx, y + dy], dslot, axis=1)
            found = jnp.where(dcode == code, got, found)
        ox = (dcode >= 9).astype(I32) + (dcode >= 18).astype(I32)
        rest = dcode - 9 * ox
        oy = (rest >= 3).astype(I32) + (rest >= 6).astype(I32)
        oz = rest - 3 * oy
        offset = jnp.concatenate([ox, oy, oz], axis=0).astype(F32) - 1.0
        predicted = own[:3] + STEP_DT * vel_ref[x, y, :, 0] + HALF_KICK * accel[:3]
        error = offset + found[4:7] - predicted
        alive = lane < cnt_ref[y, 0, x]
        out_ref[x, y, :, 0] = jnp.where(alive, error, 0.0)
        squared = jnp.where(alive, jnp.sum(error * error, axis=0, keepdims=True), 0.0)
        sq_ref[x, y] = squared
        return squared

    def one_row(x, carry):
        total, count = carry
        for y in range(cy):
            total = total + one_cell(x, y)
            count = count + cnt_ref[y, 0, x]
        pltpu.make_async_copy(out_ref.at[x], drift_ref.at[x], sems.at[x]).start()
        return total, count

    total, count = lax.fori_loop(0, cx, one_row, (jnp.zeros((1, 128), F32), jnp.int32(0)))
    folded = total + pltpu.roll(jnp.broadcast_to(total, (8, 128)), 64, 1)[:1]
    live = jnp.where(lane == 64, count.astype(F32), 0.0)
    part_ref[...] = jnp.where(lane < 64, folded, live)
    for x in range(cx):
        pltpu.make_async_copy(out_ref.at[x], drift_ref.at[x], sems.at[x]).wait()


SMEM = pl.BlockSpec(memory_space=pltpu.SMEM)
VMEM = pl.BlockSpec(memory_space=pltpu.VMEM)


def cost(items):
    pairs = items * 128 * 128
    return pl.CostEstimate(flops=400 * pairs, transcendentals=pairs, bytes_accessed=1 << 20)


def params():
    return pltpu.CompilerParams(vmem_limit_bytes=40 << 20)


def features_of(sources):
    return [pltpu.VMEM((sources, 128, 48), BF16), pltpu.VMEM((sources, 32, 128), BF16)]


def first_forces(half, neighbour_lists, own):
    cx, cy = own.shape[:2]
    items = cx * cy * neighbour_lists.shape[3]
    cap = items + 2 * BATCH
    return pl.pallas_call(
        functools.partial(own_pass, cap=cap),
        in_specs=[SMEM, SMEM, SMEM, VMEM, VMEM],
        out_specs=[SMEM, SMEM, VMEM],
        out_shape=[
            jax.ShapeDtypeStruct((CLASSES * cap,), I32),
            jax.ShapeDtypeStruct((CLASSES,), I32),
            jax.ShapeDtypeStruct((cx * cy, 8, 128), F32),
        ],
        scratch_shapes=features_of(cx * cy),
        cost_estimate=cost(items // 4),
        compiler_params=params(),
    )(half, item_table(cx, cy), neighbour_lists, offset_table(), own)


def more_forces(body, lists, counts, own, planes):
    px, cy = own.shape[:2]
    cells = (px - 2) * cy
    cap = lists.shape[0] // CLASSES
    return pl.pallas_call(
        functools.partial(body, cap=cap),
        in_specs=[SMEM, SMEM, VMEM, VMEM, VMEM],
        out_specs=VMEM,
        out_shape=jax.ShapeDtypeStruct((cells, 8, 128), F32),
        scratch_shapes=features_of((px + 2) * cy),
        cost_estimate=cost(cap // 4),
        compiler_params=params(),
    )(lists, counts, offset_table(), own, planes)


def finish(half, lists, counts, cnt, own, other, far, low, high, sums, vel, descendants):
    px, cy = own.shape[:2]
    cx = px - 2
    cap = lists.shape[0] // CLASSES
    return pl.pallas_call(
        functools.partial(last_pass, cap=cap),
        in_specs=[SMEM] * 4 + [VMEM] * 11,
        out_specs=[pl.BlockSpec(memory_space=pl.ANY), VMEM, VMEM],
        out_shape=[
            jax.ShapeDtypeStruct((cx, cy, 3, 1, 128), F32),
            jax.ShapeDtypeStruct((cx, cy, 1, 128), F32),
            jax.ShapeDtypeStruct((1, 128), F32),
        ],
        scratch_shapes=[pltpu.VMEM((cx * cy, 8, 128), F32)]
        + features_of(6 * px)
        + [
            pltpu.VMEM((3, px, cy + 2, 8, 128), F32),
            pltpu.VMEM((cx, cy, 3, 1, 128), F32),
            pltpu.SemaphoreType.DMA((cx,)),
        ],
        cost_estimate=cost(cap // 4),
        compiler_params=params(),
    )(half, lists, counts, cnt, offset_table(), own, other, far, low, high, *sums, vel, descendants)


def shards(positions_now, velocities, positions_next, halo_counts, neighbour_lists, descendants):
    cx, cy, cz, _, slots = positions_now.shape
    half = lax.axis_index("gz_1")
    xs = lax.axis_size("gz_0")
    zs = lax.axis_size("gx")
    ny = lax.axis_size(GY)
    nxt = jnp.transpose(positions_next, (0, 1, 3, 2, 4))
    vel = jnp.transpose(velocities, (0, 1, 3, 2, 4))
    cnt = jnp.transpose(halo_counts, (1, 2, 0))
    own = pl.pallas_call(
        assemble,
        in_specs=[SMEM, VMEM, VMEM],
        out_specs=VMEM,
        out_shape=jax.ShapeDtypeStruct((cx, cy, 8, slots), F32),
    )(cnt, positions_now, nxt)
    other = lax.ppermute(own, "gz_1", [(0, 1), (1, 0)])
    lists, counts, acc0 = first_forces(half[None], neighbour_lists, own)

    def both(x):
        ends = own[x], other[x]
        return jnp.where(half == 0, jnp.stack(ends), jnp.stack(ends[::-1]))

    below = lax.ppermute(both(cx - 1), ZRING, zring_pairs(zs, 1))
    above = lax.ppermute(both(0), ZRING, zring_pairs(zs, -1))

    def widened(block, plane):
        ends = [jnp.where(plane == 0, v[0], v[1])[None] for v in (below, above)]
        return jnp.concatenate([ends[0], block, ends[1]], axis=0)

    own = widened(own, half)
    other = widened(other, 1 - half)
    far = lax.ppermute(other, GZ, xhop_pairs(xs))
    acc1 = more_forces(other_pass, lists, counts, own, other)
    planes = (own, other, far)
    low = lax.ppermute(jnp.stack([v[:, cy - 1] for v in planes]), GY, ring(ny, 1))
    high = lax.ppermute(jnp.stack([v[:, 0] for v in planes]), GY, ring(ny, -1))
    acc2 = more_forces(far_pass, lists, counts, own, far)
    drift, squared, part = finish(
        half[None], lists, counts, cnt, *planes, low, high, (acc0, acc1, acc2), vel, descendants
    )

    def gathered(row, axes):
        count = lax.axis_size(axes)
        rows = jnp.broadcast_to(row, (count, slots))
        return jnp.sum(lax.all_to_all(rows, axes, 0, 0, tiled=True), axis=0, keepdims=True)

    sums = gathered(gathered(part, XYC), ZRING)
    mean_sq = jnp.sum(sums[:, :64]) / jnp.sum(sums[:, 64:])
    return jnp.transpose(drift, (0, 1, 3, 2, 4)), squared / (mean_sq + 1e-06)


def solution(mesh):
    finer = Mesh(mesh.devices.reshape(mesh.shape["gx"], 4, 2, 4, 2), AXES)
    return jax.shard_map(
        shards,
        mesh=finer,
        in_specs=(
            P("gx", GY, GZ, None, None),
            P("gx", GY, GZ, None, None),
            P("gx", GY, GZ, None, None),
            P("gx", GY, GZ),
            P("gx", GY, GZ, None),
            P("gx", GY, GZ, None, None),
        ),
        out_specs=(P("gx", GY, GZ, None, None), P("gx", GY, GZ, None)),
        check_vma=False,
    )
```

time: 110 us -> 107 us (0.973)
  Pallas kernels: 16.4 us -> 25.4 us
  starting transfers between devices: 39.5 us -> 33.7 us
  blocking collectives: 35.8 us -> 31.8 us
  waiting for transfers between devices: 12.5 us -> 9.51 us
  local copies, waits for them, and re-layouts: 0.92 us -> 2.39 us
    pallas_call x2 -> x5, Pallas kernels: 16.4 us -> 25.4 us  [the longest x2 9.76 us: more_forces(): pl.pallas_call(functools.partial(body, cap=cap), in_specs=[SMEM, SMEM, VM...]
    ppermute x5, starting transfers between devices: 23.2 us -> 17.5 us  [the longest x1 7.4 us: shards(): above = lax.ppermute(both(0), ZRING, zring_pairs(zs, -1))]
    all_to_all x2, blocking collectives: 35.8 us -> 31.8 us  [gathered(): lax.all_to_all(rows, axes, 0, 0, tiled=True)]
    ppermute x1, waiting for transfers between devices: 2.85 us -> 0.01 us  [shards(): other = lax.ppermute(own, 'gz_1', [(0, 1), (1, 0)])]
  transfers between devices with their start and end apart: 6 -> 6, of which waited for: 5 -> 2; matrix products, arithmetic and copies ran while one was open for 0% -> 0% of each run, Pallas kernels for 0% -> 16%
where the time goes in v3:
time: 107 us
  starting transfers between devices  33.7 us (31%)
  blocking collectives  31.8 us (30%)
  Pallas kernels  25.4 us (24%)
  waiting for transfers between devices  9.51 us (9%)
  local copies, waits for them, and re-layouts  2.39 us (2%)
  between operations  2.24 us (2%)
  other arithmetic  1.43 us (1%)
    all_to_all x2, blocking collectives, gathered(): lax.all_to_all(rows, axes, 0, 0, tiled=True)  31.8 us
    ppermute x1, starting transfers between devices, shards(): other = lax.ppermute(own, 'gz_1', [(0, 1), (1, 0)])  16.3 us
    pallas_call x2, Pallas kernels, more_forces(): pl.pallas_call(functools.partial(body, cap=cap), in_specs=[SMEM, SMEM, VM...  9.76 us
    pallas_call x1, Pallas kernels, first_forces(): pl.pallas_call(functools.partial(own_pass, cap=cap), in_specs=[SMEM, SMEM...  7.52 us
    ppermute x1, starting transfers between devices, shards(): above = lax.ppermute(both(0), ZRING, zring_pairs(zs, -1))  7.4 us
    pallas_call x1, Pallas kernels, finish(): pl.pallas_call(functools.partial(last_pass, cap=cap), in_specs=[SMEM] * 4...  6.58 us
    ppermute x1, waiting for transfers between devices, shards(): below = lax.ppermute(both(cx - 1), ZRING, zring_pairs(zs, 1))  5.47 us
    ppermute x1, starting transfers between devices, shards(): lax.ppermute(jnp.stack([v[:, cy - 1] for v in planes]), GY, ring(ny, 1))  4.95 us
  transfers between devices with their start and end apart: 6, of which 2 were waited for; matrix products, arithmetic and copies ran while one was open for 0% of the time, Pallas kernels for 16%

profile of v3, /device:TPU:1, one launch (start us, length us, event | category | flops | bytes accessed | tf_op | source)
XLA Modules:
  0.0 106.5 jit_solution(4618964351573628556)
XLA Ops:
  0.6 1.6 %shard_map.122.own_ref = f32[8,4,8,128]{3,2,1,0:T(8,128)} custom-call(s32[4,1,8]{2,1,0:T(1,128)} %bitcast.21, f32[8,4,1,4,128]{4,3,2,1,0:T(4,128)} %now_ref.1, f32[8,4,3,1,128]{4,3,2,1,0:T(1,128)} %bitcast.26), custom_call_target="tpu_custom_call" | custom-call | tf_op jit(solution)/shard_map/pallas_call | solution.py:378
  2.2 0.0 copy-start
  2.2 0.0 copy-start.5
  2.2 1.0 copy.35
  3.2 0.0 copy-start.4
  3.2 16.3 %collective-permute-start = (f32[8,4,8,128]{3,2,0,1:T(8,128)S(1)}, f32[8,4,8,128]{3,2,0,1:T(8,128)S(1)}, u32[]{:S(2)}, u32[]{:S(2)}) collective-permute-start(f32[8,4,8,128]{3,2,0,1:T(8,128)S(1)} %copy.35), channel_id=1, source_target_pairs={{0,1},{1,0},{2,3},{3,2},{4,5},{5,4},{6,7},{7,6},{8,9},{9,8},{10,11... | collective-permute-start | bytes 393224 | tf_op jit(solution)/shard_map/ppermute | solution.py:384
  19.5 0.0 copy-done
  19.5 0.0 copy-start.6
  19.5 0.0 copy-done.5
  19.5 0.0 copy-done.4
  19.5 0.7 copy-done.6
  20.2 7.5 %shard_map.123 = (s32[2080]{0:T(1024)S(1)}, s32[4]{0:T(128)S(1)}, f32[32,8,128]{2,1,0:T(8,128)S(1)}) custom-call(s32[1]{0:T(128)} %bitcast.half_ref, s32[486]{0:T(512)S(1)} %copy-done.6, s32[8,4,1,14]{3,2,1,0:T(1,128)S(1)} %copy-done.4, f32[27,8,128]{2,1,0:T(8,128)S(1)} %copy-done.5, f32[8,4,8,128]{3,2,1,0:T(8,128)S(1)} %copy-done), custom_call_target="tpu_custom_call" | custom-call | flops 734003200 | bytes 1048576 | tf_op jit(solution)/shard_map/pallas_call | solution.py:314
  27.7 0.0 collective-permute-done
  27.8 7.4 %collective-permute-start.2 = (f32[2,4,8,128]{3,2,0,1:T(8,128)S(1)}, f32[2,4,8,128]{3,2,0,1:T(8,128)S(1)}, u32[]{:S(2)}, u32[]{:S(2)}) collective-permute-start(f32[2,4,8,128]{3,2,0,1:T(8,128)S(1)} %maximum_select_fusion.1), channel_id=1, source_target_pairs={{0,449},{64,0},{128,64},{192,128},{256,192},{320,256},{384,320},{4... | collective-permute-start | bytes 98312 | tf_op jit(solution)/shard_map/ppermute | solution.py:392
  35.2 1.9 %collective-permute-start.1 = (f32[2,4,8,128]{3,2,0,1:T(8,128)S(1)}, f32[2,4,8,128]{3,2,0,1:T(8,128)S(1)}, u32[]{:S(2)}, u32[]{:S(2)}) collective-permute-start(f32[2,4,8,128]{3,2,0,1:T(8,128)S(1)} %maximum_select_fusion), channel_id=1, source_target_pairs={{0,64},{64,128},{128,192},{192,256},{256,320},{320,384},{384,448},... | collective-permute-start | bytes 98312 | tf_op jit(solution)/shard_map/ppermute | solution.py:391
  37.1 0.0 collective-permute-done.2
  37.1 5.5 %collective-permute-done.1 = f32[2,4,8,128]{3,2,0,1:T(8,128)S(1)} collective-permute-done((f32[2,4,8,128]{3,2,0,1:T(8,128)S(1)}, f32[2,4,8,128]{3,2,0,1:T(8,128)S(1)}, u32[]{:S(2)}, u32[]{:S(2)}) %collective-permute-start.1) | collective-permute-done | bytes 32800 | tf_op jit(solution)/shard_map/ppermute | solution.py:391
  42.6 3.2 %collective-permute-start.3 = (f32[10,4,8,128]{3,2,0,1:T(8,128)S(1)}, f32[10,4,8,128]{3,2,0,1:T(8,128)S(1)}, u32[]{:S(2)}, u32[]{:S(2)}) collective-permute-start(f32[10,4,8,128]{3,2,0,1:T(8,128)S(1)} %pad_maximum_fusion.1), channel_id=1, source_target_pairs={{0,2},{1,7},{2,4},{3,1},{4,6},{5,3},{6,0},{7,5},{8,10},{9,15},{10,... | collective-permute-start | bytes 491528 | tf_op jit(solution)/shard_map/ppermute | solution.py:400
  45.9 4.0 %collective-permute-done.3 = f32[10,4,8,128]{3,2,0,1:T(8,128)S(1)} collective-permute-done((f32[10,4,8,128]{3,2,0,1:T(8,128)S(1)}, f32[10,4,8,128]{3,2,0,1:T(8,128)S(1)}, u32[]{:S(2)}, u32[]{:S(2)}) %collective-permute-start.3) | collective-permute-done | bytes 163872 | tf_op jit(solution)/shard_map/ppermute | solution.py:400
  49.9 4.9 %collective-permute-start.4 = (f32[3,10,8,128]{3,2,1,0:T(8,128)S(1)}, f32[3,10,8,128]{3,2,1,0:T(8,128)S(1)}, u32[]{:S(2)}, u32[]{:S(2)}) collective-permute-start(f32[3,10,8,128]{3,2,1,0:T(8,128)S(1)} %pad_maximum_fusion.2), channel_id=1, source_target_pairs={{0,8},{8,16},{16,24},{24,32},{32,40},{40,48},{48,56},{56,0},{1,9},... | collective-permute-start | bytes 368648 | tf_op jit(solution)/shard_map/ppermute | solution.py:403
  54.9 0.0 collective-permute-start.5
  54.9 4.9 %shard_map.124.acc1_ref = f32[32,8,128]{2,1,0:T(8,128)S(1)} custom-call(s32[2080]{0:T(1024)S(1)} %get-tuple-element.8.list_ref, s32[4]{0:T(128)S(1)} %get-tuple-element.9.count_ref, f32[27,8,128]{2,1,0:T(8,128)S(1)} %copy-done.5, f32[10,4,8,128]{3,2,1,0:T(8,128)S(1)} %copy.43.own_ref, f32[10,4,8,128]{3,2,1,0:T(8,128)S(1)} %copy.44.other_ref), custom_call_target="tpu_custom_call" | custom-call | flops 851968000 | bytes 1048576 | tf_op jit(solution)/shard_map/pallas_call | solution.py:333
  59.9 0.0 copy-start.2
  59.9 0.0 copy-start.3
  59.9 4.8 %shard_map.125.acc2_ref = f32[32,8,128]{2,1,0:T(8,128)S(1)} custom-call(s32[2080]{0:T(1024)S(1)} %get-tuple-element.8.list_ref, s32[4]{0:T(128)S(1)} %get-tuple-element.9.count_ref, f32[27,8,128]{2,1,0:T(8,128)S(1)} %copy-done.5, f32[10,4,8,128]{3,2,1,0:T(8,128)S(1)} %copy.43.own_ref, f32[10,4,8,128]{3,2,1,0:T(8,128)S(1)} %copy.45.far_ref), custom_call_target="tpu_custom_call" | custom-call | flops 851968000 | bytes 1048576 | tf_op jit(solution)/shard_map/pallas_call | solution.py:333
  64.7 0.0 copy-start.1
  64.7 0.0 collective-permute-done.4.low_ref
  64.8 0.0 collective-permute-done.5.high_ref
  64.8 0.0 copy-done.2
  64.8 0.0 copy-done.3
  64.8 0.6 copy-done.1
  65.4 6.6 %shard_map.126 = (f32[8,4,3,1,128]{4,3,2,1,0:T(1,128)}, f32[8,4,1,128]{3,2,1,0:T(1,128)S(1)}, f32[1,128]{1,0:T(1,128)S(1)}) custom-call(s32[1]{0:T(128)} %bitcast.half_ref, s32[2080]{0:T(1024)S(1)} %get-tuple-element.8.list_ref, s32[4]{0:T(128)S(1)} %get-tuple-element.9.count_ref, s32[4,1,8]{2,1,0:T(1,128)S(1)} %bitcast.22, f32[27,8,128]{2,1,0:T(8,128)S(1)} %copy-done.5, ...), custom_call_target="tpu_custom_call" | custom-call | flops 851968000 | bytes 1048576 | tf_op jit(solution)/shard_map/pallas_call | solution.py:348
  72.0 12.3 %all_to_all.12 = f32[32,1,128]{2,1,0:T(1,128)S(1)} all-to-all(f32[32,1,128]{2,1,0:T(1,128)S(1)} %broadcast_in_dim.9), channel_id=1, replica_groups=mesh['gx'=8,'gy_0'=4,'gy_1'=2,'gz_0'=4,'gz_1'=2] {'gz_0','gy_0','gy_1'}, dimensions={0} | all-to-all | bytes 32768 | tf_op jit(solution)/shard_map/all_to_all | solution.py:413
  84.3 19.5 %all_to_all.13 = f32[16,1,128]{2,1,0:T(1,128)S(1)} all-to-all(f32[16,1,128]{2,1,0:T(1,128)S(1)} %broadcast_in_dim.10), channel_id=1, replica_groups=mesh['gx'=8,'gy_0'=4,'gy_1'=2,'gz_0'=4,'gz_1'=2] {'gx','gz_1'}, dimensions={0} | all-to-all | bytes 16384 | tf_op jit(solution)/shard_map/all_to_all | solution.py:413
  103.9 0.7 slice_reduce_fusion
  105.9 0.6 broadcast_divide_fusion
  (19 shorter events, 0.2 us)
Async XLA Ops:
  2.2 17.3 %copy-start = (f32[8,4,8,128]{3,2,1,0:T(8,128)S(1)}, f32[8,4,8,128]{3,2,1,0:T(8,128)}, u32[]{:S(2)}) copy-start(f32[8,4,8,128]{3,2,1,0:T(8,128)} %shard_map.122.own_ref) | copy-start | bytes 393220
  2.2 17.3 %copy-start.5 = (f32[27,8,128]{2,1,0:T(8,128)S(1)}, f32[27,8,128]{2,1,0:T(8,128)}, u32[]{:S(2)}) copy-start(f32[27,8,128]{2,1,0:T(8,128)} %constant.17.clone.off_ref) | copy-start | bytes 331780
  3.2 16.3 %copy-start.4 = (s32[8,4,1,14]{3,2,1,0:T(1,128)S(1)}, s32[8,4,1,14]{3,2,1,0:T(1,128)}, u32[]{:S(2)}) copy-start(s32[8,4,1,14]{3,2,1,0:T(1,128)} %nbr_ref.1) | copy-start | bytes 5380
  3.2 24.5 %collective-permute-start = (f32[8,4,8,128]{3,2,0,1:T(8,128)S(1)}, f32[8,4,8,128]{3,2,0,1:T(8,128)S(1)}, u32[]{:S(2)}, u32[]{:S(2)}) collective-permute-start(f32[8,4,8,128]{3,2,0,1:T(8,128)S(1)} %copy.35), channel_id=1, source_target_pairs={{0,1},{1,0},{2,3},{3,2},{4,5},{5,4},{6,7},{7,6},{8,9},{9,8},{10,11... | collective-permute-start | bytes 393224 | tf_op jit(solution)/shard_map/ppermute | solution.py:384
  19.5 0.7 copy-start.6
  27.8 9.4 %collective-permute-start.2 = (f32[2,4,8,128]{3,2,0,1:T(8,128)S(1)}, f32[2,4,8,128]{3,2,0,1:T(8,128)S(1)}, u32[]{:S(2)}, u32[]{:S(2)}) collective-permute-start(f32[2,4,8,128]{3,2,0,1:T(8,128)S(1)} %maximum_select_fusion.1), channel_id=1, source_target_pairs={{0,449},{64,0},{128,64},{192,128},{256,192},{320,256},{384,320},{4... | collective-permute-start | bytes 98312 | tf_op jit(solution)/shard_map/ppermute | solution.py:392
  35.2 7.4 %collective-permute-start.1 = (f32[2,4,8,128]{3,2,0,1:T(8,128)S(1)}, f32[2,4,8,128]{3,2,0,1:T(8,128)S(1)}, u32[]{:S(2)}, u32[]{:S(2)}) collective-permute-start(f32[2,4,8,128]{3,2,0,1:T(8,128)S(1)} %maximum_select_fusion), channel_id=1, source_target_pairs={{0,64},{64,128},{128,192},{192,256},{256,320},{320,384},{384,448},... | collective-permute-start | bytes 98312 | tf_op jit(solution)/shard_map/ppermute | solution.py:391
  42.6 7.3 %collective-permute-start.3 = (f32[10,4,8,128]{3,2,0,1:T(8,128)S(1)}, f32[10,4,8,128]{3,2,0,1:T(8,128)S(1)}, u32[]{:S(2)}, u32[]{:S(2)}) collective-permute-start(f32[10,4,8,128]{3,2,0,1:T(8,128)S(1)} %pad_maximum_fusion.1), channel_id=1, source_target_pairs={{0,2},{1,7},{2,4},{3,1},{4,6},{5,3},{6,0},{7,5},{8,10},{9,15},{10,... | collective-permute-start | bytes 491528 | tf_op jit(solution)/shard_map/ppermute | solution.py:400
  49.9 14.8 %collective-permute-start.4 = (f32[3,10,8,128]{3,2,1,0:T(8,128)S(1)}, f32[3,10,8,128]{3,2,1,0:T(8,128)S(1)}, u32[]{:S(2)}, u32[]{:S(2)}) collective-permute-start(f32[3,10,8,128]{3,2,1,0:T(8,128)S(1)} %pad_maximum_fusion.2), channel_id=1, source_target_pairs={{0,8},{8,16},{16,24},{24,32},{32,40},{40,48},{48,56},{56,0},{1,9},... | collective-permute-start | bytes 368648 | tf_op jit(solution)/shard_map/ppermute | solution.py:403
  54.9 9.9 %collective-permute-start.5 = (f32[3,10,8,128]{3,2,1,0:T(8,128)S(1)}, f32[3,10,8,128]{3,2,1,0:T(8,128)S(1)}, u32[]{:S(2)}, u32[]{:S(2)}) collective-permute-start(f32[3,10,8,128]{3,2,1,0:T(8,128)S(1)} %pad_maximum_fusion.3), channel_id=1, source_target_pairs={{0,56},{8,0},{16,8},{24,16},{32,24},{40,32},{48,40},{56,48},{1,57}... | collective-permute-start | bytes 368648 | tf_op jit(solution)/shard_map/ppermute | solution.py:404
  59.9 4.9 %copy-start.2 = (f32[8,4,1,3,128]{4,2,3,1,0:T(1,128)S(1)}, f32[8,4,1,3,128]{4,2,3,1,0:T(1,128)}, u32[]{:S(2)}) copy-start(f32[8,4,1,3,128]{4,2,3,1,0:T(1,128)} %param.12) | copy-start | bytes 147460
  59.9 4.9 %copy-start.3 = (s32[8,4,1,2,128]{4,3,2,1,0:T(2,128)S(1)}, s32[8,4,1,2,128]{4,3,2,1,0:T(2,128)}, u32[]{:S(2)}) copy-start(s32[8,4,1,2,128]{4,3,2,1,0:T(2,128)} %desc_ref.1) | copy-start | bytes 98308
  64.7 0.7 copy-start.1

commit v4 on v3

--- a/solution.py
+++ b/solution.py
@@ -50,12 +50,14 @@
 
 def assemble(cnt_ref, now_ref, next_ref, own_ref):
     lane = lax.broadcasted_iota(jnp.int32, (1, 128), 1)
-    for x in range(now_ref.shape[0]):
-        for y in range(now_ref.shape[1]):
-            own_ref[x, y, :3] = now_ref[x, y, 0, :3]
-            own_ref[x, y, 3:4] = jnp.where(lane < cnt_ref[y, 0, x], now_ref[x, y, 0, 3:4], 0.0)
-            own_ref[x, y, 4:7] = next_ref[x, y, :, 0]
-            own_ref[x, y, 7:] = jnp.zeros((1, 128), jnp.float32)
+    cx, cy = now_ref.shape[:2]
+    for x in range(cx):
+        for y in range(cy):
+            cell = x * cy + y
+            own_ref[cell, :3] = now_ref[x, y, 0, :3]
+            own_ref[cell, 3:4] = jnp.where(lane < cnt_ref[y, 0, x], now_ref[x, y, 0, 3:4], 0.0)
+            own_ref[cell, 4:7] = next_ref[x, y, :, 0]
+            own_ref[cell, 7:] = jnp.zeros((1, 128), jnp.float32)
 
 
 CLASSES = 4
@@ -144,10 +146,14 @@
     lax.fori_loop(0, (count + BATCH - 1) // BATCH, batch, 0)
 
 
-def own_pass(half_ref, table_ref, nbr_ref, off_ref, own_ref, list_ref, count_ref, acc_ref, st_ref, mc_ref, *, cap):
-    cx, cy = own_ref.shape[0], own_ref.shape[1]
+def own_pass(
+    half_ref, table_ref, nbr_ref, cnt_ref, off_ref, own_ref, vel_ref, desc_ref,
+    list_ref, count_ref, acc_ref, base_ref, link_ref, st_ref, mc_ref, *, cap
+):
+    cx, cy = nbr_ref.shape[:2]
     width = nbr_ref.shape[3]
     half = half_ref[0]
+    lane = lax.broadcasted_iota(I32, (1, 128), 1)
     for kind in range(CLASSES):
         count_ref[kind] = 0
     acc_ref[...] = jnp.zeros(acc_ref.shape, F32)
@@ -165,62 +171,70 @@
                 place = count_ref[kind]
                 list_ref[kind * cap + place] = item
                 count_ref[kind] = place + 1
-            source_features(own_ref[x, y], cell, st_ref, mc_ref)
+            own = own_ref[cell]
+            source_features(own, cell, st_ref, mc_ref)
+            dcode = desc_ref[x, y, 0, 0:1, :]
+            ox = (dcode >= 9).astype(I32) + (dcode >= 18).astype(I32)
+            rest = dcode - 9 * ox
+            oy = (rest >= 3).astype(I32) + (rest >= 6).astype(I32)
+            oz = rest - 3 * oy
+            offset = jnp.concatenate([ox, oy, oz], axis=0).astype(F32) - 1.0
+            base_ref[cell, :3] = offset - (own[:3] + STEP_DT * vel_ref[x, y, :, 0])
+            base_ref[cell, 3:4] = (lane < cnt_ref[y, 0, x]).astype(F32)
+            link_ref[cell, :2] = desc_ref[x, y, 0]
         return carry
 
     lax.fori_loop(0, cx, one_row, 0)
-    run_items(0, cap, list_ref, count_ref, st_ref, mc_ref, lambda c: own_ref[c // cy, c % cy], off_ref, acc_ref)
-
-
-def other_pass(list_ref, count_ref, off_ref, own_ref, other_ref, acc_ref, st_ref, mc_ref, *, cap):
-    px, cy = own_ref.shape[0], own_ref.shape[1]
+    run_items(0, cap, list_ref, count_ref, st_ref, mc_ref, lambda c: own_ref[c], off_ref, acc_ref)
+
+
+def all_features(ref, count, st_ref, mc_ref):
+    part = count // 2
+
+    def some(i, carry):
+        for step in range(part):
+            source_features(ref[i * part + step], i * part + step, st_ref, mc_ref)
+        return carry
+
+    lax.fori_loop(0, 2, some, 0)
+
+
+def other_pass(
+    list_ref, count_ref, off_ref, own_ref, other_ref, acc_ref, top_ref, bottom_ref, st_ref, mc_ref, *, cap
+):
+    px = top_ref.shape[1]
+    cells = own_ref.shape[0]
+    cy = cells // px
     acc_ref[...] = jnp.zeros(acc_ref.shape, F32)
-
-    rows = px // 2
-
-    def some_rows(part, carry):
-        for step in range(rows):
-            x = part * rows + step
-            for y in range(cy):
-                source_features(other_ref[x, y], x * cy + y, st_ref, mc_ref)
-        return carry
-
-    lax.fori_loop(0, 2, some_rows, 0)
+    for plane, ref in enumerate((own_ref, other_ref)):
+        for x in range(px):
+            top_ref[plane, x] = ref[x * cy + cy - 1]
+            bottom_ref[plane, x] = ref[x * cy]
+    all_features(other_ref, cells, st_ref, mc_ref)
     for y in range(cy):
-        source_features(own_ref[0, y], px * cy + y, st_ref, mc_ref)
-        source_features(own_ref[px - 1, y], (px + 1) * cy + y, st_ref, mc_ref)
-    run_items(1, cap, list_ref, count_ref, st_ref, mc_ref, lambda c: own_ref[c // cy + 1, c % cy], off_ref, acc_ref)
+        source_features(own_ref[y], cells + y, st_ref, mc_ref)
+        source_features(own_ref[cells - cy + y], cells + cy + y, st_ref, mc_ref)
+    run_items(1, cap, list_ref, count_ref, st_ref, mc_ref, lambda c: own_ref[c + cy], off_ref, acc_ref)
 
 
 def far_pass(list_ref, count_ref, off_ref, own_ref, far_ref, acc_ref, st_ref, mc_ref, *, cap):
-    px, cy = own_ref.shape[0], own_ref.shape[1]
+    edge = (own_ref.shape[0] - acc_ref.shape[0]) // 2
     acc_ref[...] = jnp.zeros(acc_ref.shape, F32)
-
-    rows = px // 2
-
-    def some_rows(part, carry):
-        for step in range(rows):
-            x = part * rows + step
-            for y in range(cy):
-                source_features(far_ref[x, y], x * cy + y, st_ref, mc_ref)
-        return carry
-
-    lax.fori_loop(0, 2, some_rows, 0)
-    run_items(2, cap, list_ref, count_ref, st_ref, mc_ref, lambda c: own_ref[c // cy + 1, c % cy], off_ref, acc_ref)
+    all_features(far_ref, far_ref.shape[0], st_ref, mc_ref)
+    run_items(2, cap, list_ref, count_ref, st_ref, mc_ref, lambda c: own_ref[c + edge], off_ref, acc_ref)
 
 
 def last_pass(
-    half_ref, list_ref, count_ref, cnt_ref, off_ref, own_ref, other_ref, far_ref, low_ref, high_ref,
-    acc0_ref, acc1_ref, acc2_ref, vel_ref, desc_ref,
+    half_ref, list_ref, count_ref, off_ref, own_ref, other_ref, far_ref, low_ref, high_ref,
+    acc0_ref, acc1_ref, acc2_ref, base_ref, link_ref,
     drift_ref, sq_ref, part_ref,
     acc_ref, st_ref, mc_ref, cube_ref, out_ref, sems, *, cap
 ):
-    px, cy = own_ref.shape[0], own_ref.shape[1]
-    cx = px - 2
+    cx, cy = out_ref.shape[:2]
+    px = cx + 2
     half = half_ref[0]
     lane = lax.broadcasted_iota(I32, (1, 128), 1)
     acc_ref[...] = acc0_ref[...] + acc1_ref[...] + acc2_ref[...]
-
     rows = px // 2
 
     def strips(part, carry):
@@ -232,12 +246,13 @@
         return carry
 
     lax.fori_loop(0, 2, strips, 0)
-    run_items(3, cap, list_ref, count_ref, st_ref, mc_ref, lambda c: own_ref[c // cy + 1, c % cy], off_ref, acc_ref)
+    run_items(3, cap, list_ref, count_ref, st_ref, mc_ref, lambda c: own_ref[c + cy], off_ref, acc_ref)
 
     def fill(z, ref, plane):
-        cube_ref[z, :, 0] = low_ref[plane]
-        cube_ref[z, :, 1 : cy + 1] = ref[...]
-        cube_ref[z, :, cy + 1] = high_ref[plane]
+        for x in range(px):
+            cube_ref[z, x, 0] = low_ref[plane, x]
+            cube_ref[z, x, 1 : cy + 1] = ref[x * cy : (x + 1) * cy]
+            cube_ref[z, x, cy + 1] = high_ref[plane, x]
 
     fill(1, own_ref, 0)
 
@@ -252,42 +267,50 @@
         fill(2, far_ref, 2)
 
     def one_cell(x, y):
-        own = own_ref[x + 1, y]
-        accel = acc_ref[x * cy + y]
-        dcode = desc_ref[x, y, 0, 0:1, :]
-        dslot = jnp.broadcast_to(desc_ref[x, y, 0, 1:2, :], (8, 128))
+        cell = x * cy + y
+        dcode = link_ref[cell, 0:1]
+        dslot = jnp.broadcast_to(link_ref[cell, 1:2], (8, 128))
         found = jnp.zeros((8, 128), F32)
         for code in range(27):
             dx, dy, dz = code // 9, code // 3 % 3, code % 3
             got = jnp.take_along_axis(cube_ref[dz, x + dx, y + dy], dslot, axis=1)
             found = jnp.where(dcode == code, got, found)
-        ox = (dcode >= 9).astype(I32) + (dcode >= 18).astype(I32)
-        rest = dcode - 9 * ox
-        oy = (rest >= 3).astype(I32) + (rest >= 6).astype(I32)
-        oz = rest - 3 * oy
-        offset = jnp.concatenate([ox, oy, oz], axis=0).astype(F32) - 1.0
-        predicted = own[:3] + STEP_DT * vel_ref[x, y, :, 0] + HALF_KICK * accel[:3]
-        error = offset + found[4:7] - predicted
-        alive = lane < cnt_ref[y, 0, x]
-        out_ref[x, y, :, 0] = jnp.where(alive, error, 0.0)
-        squared = jnp.where(alive, jnp.sum(error * error, axis=0, keepdims=True), 0.0)
+        error = base_ref[cell, :3] + found[4:7] - HALF_KICK * acc_ref[cell, :3]
+        alive = base_ref[cell, 3:4]
+        out_ref[x, y, :, 0] = jnp.where(alive > 0.0, error, 0.0)
+        squared = jnp.where(alive > 0.0, jnp.sum(error * error, axis=0, keepdims=True), 0.0)
         sq_ref[x, y] = squared
-        return squared
+        return squared, alive
 
     def one_row(x, carry):
-        total, count = carry
+        total, live = carry
         for y in range(cy):
-            total = total + one_cell(x, y)
-            count = count + cnt_ref[y, 0, x]
+            squared, alive = one_cell(x, y)
+            total = total + squared
+            live = live + alive
         pltpu.make_async_copy(out_ref.at[x], drift_ref.at[x], sems.at[x]).start()
-        return total, count
-
-    total, count = lax.fori_loop(0, cx, one_row, (jnp.zeros((1, 128), F32), jnp.int32(0)))
-    folded = total + pltpu.roll(jnp.broadcast_to(total, (8, 128)), 64, 1)[:1]
-    live = jnp.where(lane == 64, count.astype(F32), 0.0)
-    part_ref[...] = jnp.where(lane < 64, folded, live)
+        return total, live
+
+    zero = jnp.zeros((1, 128), F32)
+    total, live = lax.fori_loop(0, cx, one_row, (zero, zero))
+
+    def folded(v):
+        return v + pltpu.roll(jnp.broadcast_to(v, (8, 128)), 64, 1)[:1]
+
+    part_ref[...] = jnp.where(lane < 64, folded(total), folded(live))
     for x in range(cx):
         pltpu.make_async_copy(out_ref.at[x], drift_ref.at[x], sems.at[x]).wait()
+
+
+def scaled(rows_ref, sq_ref, tension_ref):
+    lane = lax.broadcasted_iota(I32, (1, 128), 1)
+    sums = jnp.sum(rows_ref[...], axis=0, keepdims=True)
+    total = jnp.sum(jnp.where(lane < 64, sums, 0.0), axis=1, keepdims=True)
+    live = jnp.sum(jnp.where(lane < 64, 0.0, sums), axis=1, keepdims=True)
+    bound = jnp.broadcast_to(total / live + 1e-06, (1, 128))
+    for x in range(sq_ref.shape[0]):
+        for y in range(sq_ref.shape[1]):
+            tension_ref[x, y] = sq_ref[x, y] / bound
 
 
 SMEM = pl.BlockSpec(memory_space=pltpu.SMEM)
@@ -307,47 +330,62 @@
     return [pltpu.VMEM((sources, 128, 48), BF16), pltpu.VMEM((sources, 32, 128), BF16)]
 
 
-def first_forces(half, neighbour_lists, own):
-    cx, cy = own.shape[:2]
-    items = cx * cy * neighbour_lists.shape[3]
+def first_forces(half, neighbour_lists, cnt, own, vel, descendants):
+    cx, cy = neighbour_lists.shape[:2]
+    cells = cx * cy
+    items = cells * neighbour_lists.shape[3]
     cap = items + 2 * BATCH
+    rows = jax.ShapeDtypeStruct((cells, 8, 128), F32)
     return pl.pallas_call(
         functools.partial(own_pass, cap=cap),
-        in_specs=[SMEM, SMEM, SMEM, VMEM, VMEM],
-        out_specs=[SMEM, SMEM, VMEM],
+        in_specs=[SMEM] * 4 + [VMEM] * 4,
+        out_specs=[SMEM, SMEM, VMEM, VMEM, VMEM],
         out_shape=[
             jax.ShapeDtypeStruct((CLASSES * cap,), I32),
             jax.ShapeDtypeStruct((CLASSES,), I32),
-            jax.ShapeDtypeStruct((cx * cy, 8, 128), F32),
+            rows,
+            rows,
+            jax.ShapeDtypeStruct((cells, 8, 128), I32),
         ],
-        scratch_shapes=features_of(cx * cy),
+        scratch_shapes=features_of(cells),
         cost_estimate=cost(items // 4),
         compiler_params=params(),
-    )(half, item_table(cx, cy), neighbour_lists, offset_table(), own)
-
-
-def more_forces(body, lists, counts, own, planes):
-    px, cy = own.shape[:2]
-    cells = (px - 2) * cy
+    )(half, item_table(cx, cy), neighbour_lists, cnt, offset_table(), own, vel, descendants)
+
+
+def other_forces(lists, counts, own, other, cells, px):
+    cap = lists.shape[0] // CLASSES
+    strip = jax.ShapeDtypeStruct((2, px, 8, 128), F32)
+    return pl.pallas_call(
+        functools.partial(other_pass, cap=cap),
+        in_specs=[SMEM, SMEM, VMEM, VMEM, VMEM],
+        out_specs=[VMEM] * 3,
+        out_shape=[jax.ShapeDtypeStruct((cells, 8, 128), F32), strip, strip],
+        scratch_shapes=features_of(2 * own.shape[0] - cells),
+        cost_estimate=cost(cap // 4),
+        compiler_params=params(),
+    )(lists, counts, offset_table(), own, other)
+
+
+def far_forces(lists, counts, own, far, cells):
     cap = lists.shape[0] // CLASSES
     return pl.pallas_call(
-        functools.partial(body, cap=cap),
+        functools.partial(far_pass, cap=cap),
         in_specs=[SMEM, SMEM, VMEM, VMEM, VMEM],
         out_specs=VMEM,
         out_shape=jax.ShapeDtypeStruct((cells, 8, 128), F32),
-        scratch_shapes=features_of((px + 2) * cy),
+        scratch_shapes=features_of(far.shape[0]),
         cost_estimate=cost(cap // 4),
         compiler_params=params(),
-    )(lists, counts, offset_table(), own, planes)
-
-
-def finish(half, lists, counts, cnt, own, other, far, low, high, sums, vel, descendants):
-    px, cy = own.shape[:2]
-    cx = px - 2
+    )(lists, counts, offset_table(), own, far)
+
+
+def finish(half, lists, counts, planes, low, high, sums, base, links, cx, cy):
+    px = cx + 2
     cap = lists.shape[0] // CLASSES
     return pl.pallas_call(
         functools.partial(last_pass, cap=cap),
-        in_specs=[SMEM] * 4 + [VMEM] * 11,
+        in_specs=[SMEM] * 3 + [VMEM] * 11,
         out_specs=[pl.BlockSpec(memory_space=pl.ANY), VMEM, VMEM],
         out_shape=[
             jax.ShapeDtypeStruct((cx, cy, 3, 1, 128), F32),
@@ -363,7 +401,7 @@
         ],
         cost_estimate=cost(cap // 4),
         compiler_params=params(),
-    )(half, lists, counts, cnt, offset_table(), own, other, far, low, high, *sums, vel, descendants)
+    )(half, lists, counts, offset_table(), *planes, low, high, *sums, base, links)
 
 
 def shards(positions_now, velocities, positions_next, halo_counts, neighbour_lists, descendants):
@@ -379,42 +417,46 @@
         assemble,
         in_specs=[SMEM, VMEM, VMEM],
         out_specs=VMEM,
-        out_shape=jax.ShapeDtypeStruct((cx, cy, 8, slots), F32),
+        out_shape=jax.ShapeDtypeStruct((cx * cy, 8, slots), F32),
     )(cnt, positions_now, nxt)
     other = lax.ppermute(own, "gz_1", [(0, 1), (1, 0)])
-    lists, counts, acc0 = first_forces(half[None], neighbour_lists, own)
-
-    def both(x):
-        ends = own[x], other[x]
+    lists, counts, acc0, base, links = first_forces(half[None], neighbour_lists, cnt, own, vel, descendants)
+
+    def both(start):
+        ends = own[start : start + cy], other[start : start + cy]
         return jnp.where(half == 0, jnp.stack(ends), jnp.stack(ends[::-1]))
 
-    below = lax.ppermute(both(cx - 1), ZRING, zring_pairs(zs, 1))
+    below = lax.ppermute(both(cx * cy - cy), ZRING, zring_pairs(zs, 1))
     above = lax.ppermute(both(0), ZRING, zring_pairs(zs, -1))
 
     def widened(block, plane):
-        ends = [jnp.where(plane == 0, v[0], v[1])[None] for v in (below, above)]
+        ends = [jnp.where(plane == 0, v[0], v[1]) for v in (below, above)]
         return jnp.concatenate([ends[0], block, ends[1]], axis=0)
 
     own = widened(own, half)
     other = widened(other, 1 - half)
     far = lax.ppermute(other, GZ, xhop_pairs(xs))
-    acc1 = more_forces(other_pass, lists, counts, own, other)
-    planes = (own, other, far)
-    low = lax.ppermute(jnp.stack([v[:, cy - 1] for v in planes]), GY, ring(ny, 1))
-    high = lax.ppermute(jnp.stack([v[:, 0] for v in planes]), GY, ring(ny, -1))
-    acc2 = more_forces(far_pass, lists, counts, own, far)
+    acc1, top, bottom = other_forces(lists, counts, own, other, cx * cy, cx + 2)
+    rows = far.reshape(cx + 2, cy * 8, slots)
+    low = lax.ppermute(jnp.concatenate([top, rows[None, :, 8 * cy - 8 :]]), GY, ring(ny, 1))
+    high = lax.ppermute(jnp.concatenate([bottom, rows[None, :, :8]]), GY, ring(ny, -1))
+    acc2 = far_forces(lists, counts, own, far, cx * cy)
     drift, squared, part = finish(
-        half[None], lists, counts, cnt, *planes, low, high, (acc0, acc1, acc2), vel, descendants
+        half[None], lists, counts, (own, other, far), low, high, (acc0, acc1, acc2), base, links, cx, cy
     )
 
     def gathered(row, axes):
         count = lax.axis_size(axes)
-        rows = jnp.broadcast_to(row, (count, slots))
-        return jnp.sum(lax.all_to_all(rows, axes, 0, 0, tiled=True), axis=0, keepdims=True)
-
-    sums = gathered(gathered(part, XYC), ZRING)
-    mean_sq = jnp.sum(sums[:, :64]) / jnp.sum(sums[:, 64:])
-    return jnp.transpose(drift, (0, 1, 3, 2, 4)), squared / (mean_sq + 1e-06)
+        return lax.all_to_all(jnp.broadcast_to(row, (count, slots)), axes, 0, 0, tiled=True)
+
+    sums = jnp.sum(gathered(part, XYC), axis=0, keepdims=True)
+    tension = pl.pallas_call(
+        scaled,
+        in_specs=[VMEM, VMEM],
+        out_specs=VMEM,
+        out_shape=jax.ShapeDtypeStruct((cx, cy, cz, slots), F32),
+    )(gathered(sums, ZRING), squared)
+    return jnp.transpose(drift, (0, 1, 3, 2, 4)), tension
 
 
 def solution(mesh):

time: 107 us -> 99.7 us (0.932)
  waiting for transfers between devices: 9.51 us -> 5.48 us
  starting transfers between devices: 33.7 us -> 31.4 us
  between operations: 2.24 us -> 0.86 us
  other arithmetic: 1.43 us -> 0.09 us
    ppermute x1, waiting for transfers between devices: 4.03 us -> 0.01 us  [shards(): far = lax.ppermute(other, GZ, xhop_pairs(xs))]
    ppermute x1, starting transfers between devices: 7.4 us -> 5.86 us  [shards(): above = lax.ppermute(both(0), ZRING, zring_pairs(zs, -1))]
    pallas_call x4 -> x5, Pallas kernels: 23.9 us -> 24.5 us  [the longest x1 7.61 us: first_forces(): pl.pallas_call(functools.partial(own_pass, cap=cap), in_specs=[SMEM] * 4...]
  transfers between devices with their start and end apart: 6 -> 6, of which waited for: 2 -> 1; matrix products, arithmetic and copies ran while one was open for 0% -> 1% of each run, Pallas kernels for 16% -> 18%
where the time goes in v4:
time: 99.7 us; the launch traced here: 99.1 us
  blocking collectives  32.8 us (33%)
  starting transfers between devices  31.4 us (31%)
  Pallas kernels  26.1 us (26%)
  waiting for transfers between devices  5.48 us (5%)
  local copies, waits for them, and re-layouts  2.39 us (2%)
    all_to_all x2, blocking collectives, gathered(): lax.all_to_all(jnp.broadcast_to(row, (count, slots)), axes, 0, 0, tiled=T...  32.8 us
    ppermute x1, starting transfers between devices, shards(): other = lax.ppermute(own, 'gz_1', [(0, 1), (1, 0)])  16.4 us
    pallas_call x1, Pallas kernels, first_forces(): pl.pallas_call(functools.partial(own_pass, cap=cap), in_specs=[SMEM] * 4...  7.61 us
    ppermute x1, starting transfers between devices, shards(): above = lax.ppermute(both(0), ZRING, zring_pairs(zs, -1))  5.86 us
    pallas_call x1, Pallas kernels, finish(): pl.pallas_call(functools.partial(last_pass, cap=cap), in_specs=[SMEM] * 3...  5.66 us
    ppermute x1, waiting for transfers between devices, shards(): below = lax.ppermute(both(cx * cy - cy), ZRING, zring_pairs(zs, 1))  5.47 us
    pallas_call x1, Pallas kernels, other_forces(): pl.pallas_call(functools.partial(other_pass, cap=cap), in_specs=[SMEM, SM...  4.95 us
    pallas_call x1, Pallas kernels, far_forces(): pl.pallas_call(functools.partial(far_pass, cap=cap), in_specs=[SMEM, SMEM...  4.8 us
  transfers between devices with their start and end apart: 6, of which 1 were waited for; matrix products, arithmetic and copies ran while one was open for 1% of the time, Pallas kernels for 18%

profile of v4, /device:TPU:1, one launch (start us, length us, event | category | flops | bytes accessed | tf_op | source)
XLA Modules:
  0.0 99.1 jit_solution(12721333719678835956)
XLA Ops:
  0.6 0.0 copy-start.4
  0.6 0.0 copy-start.6
  0.7 1.6 %shard_map.122.own_ref = f32[32,8,128]{2,1,0:T(8,128)} custom-call(s32[4,1,8]{2,1,0:T(1,128)} %bitcast.30, f32[8,4,1,4,128]{4,3,2,1,0:T(4,128)} %now_ref.1, f32[8,4,3,1,128]{4,3,2,1,0:T(1,128)} %bitcast.35), custom_call_target="tpu_custom_call" | custom-call | tf_op jit(solution)/shard_map/pallas_call | solution.py:416
  2.3 0.0 copy-start.3
  2.3 0.0 copy-start.5
  2.3 16.4 %collective-permute-start = (f32[32,8,128]{2,1,0:T(8,128)}, f32[32,8,128]{2,1,0:T(8,128)S(1)}, u32[]{:S(2)}, u32[]{:S(2)}) collective-permute-start(f32[32,8,128]{2,1,0:T(8,128)} %shard_map.122.own_ref), channel_id=1, source_target_pairs={{0,1},{1,0},{2,3},{3,2},{4,5},{5,4},{6,7},{7,6},{8,9},{9,8},{10,11... | collective-permute-start | bytes 393224 | tf_op jit(solution)/shard_map/ppermute | solution.py:422
  18.7 0.8 slice_bitcast_fusion.5
  19.4 0.0 copy-start.7
  19.4 0.0 copy-start.2
  19.4 0.0 copy-done.4
  19.4 0.0 copy-done.6
  19.5 0.0 copy-done.3
  19.5 0.0 copy-done.5
  19.5 0.6 copy-done.7
  20.1 0.0 copy-done.2
  20.1 0.0 copy-start
  20.1 0.9 copy-done
  21.0 7.6 %shard_map.123 = (s32[2080]{0:T(1024)S(1)}, s32[4]{0:T(128)S(1)}, f32[32,8,128]{2,1,0:T(8,128)S(1)}, f32[32,8,128]{2,1,0:T(8,128)S(1)}, s32[32,8,128]{2,1,0:T(8,128)S(1)}) custom-call(s32[1]{0:T(128)} %bitcast.half_ref, s32[486]{0:T(512)S(1)} %copy-done.7, s32[8,4,1,14]{3,2,1,0:T(1,128)S(1)} %copy-done.5, s32[4,1,8]{2,1,0:T(1,128)S(1)} %bitcast.31, ...), custom_call_target="tpu_custom_call" | custom-call | flops 734003200 | bytes 1048576 | tf_op jit(solution)/shard_map/pallas_call | solution.py:339
  28.7 0.0 collective-permute-done
  28.7 5.9 %collective-permute-start.2 = (f32[2,4,8,128]{3,2,1,0:T(8,128)S(1)}, f32[2,4,8,128]{3,2,1,0:T(8,128)S(1)}, u32[]{:S(2)}, u32[]{:S(2)}) collective-permute-start(f32[2,4,8,128]{3,2,1,0:T(8,128)S(1)} %maximum_select_fusion.1), channel_id=1, source_target_pairs={{0,449},{64,0},{128,64},{192,128},{256,192},{320,256},{384,320},{4... | collective-permute-start | bytes 98312 | tf_op jit(solution)/shard_map/ppermute | solution.py:430
  34.6 1.9 %collective-permute-start.1 = (f32[2,4,8,128]{3,2,1,0:T(8,128)S(1)}, f32[2,4,8,128]{3,2,1,0:T(8,128)S(1)}, u32[]{:S(2)}, u32[]{:S(2)}) collective-permute-start(f32[2,4,8,128]{3,2,1,0:T(8,128)S(1)} %maximum_select_fusion), channel_id=1, source_target_pairs={{0,64},{64,128},{128,192},{192,256},{256,320},{320,384},{384,448},... | collective-permute-start | bytes 98312 | tf_op jit(solution)/shard_map/ppermute | solution.py:429
  36.5 0.0 collective-permute-done.2
  36.5 5.5 %collective-permute-done.1 = f32[2,4,8,128]{3,2,1,0:T(8,128)S(1)} collective-permute-done((f32[2,4,8,128]{3,2,1,0:T(8,128)S(1)}, f32[2,4,8,128]{3,2,1,0:T(8,128)S(1)}, u32[]{:S(2)}, u32[]{:S(2)}) %collective-permute-start.1) | collective-permute-done | bytes 32800 | tf_op jit(solution)/shard_map/ppermute | solution.py:429
  42.0 3.2 %collective-permute-start.3 = (f32[40,8,128]{2,1,0:T(8,128)S(1)}, f32[40,8,128]{2,1,0:T(8,128)S(1)}, u32[]{:S(2)}, u32[]{:S(2)}) collective-permute-start(f32[40,8,128]{2,1,0:T(8,128)S(1)} %pad_maximum_fusion.1.other_ref), channel_id=1, source_target_pairs={{0,2},{1,7},{2,4},{3,1},{4,6},{5,3},{6,0},{7,5},{8,10},{9,15},{10,... | collective-permute-start | bytes 491528 | tf_op jit(solution)/shard_map/ppermute | solution.py:438
  45.2 4.9 %shard_map.124 = (f32[32,8,128]{2,1,0:T(8,128)S(1)}, f32[2,10,8,128]{3,2,1,0:T(8,128)S(1)}, f32[2,10,8,128]{3,2,1,0:T(8,128)S(1)}) custom-call(s32[2080]{0:T(1024)S(1)} %get-tuple-element.13.list_ref, s32[4]{0:T(128)S(1)} %get-tuple-element.14.count_ref, f32[27,8,128]{2,1,0:T(8,128)S(1)} %copy-done.6, f32[40,8,128]{2,1,0:T(8,128)S(1)} %pad_maximum_fusion.own_ref, ...), custom_call_target="tpu_custom_call" | custom-call | flops 851968000 | bytes 1048576 | tf_op jit(solution)/shard_map/pallas_call | solution.py:359
  50.2 0.0 collective-permute-done.3.far_ref
  50.2 4.0 %collective-permute-start.4 = (f32[3,10,8,128]{3,2,1,0:T(8,128)S(1)}, f32[3,10,8,128]{3,2,1,0:T(8,128)S(1)}, u32[]{:S(2)}, u32[]{:S(2)}) collective-permute-start(f32[3,10,8,128]{3,2,1,0:T(8,128)S(1)} %pad_maximum_fusion.2), channel_id=1, source_target_pairs={{0,8},{8,16},{16,24},{24,32},{32,40},{40,48},{48,56},{56,0},{1,9},... | collective-permute-start | bytes 368648 | tf_op jit(solution)/shard_map/ppermute | solution.py:441
  54.3 0.0 collective-permute-start.5
  54.3 4.8 %shard_map.125.acc2_ref = f32[32,8,128]{2,1,0:T(8,128)S(1)} custom-call(s32[2080]{0:T(1024)S(1)} %get-tuple-element.13.list_ref, s32[4]{0:T(128)S(1)} %get-tuple-element.14.count_ref, f32[27,8,128]{2,1,0:T(8,128)S(1)} %copy-done.6, f32[40,8,128]{2,1,0:T(8,128)S(1)} %pad_maximum_fusion.own_ref, f32[40,8,128]{2,1,0:T(8,128)S(1)} %collective-permute-done.3.far_ref), custom_call_target="tpu_custom_call" | custom-call | flops 851968000 | bytes 1048576 | tf_op jit(solution)/shard_map/pallas_call | solution.py:372
  59.1 0.0 collective-permute-done.4.low_ref
  59.1 0.0 collective-permute-done.5.high_ref
  59.1 5.7 %shard_map.126 = (f32[8,4,3,1,128]{4,3,2,1,0:T(1,128)}, f32[8,4,1,128]{3,2,1,0:T(1,128)S(1)}, f32[1,128]{1,0:T(1,128)S(1)}) custom-call(s32[1]{0:T(128)} %bitcast.half_ref, s32[2080]{0:T(1024)S(1)} %get-tuple-element.13.list_ref, s32[4]{0:T(128)S(1)} %get-tuple-element.14.count_ref, f32[27,8,128]{2,1,0:T(8,128)S(1)} %copy-done.6, ...), custom_call_target="tpu_custom_call" | custom-call | flops 851968000 | bytes 1048576 | tf_op jit(solution)/shard_map/pallas_call | solution.py:386
  64.8 0.0 copy-start.1
  64.8 14.8 %all_to_all.14 = f32[32,1,128]{2,1,0:T(1,128)S(1)} all-to-all(f32[32,1,128]{2,1,0:T(1,128)S(1)} %broadcast_in_dim.24), channel_id=1, replica_groups=mesh['gx'=8,'gy_0'=4,'gy_1'=2,'gz_0'=4,'gz_1'=2] {'gz_0','gy_0','gy_1'}, dimensions={0} | all-to-all | bytes 32768 | tf_op jit(solution)/shard_map/all_to_all | solution.py:450
  79.6 0.0 copy-done.1
  79.6 18.0 %all_to_all.15 = f32[16,1,128]{2,1,0:T(1,128)} all-to-all(f32[16,1,128]{2,1,0:T(1,128)S(1)} %broadcast_in_dim.25), channel_id=1, replica_groups=mesh['gx'=8,'gy_0'=4,'gy_1'=2,'gz_0'=4,'gz_1'=2] {'gx','gz_1'}, dimensions={0} | all-to-all | bytes 16384 | tf_op jit(solution)/shard_map/all_to_all | solution.py:450
  97.6 1.4 %shard_map.127 = f32[8,4,1,128]{3,2,1,0:T(1,128)} custom-call(f32[16,128]{1,0:T(8,128)} %bitcast.36, f32[8,4,1,128]{3,2,1,0:T(1,128)} %copy-done.1), custom_call_target="tpu_custom_call" | custom-call | tf_op jit(solution)/shard_map/pallas_call | solution.py:453
  (13 shorter events, 0.1 us)
Async XLA Ops:
  0.6 18.8 %copy-start.4 = (s32[8,4,1,2,128]{4,3,2,1,0:T(2,128)S(1)}, s32[8,4,1,2,128]{4,3,2,1,0:T(2,128)}, u32[]{:S(2)}) copy-start(s32[8,4,1,2,128]{4,3,2,1,0:T(2,128)} %desc_ref.1) | copy-start | bytes 98308
  0.6 18.8 %copy-start.6 = (f32[27,8,128]{2,1,0:T(8,128)S(1)}, f32[27,8,128]{2,1,0:T(8,128)}, u32[]{:S(2)}) copy-start(f32[27,8,128]{2,1,0:T(8,128)} %constant.15.clone.off_ref) | copy-start | bytes 331780
  2.3 17.2 %copy-start.3 = (f32[8,4,1,3,128]{4,2,3,1,0:T(1,128)S(1)}, f32[8,4,1,3,128]{4,2,3,1,0:T(1,128)}, u32[]{:S(2)}) copy-start(f32[8,4,1,3,128]{4,2,3,1,0:T(1,128)} %param.12) | copy-start | bytes 147460
  2.3 17.2 %copy-start.5 = (s32[8,4,1,14]{3,2,1,0:T(1,128)S(1)}, s32[8,4,1,14]{3,2,1,0:T(1,128)}, u32[]{:S(2)}) copy-start(s32[8,4,1,14]{3,2,1,0:T(1,128)} %nbr_ref.1) | copy-start | bytes 5380
  2.3 26.4 %collective-permute-start = (f32[32,8,128]{2,1,0:T(8,128)}, f32[32,8,128]{2,1,0:T(8,128)S(1)}, u32[]{:S(2)}, u32[]{:S(2)}) collective-permute-start(f32[32,8,128]{2,1,0:T(8,128)} %shard_map.122.own_ref), channel_id=1, source_target_pairs={{0,1},{1,0},{2,3},{3,2},{4,5},{5,4},{6,7},{7,6},{8,9},{9,8},{10,11... | collective-permute-start | bytes 393224 | tf_op jit(solution)/shard_map/ppermute | solution.py:422
  19.4 0.7 copy-start.7
  19.4 0.7 copy-start.2
  20.1 0.9 copy-start
  28.7 7.8 %collective-permute-start.2 = (f32[2,4,8,128]{3,2,1,0:T(8,128)S(1)}, f32[2,4,8,128]{3,2,1,0:T(8,128)S(1)}, u32[]{:S(2)}, u32[]{:S(2)}) collective-permute-start(f32[2,4,8,128]{3,2,1,0:T(8,128)S(1)} %maximum_select_fusion.1), channel_id=1, source_target_pairs={{0,449},{64,0},{128,64},{192,128},{256,192},{320,256},{384,320},{4... | collective-permute-start | bytes 98312 | tf_op jit(solution)/shard_map/ppermute | solution.py:430
  34.6 7.4 %collective-permute-start.1 = (f32[2,4,8,128]{3,2,1,0:T(8,128)S(1)}, f32[2,4,8,128]{3,2,1,0:T(8,128)S(1)}, u32[]{:S(2)}, u32[]{:S(2)}) collective-permute-start(f32[2,4,8,128]{3,2,1,0:T(8,128)S(1)} %maximum_select_fusion), channel_id=1, source_target_pairs={{0,64},{64,128},{128,192},{192,256},{256,320},{320,384},{384,448},... | collective-permute-start | bytes 98312 | tf_op jit(solution)/shard_map/ppermute | solution.py:429
  42.0 8.2 %collective-permute-start.3 = (f32[40,8,128]{2,1,0:T(8,128)S(1)}, f32[40,8,128]{2,1,0:T(8,128)S(1)}, u32[]{:S(2)}, u32[]{:S(2)}) collective-permute-start(f32[40,8,128]{2,1,0:T(8,128)S(1)} %pad_maximum_fusion.1.other_ref), channel_id=1, source_target_pairs={{0,2},{1,7},{2,4},{3,1},{4,6},{5,3},{6,0},{7,5},{8,10},{9,15},{10,... | collective-permute-start | bytes 491528 | tf_op jit(solution)/shard_map/ppermute | solution.py:438
  50.2 8.9 %collective-permute-start.4 = (f32[3,10,8,128]{3,2,1,0:T(8,128)S(1)}, f32[3,10,8,128]{3,2,1,0:T(8,128)S(1)}, u32[]{:S(2)}, u32[]{:S(2)}) collective-permute-start(f32[3,10,8,128]{3,2,1,0:T(8,128)S(1)} %pad_maximum_fusion.2), channel_id=1, source_target_pairs={{0,8},{8,16},{16,24},{24,32},{32,40},{40,48},{48,56},{56,0},{1,9},... | collective-permute-start | bytes 368648 | tf_op jit(solution)/shard_map/ppermute | solution.py:441
  54.3 4.8 %collective-permute-start.5 = (f32[3,10,8,128]{3,2,1,0:T(8,128)S(1)}, f32[3,10,8,128]{3,2,1,0:T(8,128)S(1)}, u32[]{:S(2)}, u32[]{:S(2)}) collective-permute-start(f32[3,10,8,128]{3,2,1,0:T(8,128)S(1)} %pad_maximum_fusion.3), channel_id=1, source_target_pairs={{0,56},{8,0},{16,8},{24,16},{32,24},{40,32},{48,40},{56,48},{1,57}... | collective-permute-start | bytes 368648 | tf_op jit(solution)/shard_map/ppermute | solution.py:442
  64.8 14.8 %copy-start.1 = (f32[8,4,1,128]{3,2,1,0:T(1,128)}, f32[8,4,1,128]{3,2,1,0:T(1,128)S(1)}, u32[]{:S(2)}) copy-start(f32[8,4,1,128]{3,2,1,0:T(1,128)S(1)} %get-tuple-element.23.sq_ref) | copy-start | bytes 49156

commit v5 on v4

--- a/solution.py
+++ b/solution.py
@@ -61,7 +61,7 @@
 
 
 CLASSES = 4
-BATCH = 36
+BATCHES = (40, 38, 47, 44)
 F32, BF16, I32 = jnp.float32, jnp.bfloat16, jnp.int32
 
 
@@ -114,12 +114,13 @@
 
 def run_items(kind, cap, list_ref, count_ref, st_ref, mc_ref, own_of, off_ref, acc_ref):
     sub = sublanes()
+    size = BATCHES[kind]
     count = count_ref[kind]
 
     def batch(b, carry):
         sums = []
-        for t in range(BATCH):
-            place = b * BATCH + t
+        for t in range(size):
+            place = b * size + t
             valid = place < count
             item = jnp.where(valid, list_ref[kind * cap + place], 0)
             src, code, cell = item >> 10, (item >> 5) & 31, item & 31
@@ -143,7 +144,7 @@
             acc_ref[cell] = acc_ref[cell] + add
         return carry
 
-    lax.fori_loop(0, (count + BATCH - 1) // BATCH, batch, 0)
+    lax.fori_loop(0, (count + size - 1) // size, batch, 0)
 
 
 def own_pass(
@@ -326,6 +327,10 @@
     return pltpu.CompilerParams(vmem_limit_bytes=40 << 20)
 
 
+def small_params():
+    return pltpu.CompilerParams(vmem_limit_bytes=4 << 20)
+
+
 def features_of(sources):
     return [pltpu.VMEM((sources, 128, 48), BF16), pltpu.VMEM((sources, 32, 128), BF16)]
 
@@ -334,7 +339,7 @@
     cx, cy = neighbour_lists.shape[:2]
     cells = cx * cy
     items = cells * neighbour_lists.shape[3]
-    cap = items + 2 * BATCH
+    cap = items + max(BATCHES)
     rows = jax.ShapeDtypeStruct((cells, 8, 128), F32)
     return pl.pallas_call(
         functools.partial(own_pass, cap=cap),
@@ -455,6 +460,7 @@
         in_specs=[VMEM, VMEM],
         out_specs=VMEM,
         out_shape=jax.ShapeDtypeStruct((cx, cy, cz, slots), F32),
+        compiler_params=small_params(),
     )(gathered(sums, ZRING), squared)
     return jnp.transpose(drift, (0, 1, 3, 2, 4)), tension
 

time: 99.7 us -> 97.8 us (0.981)
  blocking collectives: 32.8 us -> 31.7 us
    all_to_all x2, blocking collectives: 32.8 us -> 31.7 us  [gathered(): lax.all_to_all(jnp.broadcast_to(row, (count, slots)), axes, 0, 0, tiled=T...]
where the time goes in v5:
time: 97.8 us; the launch traced here: 97.3 us
  blocking collectives  31.7 us (32%)
  starting transfers between devices  31.1 us (32%)
  Pallas kernels  25.6 us (26%)
  waiting for transfers between devices  5.48 us (6%)
  local copies, waits for them, and re-layouts  2.38 us (2%)
    all_to_all x2, blocking collectives, gathered(): lax.all_to_all(jnp.broadcast_to(row, (count, slots)), axes, 0, 0, tiled=T...  31.7 us
    ppermute x1, starting transfers between devices, shards(): other = lax.ppermute(own, 'gz_1', [(0, 1), (1, 0)])  16.4 us
    pallas_call x1, Pallas kernels, first_forces(): pl.pallas_call(functools.partial(own_pass, cap=cap), in_specs=[SMEM] * 4...  7.87 us
    pallas_call x1, Pallas kernels, finish(): pl.pallas_call(functools.partial(last_pass, cap=cap), in_specs=[SMEM] * 3...  5.91 us
    ppermute x1, starting transfers between devices, shards(): above = lax.ppermute(both(0), ZRING, zring_pairs(zs, -1))  5.6 us
    ppermute x1, waiting for transfers between devices, shards(): below = lax.ppermute(both(cx * cy - cy), ZRING, zring_pairs(zs, 1))  5.47 us
    pallas_call x1, Pallas kernels, other_forces(): pl.pallas_call(functools.partial(other_pass, cap=cap), in_specs=[SMEM, SM...  5.08 us
    pallas_call x1, Pallas kernels, far_forces(): pl.pallas_call(functools.partial(far_pass, cap=cap), in_specs=[SMEM, SMEM...  4.46 us
  transfers between devices with their start and end apart: 6, of which 1 were waited for; matrix products, arithmetic and copies ran while one was open for 1% of the time, Pallas kernels for 18%

profile of v5, /device:TPU:1, one launch (start us, length us, event | category | flops | bytes accessed | tf_op | source)
XLA Modules:
  0.0 97.3 jit_solution(17445745854901407590)
XLA Ops:
  0.6 0.0 copy-start.3
  0.6 0.0 copy-start.5
  0.7 1.6 %shard_map.122.own_ref = f32[32,8,128]{2,1,0:T(8,128)} custom-call(s32[4,1,8]{2,1,0:T(1,128)} %bitcast.31, f32[8,4,1,4,128]{4,3,2,1,0:T(4,128)} %now_ref.1, f32[8,4,3,1,128]{4,3,2,1,0:T(1,128)} %bitcast.36), custom_call_target="tpu_custom_call" | custom-call | tf_op jit(solution)/shard_map/pallas_call | solution.py:421
  2.3 0.0 copy-start.2
  2.3 0.0 copy-start.4
  2.3 16.4 %collective-permute-start = (f32[32,8,128]{2,1,0:T(8,128)}, f32[32,8,128]{2,1,0:T(8,128)S(1)}, u32[]{:S(2)}, u32[]{:S(2)}) collective-permute-start(f32[32,8,128]{2,1,0:T(8,128)} %shard_map.122.own_ref), channel_id=1, source_target_pairs={{0,1},{1,0},{2,3},{3,2},{4,5},{5,4},{6,7},{7,6},{8,9},{9,8},{10,11... | collective-permute-start | bytes 393224 | tf_op jit(solution)/shard_map/ppermute | solution.py:427
  18.7 0.8 slice_bitcast_fusion.5
  19.5 0.0 copy-start.6
  19.5 0.0 copy-start.1
  19.5 0.0 copy-done.3
  19.5 0.0 copy-done.5
  19.5 0.0 copy-done.2
  19.5 0.0 copy-done.4
  19.5 0.6 copy-done.6
  20.1 0.0 copy-done.1
  20.1 0.0 copy-start
  20.2 0.9 copy-done
  21.1 7.9 %shard_map.123 = (s32[1980]{0:T(1024)S(1)}, s32[4]{0:T(128)S(1)}, f32[32,8,128]{2,1,0:T(8,128)S(1)}, f32[32,8,128]{2,1,0:T(8,128)S(1)}, s32[32,8,128]{2,1,0:T(8,128)S(1)}) custom-call(s32[1]{0:T(128)} %bitcast.half_ref, s32[486]{0:T(512)S(1)} %copy-done.6, s32[8,4,1,14]{3,2,1,0:T(1,128)S(1)} %copy-done.4, s32[4,1,8]{2,1,0:T(1,128)S(1)} %bitcast.32, ...), custom_call_target="tpu_custom_call" | custom-call | flops 734003200 | bytes 1048576 | tf_op jit(solution)/shard_map/pallas_call | solution.py:344
  28.9 0.0 collective-permute-done
  29.0 5.6 %collective-permute-start.2 = (f32[2,4,8,128]{3,2,1,0:T(8,128)S(1)}, f32[2,4,8,128]{3,2,1,0:T(8,128)S(1)}, u32[]{:S(2)}, u32[]{:S(2)}) collective-permute-start(f32[2,4,8,128]{3,2,1,0:T(8,128)S(1)} %maximum_select_fusion.1), channel_id=1, source_target_pairs={{0,449},{64,0},{128,64},{192,128},{256,192},{320,256},{384,320},{4... | collective-permute-start | bytes 98312 | tf_op jit(solution)/shard_map/ppermute | solution.py:435
  34.6 1.9 %collective-permute-start.1 = (f32[2,4,8,128]{3,2,1,0:T(8,128)S(1)}, f32[2,4,8,128]{3,2,1,0:T(8,128)S(1)}, u32[]{:S(2)}, u32[]{:S(2)}) collective-permute-start(f32[2,4,8,128]{3,2,1,0:T(8,128)S(1)} %maximum_select_fusion), channel_id=1, source_target_pairs={{0,64},{64,128},{128,192},{192,256},{256,320},{320,384},{384,448},... | collective-permute-start | bytes 98312 | tf_op jit(solution)/shard_map/ppermute | solution.py:434
  36.5 0.0 collective-permute-done.2
  36.5 5.5 %collective-permute-done.1 = f32[2,4,8,128]{3,2,1,0:T(8,128)S(1)} collective-permute-done((f32[2,4,8,128]{3,2,1,0:T(8,128)S(1)}, f32[2,4,8,128]{3,2,1,0:T(8,128)S(1)}, u32[]{:S(2)}, u32[]{:S(2)}) %collective-permute-start.1) | collective-permute-done | bytes 32800 | tf_op jit(solution)/shard_map/ppermute | solution.py:434
  42.0 3.2 %collective-permute-start.3 = (f32[40,8,128]{2,1,0:T(8,128)S(1)}, f32[40,8,128]{2,1,0:T(8,128)S(1)}, u32[]{:S(2)}, u32[]{:S(2)}) collective-permute-start(f32[40,8,128]{2,1,0:T(8,128)S(1)} %pad_maximum_fusion.1.other_ref), channel_id=1, source_target_pairs={{0,2},{1,7},{2,4},{3,1},{4,6},{5,3},{6,0},{7,5},{8,10},{9,15},{10,... | collective-permute-start | bytes 491528 | tf_op jit(solution)/shard_map/ppermute | solution.py:443
  45.2 5.1 %shard_map.124 = (f32[32,8,128]{2,1,0:T(8,128)S(1)}, f32[2,10,8,128]{3,2,1,0:T(8,128)S(1)}, f32[2,10,8,128]{3,2,1,0:T(8,128)S(1)}) custom-call(s32[1980]{0:T(1024)S(1)} %get-tuple-element.13.list_ref, s32[4]{0:T(128)S(1)} %get-tuple-element.14.count_ref, f32[27,8,128]{2,1,0:T(8,128)S(1)} %copy-done.5, f32[40,8,128]{2,1,0:T(8,128)S(1)} %pad_maximum_fusion.own_ref, ...), custom_call_target="tpu_custom_call" | custom-call | flops 806092800 | bytes 1048576 | tf_op jit(solution)/shard_map/pallas_call | solution.py:364
  50.3 0.0 collective-permute-done.3.far_ref
  50.4 4.0 %collective-permute-start.4 = (f32[3,10,8,128]{3,2,1,0:T(8,128)S(1)}, f32[3,10,8,128]{3,2,1,0:T(8,128)S(1)}, u32[]{:S(2)}, u32[]{:S(2)}) collective-permute-start(f32[3,10,8,128]{3,2,1,0:T(8,128)S(1)} %pad_maximum_fusion.2), channel_id=1, source_target_pairs={{0,8},{8,16},{16,24},{24,32},{32,40},{40,48},{48,56},{56,0},{1,9},... | collective-permute-start | bytes 368648 | tf_op jit(solution)/shard_map/ppermute | solution.py:446
  54.4 0.0 collective-permute-start.5
  54.4 4.5 %shard_map.125.acc2_ref = f32[32,8,128]{2,1,0:T(8,128)S(1)} custom-call(s32[1980]{0:T(1024)S(1)} %get-tuple-element.13.list_ref, s32[4]{0:T(128)S(1)} %get-tuple-element.14.count_ref, f32[27,8,128]{2,1,0:T(8,128)S(1)} %copy-done.5, f32[40,8,128]{2,1,0:T(8,128)S(1)} %pad_maximum_fusion.own_ref, f32[40,8,128]{2,1,0:T(8,128)S(1)} %collective-permute-done.3.far_ref), custom_call_target="tpu_custom_call" | custom-call | flops 806092800 | bytes 1048576 | tf_op jit(solution)/shard_map/pallas_call | solution.py:377
  58.9 0.0 collective-permute-done.4.low_ref
  58.9 0.0 collective-permute-done.5.high_ref
  58.9 5.9 %shard_map.126 = (f32[8,4,3,1,128]{4,3,2,1,0:T(1,128)}, f32[8,4,1,128]{3,2,1,0:T(1,128)S(1)}, f32[1,128]{1,0:T(1,128)S(1)}) custom-call(s32[1]{0:T(128)} %bitcast.half_ref, s32[1980]{0:T(1024)S(1)} %get-tuple-element.13.list_ref, s32[4]{0:T(128)S(1)} %get-tuple-element.14.count_ref, f32[27,8,128]{2,1,0:T(8,128)S(1)} %copy-done.5, ...), custom_call_target="tpu_custom_call" | custom-call | flops 806092800 | bytes 1048576 | tf_op jit(solution)/shard_map/pallas_call | solution.py:391
  64.8 14.1 %all_to_all.14 = f32[32,1,128]{2,1,0:T(1,128)S(1)} all-to-all(f32[32,1,128]{2,1,0:T(1,128)S(1)} %broadcast_in_dim.24), channel_id=1, replica_groups=mesh['gx'=8,'gy_0'=4,'gy_1'=2,'gz_0'=4,'gz_1'=2] {'gz_0','gy_0','gy_1'}, dimensions={0} | all-to-all | bytes 32768 | tf_op jit(solution)/shard_map/all_to_all | solution.py:455
  79.0 17.6 %all_to_all.15 = f32[16,1,128]{2,1,0:T(1,128)S(1)} all-to-all(f32[16,1,128]{2,1,0:T(1,128)S(1)} %broadcast_in_dim.25), channel_id=1, replica_groups=mesh['gx'=8,'gy_0'=4,'gy_1'=2,'gz_0'=4,'gz_1'=2] {'gx','gz_1'}, dimensions={0} | all-to-all | bytes 16384 | tf_op jit(solution)/shard_map/all_to_all | solution.py:455
  96.6 0.7 shard_map.127
  (13 shorter events, 0.1 us)
Async XLA Ops:
  0.6 18.8 %copy-start.3 = (s32[8,4,1,2,128]{4,3,2,1,0:T(2,128)S(1)}, s32[8,4,1,2,128]{4,3,2,1,0:T(2,128)}, u32[]{:S(2)}) copy-start(s32[8,4,1,2,128]{4,3,2,1,0:T(2,128)} %desc_ref.1) | copy-start | bytes 98308
  0.6 18.8 %copy-start.5 = (f32[27,8,128]{2,1,0:T(8,128)S(1)}, f32[27,8,128]{2,1,0:T(8,128)}, u32[]{:S(2)}) copy-start(f32[27,8,128]{2,1,0:T(8,128)} %constant.15.clone.off_ref) | copy-start | bytes 331780
  2.3 17.2 %copy-start.2 = (f32[8,4,1,3,128]{4,2,3,1,0:T(1,128)S(1)}, f32[8,4,1,3,128]{4,2,3,1,0:T(1,128)}, u32[]{:S(2)}) copy-start(f32[8,4,1,3,128]{4,2,3,1,0:T(1,128)} %param.12) | copy-start | bytes 147460
  2.3 17.2 %copy-start.4 = (s32[8,4,1,14]{3,2,1,0:T(1,128)S(1)}, s32[8,4,1,14]{3,2,1,0:T(1,128)}, u32[]{:S(2)}) copy-start(s32[8,4,1,14]{3,2,1,0:T(1,128)} %nbr_ref.1) | copy-start | bytes 5380
  2.3 26.7 %collective-permute-start = (f32[32,8,128]{2,1,0:T(8,128)}, f32[32,8,128]{2,1,0:T(8,128)S(1)}, u32[]{:S(2)}, u32[]{:S(2)}) collective-permute-start(f32[32,8,128]{2,1,0:T(8,128)} %shard_map.122.own_ref), channel_id=1, source_target_pairs={{0,1},{1,0},{2,3},{3,2},{4,5},{5,4},{6,7},{7,6},{8,9},{9,8},{10,11... | collective-permute-start | bytes 393224 | tf_op jit(solution)/shard_map/ppermute | solution.py:427
  19.5 0.7 copy-start.6
  19.5 0.7 copy-start.1
  20.1 0.9 copy-start
  29.0 7.5 %collective-permute-start.2 = (f32[2,4,8,128]{3,2,1,0:T(8,128)S(1)}, f32[2,4,8,128]{3,2,1,0:T(8,128)S(1)}, u32[]{:S(2)}, u32[]{:S(2)}) collective-permute-start(f32[2,4,8,128]{3,2,1,0:T(8,128)S(1)} %maximum_select_fusion.1), channel_id=1, source_target_pairs={{0,449},{64,0},{128,64},{192,128},{256,192},{320,256},{384,320},{4... | collective-permute-start | bytes 98312 | tf_op jit(solution)/shard_map/ppermute | solution.py:435
  34.6 7.4 %collective-permute-start.1 = (f32[2,4,8,128]{3,2,1,0:T(8,128)S(1)}, f32[2,4,8,128]{3,2,1,0:T(8,128)S(1)}, u32[]{:S(2)}, u32[]{:S(2)}) collective-permute-start(f32[2,4,8,128]{3,2,1,0:T(8,128)S(1)} %maximum_select_fusion), channel_id=1, source_target_pairs={{0,64},{64,128},{128,192},{192,256},{256,320},{320,384},{384,448},... | collective-permute-start | bytes 98312 | tf_op jit(solution)/shard_map/ppermute | solution.py:434
  42.0 8.3 %collective-permute-start.3 = (f32[40,8,128]{2,1,0:T(8,128)S(1)}, f32[40,8,128]{2,1,0:T(8,128)S(1)}, u32[]{:S(2)}, u32[]{:S(2)}) collective-permute-start(f32[40,8,128]{2,1,0:T(8,128)S(1)} %pad_maximum_fusion.1.other_ref), channel_id=1, source_target_pairs={{0,2},{1,7},{2,4},{3,1},{4,6},{5,3},{6,0},{7,5},{8,10},{9,15},{10,... | collective-permute-start | bytes 491528 | tf_op jit(solution)/shard_map/ppermute | solution.py:443
  50.4 8.5 %collective-permute-start.4 = (f32[3,10,8,128]{3,2,1,0:T(8,128)S(1)}, f32[3,10,8,128]{3,2,1,0:T(8,128)S(1)}, u32[]{:S(2)}, u32[]{:S(2)}) collective-permute-start(f32[3,10,8,128]{3,2,1,0:T(8,128)S(1)} %pad_maximum_fusion.2), channel_id=1, source_target_pairs={{0,8},{8,16},{16,24},{24,32},{32,40},{40,48},{48,56},{56,0},{1,9},... | collective-permute-start | bytes 368648 | tf_op jit(solution)/shard_map/ppermute | solution.py:446
  54.4 4.5 %collective-permute-start.5 = (f32[3,10,8,128]{3,2,1,0:T(8,128)S(1)}, f32[3,10,8,128]{3,2,1,0:T(8,128)S(1)}, u32[]{:S(2)}, u32[]{:S(2)}) collective-permute-start(f32[3,10,8,128]{3,2,1,0:T(8,128)S(1)} %pad_maximum_fusion.3), channel_id=1, source_target_pairs={{0,56},{8,0},{16,8},{24,16},{32,24},{40,32},{48,40},{56,48},{1,57}... | collective-permute-start | bytes 368648 | tf_op jit(solution)/shard_map/ppermute | solution.py:447

commit v6 on v5

--- a/solution.py
+++ b/solution.py
@@ -61,7 +61,7 @@
 
 
 CLASSES = 4
-BATCHES = (40, 38, 47, 44)
+BATCHES = (40, 75, 70, 88)
 F32, BF16, I32 = jnp.float32, jnp.bfloat16, jnp.int32
 
 
@@ -229,9 +229,9 @@
     half_ref, list_ref, count_ref, off_ref, own_ref, other_ref, far_ref, low_ref, high_ref,
     acc0_ref, acc1_ref, acc2_ref, base_ref, link_ref,
     drift_ref, sq_ref, part_ref,
-    acc_ref, st_ref, mc_ref, cube_ref, out_ref, sems, *, cap
+    acc_ref, st_ref, mc_ref, cube_ref, *, cap
 ):
-    cx, cy = out_ref.shape[:2]
+    cx, cy = drift_ref.shape[:2]
     px = cx + 2
     half = half_ref[0]
     lane = lax.broadcasted_iota(I32, (1, 128), 1)
@@ -278,7 +278,7 @@
             found = jnp.where(dcode == code, got, found)
         error = base_ref[cell, :3] + found[4:7] - HALF_KICK * acc_ref[cell, :3]
         alive = base_ref[cell, 3:4]
-        out_ref[x, y, :, 0] = jnp.where(alive > 0.0, error, 0.0)
+        drift_ref[x, y, :, 0] = jnp.where(alive > 0.0, error, 0.0)
         squared = jnp.where(alive > 0.0, jnp.sum(error * error, axis=0, keepdims=True), 0.0)
         sq_ref[x, y] = squared
         return squared, alive
@@ -289,21 +289,20 @@
             squared, alive = one_cell(x, y)
             total = total + squared
             live = live + alive
-        pltpu.make_async_copy(out_ref.at[x], drift_ref.at[x], sems.at[x]).start()
         return total, live
 
     zero = jnp.zeros((1, 128), F32)
-    total, live = lax.fori_loop(0, cx, one_row, (zero, zero))
+    total, live = lax.fori_loop(0, cx, one_row, (zero, zero), unroll=4)
 
     def folded(v):
         return v + pltpu.roll(jnp.broadcast_to(v, (8, 128)), 64, 1)[:1]
 
     part_ref[...] = jnp.where(lane < 64, folded(total), folded(live))
-    for x in range(cx):
-        pltpu.make_async_copy(out_ref.at[x], drift_ref.at[x], sems.at[x]).wait()
-
-
-def scaled(rows_ref, sq_ref, tension_ref):
+
+
+def scaled(rows_ref, sq_ref, drift_ref, tension_ref, out_ref, sem):
+    copy = pltpu.make_async_copy(drift_ref, out_ref, sem)
+    copy.start()
     lane = lax.broadcasted_iota(I32, (1, 128), 1)
     sums = jnp.sum(rows_ref[...], axis=0, keepdims=True)
     total = jnp.sum(jnp.where(lane < 64, sums, 0.0), axis=1, keepdims=True)
@@ -312,6 +311,7 @@
     for x in range(sq_ref.shape[0]):
         for y in range(sq_ref.shape[1]):
             tension_ref[x, y] = sq_ref[x, y] / bound
+    copy.wait()
 
 
 SMEM = pl.BlockSpec(memory_space=pltpu.SMEM)
@@ -391,7 +391,7 @@
     return pl.pallas_call(
         functools.partial(last_pass, cap=cap),
         in_specs=[SMEM] * 3 + [VMEM] * 11,
-        out_specs=[pl.BlockSpec(memory_space=pl.ANY), VMEM, VMEM],
+        out_specs=[VMEM, VMEM, VMEM],
         out_shape=[
             jax.ShapeDtypeStruct((cx, cy, 3, 1, 128), F32),
             jax.ShapeDtypeStruct((cx, cy, 1, 128), F32),
@@ -399,11 +399,7 @@
         ],
         scratch_shapes=[pltpu.VMEM((cx * cy, 8, 128), F32)]
         + features_of(6 * px)
-        + [
-            pltpu.VMEM((3, px, cy + 2, 8, 128), F32),
-            pltpu.VMEM((cx, cy, 3, 1, 128), F32),
-            pltpu.SemaphoreType.DMA((cx,)),
-        ],
+        + [pltpu.VMEM((3, px, cy + 2, 8, 128), F32)],
         cost_estimate=cost(cap // 4),
         compiler_params=params(),
     )(half, lists, counts, offset_table(), *planes, low, high, *sums, base, links)
@@ -455,13 +451,17 @@
         return lax.all_to_all(jnp.broadcast_to(row, (count, slots)), axes, 0, 0, tiled=True)
 
     sums = jnp.sum(gathered(part, XYC), axis=0, keepdims=True)
-    tension = pl.pallas_call(
+    tension, drift = pl.pallas_call(
         scaled,
-        in_specs=[VMEM, VMEM],
-        out_specs=VMEM,
-        out_shape=jax.ShapeDtypeStruct((cx, cy, cz, slots), F32),
+        in_specs=[VMEM, VMEM, VMEM],
+        out_specs=[VMEM, pl.BlockSpec(memory_space=pl.ANY)],
+        out_shape=[
+            jax.ShapeDtypeStruct((cx, cy, cz, slots), F32),
+            jax.ShapeDtypeStruct(drift.shape, F32),
+        ],
+        scratch_shapes=[pltpu.SemaphoreType.DMA],
         compiler_params=small_params(),
-    )(gathered(sums, ZRING), squared)
+    )(gathered(sums, ZRING), squared, drift)
     return jnp.transpose(drift, (0, 1, 3, 2, 4)), tension
 
 

time: 97.8 us -> 96.6 us (0.988)
  Pallas kernels: 25.6 us -> 23.9 us
    pallas_call x1, Pallas kernels: 5.91 us -> 4.53 us  [finish(): pl.pallas_call(functools.partial(last_pass, cap=cap), in_specs=[SMEM] * 3...]
  transfers between devices with their start and end apart: 6 -> 6, of which waited for: 1 -> 2; matrix products, arithmetic and copies ran while one was open for 1% -> 1% of each run, Pallas kernels for 18% -> 17%
where the time goes in v6:
time: 96.6 us; the launch traced here: 96.1 us
  blocking collectives  31.7 us (33%)
  starting transfers between devices  31.6 us (33%)
  Pallas kernels  23.9 us (25%)
  waiting for transfers between devices  5.59 us (6%)
  local copies, waits for them, and re-layouts  2.39 us (2%)
    all_to_all x2, blocking collectives, gathered(): lax.all_to_all(jnp.broadcast_to(row, (count, slots)), axes, 0, 0, tiled=T...  31.7 us
    ppermute x1, starting transfers between devices, shards(): other = lax.ppermute(own, 'gz_1', [(0, 1), (1, 0)])  16.4 us
    pallas_call x1, Pallas kernels, first_forces(): pl.pallas_call(functools.partial(own_pass, cap=cap), in_specs=[SMEM] * 4...  7.88 us
    ppermute x1, starting transfers between devices, shards(): above = lax.ppermute(both(0), ZRING, zring_pairs(zs, -1))  5.59 us
    ppermute x1, waiting for transfers between devices, shards(): below = lax.ppermute(both(cx * cy - cy), ZRING, zring_pairs(zs, 1))  5.47 us
    pallas_call x1, Pallas kernels, finish(): pl.pallas_call(functools.partial(last_pass, cap=cap), in_specs=[SMEM] * 3...  4.53 us
    ppermute x1, starting transfers between devices, shards(): lax.ppermute(jnp.concatenate([top, rows[None, :, 8 * cy - 8:]]), GY, ring...  4.5 us
    pallas_call x1, Pallas kernels, other_forces(): pl.pallas_call(functools.partial(other_pass, cap=cap), in_specs=[SMEM, SM...  4.49 us
  transfers between devices with their start and end apart: 6, of which 2 were waited for; matrix products, arithmetic and copies ran while one was open for 1% of the time, Pallas kernels for 17%

profile of v6, /device:TPU:1, one launch (start us, length us, event | category | flops | bytes accessed | tf_op | source)
XLA Modules:
  0.0 96.1 jit_solution(5360450358777782653)
XLA Ops:
  0.6 0.0 copy-start.3
  0.6 0.0 copy-start.5
  0.7 1.6 %shard_map.122.own_ref = f32[32,8,128]{2,1,0:T(8,128)} custom-call(s32[4,1,8]{2,1,0:T(1,128)} %bitcast.31, f32[8,4,1,4,128]{4,3,2,1,0:T(4,128)} %now_ref.1, f32[8,4,3,1,128]{4,3,2,1,0:T(1,128)} %bitcast.36), custom_call_target="tpu_custom_call" | custom-call | tf_op jit(solution)/shard_map/pallas_call | solution.py:417
  2.3 0.0 copy-start.2
  2.3 0.0 copy-start.4
  2.3 16.4 %collective-permute-start = (f32[32,8,128]{2,1,0:T(8,128)}, f32[32,8,128]{2,1,0:T(8,128)S(1)}, u32[]{:S(2)}, u32[]{:S(2)}) collective-permute-start(f32[32,8,128]{2,1,0:T(8,128)} %shard_map.122.own_ref), channel_id=1, source_target_pairs={{0,1},{1,0},{2,3},{3,2},{4,5},{5,4},{6,7},{7,6},{8,9},{9,8},{10,11... | collective-permute-start | bytes 393224 | tf_op jit(solution)/shard_map/ppermute | solution.py:423
  18.7 0.8 slice_bitcast_fusion.5
  19.4 0.0 copy-start.6
  19.4 0.0 copy-start.1
  19.4 0.0 copy-done.3
  19.4 0.0 copy-done.5
  19.5 0.0 copy-done.2
  19.5 0.0 copy-done.4
  19.5 0.6 copy-done.6
  20.1 0.0 copy-done.1
  20.1 0.0 copy-start
  20.1 0.9 copy-done
  21.0 7.9 %shard_map.123 = (s32[2144]{0:T(1024)S(1)}, s32[4]{0:T(128)S(1)}, f32[32,8,128]{2,1,0:T(8,128)S(1)}, f32[32,8,128]{2,1,0:T(8,128)S(1)}, s32[32,8,128]{2,1,0:T(8,128)S(1)}) custom-call(s32[1]{0:T(128)} %bitcast.half_ref, s32[486]{0:T(512)S(1)} %copy-done.6, s32[8,4,1,14]{3,2,1,0:T(1,128)S(1)} %copy-done.4, s32[4,1,8]{2,1,0:T(1,128)S(1)} %bitcast.32, ...), custom_call_target="tpu_custom_call" | custom-call | flops 734003200 | bytes 1048576 | tf_op jit(solution)/shard_map/pallas_call | solution.py:344
  28.9 0.0 collective-permute-done
  29.0 5.6 %collective-permute-start.2 = (f32[2,4,8,128]{3,2,1,0:T(8,128)S(1)}, f32[2,4,8,128]{3,2,1,0:T(8,128)S(1)}, u32[]{:S(2)}, u32[]{:S(2)}) collective-permute-start(f32[2,4,8,128]{3,2,1,0:T(8,128)S(1)} %maximum_select_fusion.1), channel_id=1, source_target_pairs={{0,449},{64,0},{128,64},{192,128},{256,192},{320,256},{384,320},{4... | collective-permute-start | bytes 98312 | tf_op jit(solution)/shard_map/ppermute | solution.py:431
  34.6 1.9 %collective-permute-start.1 = (f32[2,4,8,128]{3,2,1,0:T(8,128)S(1)}, f32[2,4,8,128]{3,2,1,0:T(8,128)S(1)}, u32[]{:S(2)}, u32[]{:S(2)}) collective-permute-start(f32[2,4,8,128]{3,2,1,0:T(8,128)S(1)} %maximum_select_fusion), channel_id=1, source_target_pairs={{0,64},{64,128},{128,192},{192,256},{256,320},{320,384},{384,448},... | collective-permute-start | bytes 98312 | tf_op jit(solution)/shard_map/ppermute | solution.py:430
  36.5 0.0 collective-permute-done.2
  36.5 5.5 %collective-permute-done.1 = f32[2,4,8,128]{3,2,1,0:T(8,128)S(1)} collective-permute-done((f32[2,4,8,128]{3,2,1,0:T(8,128)S(1)}, f32[2,4,8,128]{3,2,1,0:T(8,128)S(1)}, u32[]{:S(2)}, u32[]{:S(2)}) %collective-permute-start.1) | collective-permute-done | bytes 32800 | tf_op jit(solution)/shard_map/ppermute | solution.py:430
  42.0 3.2 %collective-permute-start.3 = (f32[40,8,128]{2,1,0:T(8,128)S(1)}, f32[40,8,128]{2,1,0:T(8,128)S(1)}, u32[]{:S(2)}, u32[]{:S(2)}) collective-permute-start(f32[40,8,128]{2,1,0:T(8,128)S(1)} %pad_maximum_fusion.1.other_ref), channel_id=1, source_target_pairs={{0,2},{1,7},{2,4},{3,1},{4,6},{5,3},{6,0},{7,5},{8,10},{9,15},{10,... | collective-permute-start | bytes 491528 | tf_op jit(solution)/shard_map/ppermute | solution.py:439
  45.2 4.5 %shard_map.124 = (f32[32,8,128]{2,1,0:T(8,128)S(1)}, f32[2,10,8,128]{3,2,1,0:T(8,128)S(1)}, f32[2,10,8,128]{3,2,1,0:T(8,128)S(1)}) custom-call(s32[2144]{0:T(1024)S(1)} %get-tuple-element.15.list_ref, s32[4]{0:T(128)S(1)} %get-tuple-element.16.count_ref, f32[27,8,128]{2,1,0:T(8,128)S(1)} %copy-done.5, f32[40,8,128]{2,1,0:T(8,128)S(1)} %pad_maximum_fusion.own_ref, ...), custom_call_target="tpu_custom_call" | custom-call | flops 878182400 | bytes 1048576 | tf_op jit(solution)/shard_map/pallas_call | solution.py:364
  49.7 0.0 collective-permute-done.3.far_ref
  49.8 4.5 %collective-permute-start.4 = (f32[3,10,8,128]{3,2,1,0:T(8,128)S(1)}, f32[3,10,8,128]{3,2,1,0:T(8,128)S(1)}, u32[]{:S(2)}, u32[]{:S(2)}) collective-permute-start(f32[3,10,8,128]{3,2,1,0:T(8,128)S(1)} %pad_maximum_fusion.2), channel_id=1, source_target_pairs={{0,8},{8,16},{16,24},{24,32},{32,40},{40,48},{48,56},{56,0},{1,9},... | collective-permute-start | bytes 368648 | tf_op jit(solution)/shard_map/ppermute | solution.py:442
  54.3 0.0 collective-permute-start.5
  54.3 4.2 %shard_map.125.acc2_ref = f32[32,8,128]{2,1,0:T(8,128)S(1)} custom-call(s32[2144]{0:T(1024)S(1)} %get-tuple-element.15.list_ref, s32[4]{0:T(128)S(1)} %get-tuple-element.16.count_ref, f32[27,8,128]{2,1,0:T(8,128)S(1)} %copy-done.5, f32[40,8,128]{2,1,0:T(8,128)S(1)} %pad_maximum_fusion.own_ref, f32[40,8,128]{2,1,0:T(8,128)S(1)} %collective-permute-done.3.far_ref), custom_call_target="tpu_custom_call" | custom-call | flops 878182400 | bytes 1048576 | tf_op jit(solution)/shard_map/pallas_call | solution.py:377
  58.5 0.0 collective-permute-done.4.low_ref
  58.5 0.1 collective-permute-done.5.high_ref
  58.6 4.5 %shard_map.126 = (f32[8,4,3,1,128]{4,3,2,1,0:T(1,128)S(1)}, f32[8,4,1,128]{3,2,1,0:T(1,128)S(1)}, f32[1,128]{1,0:T(1,128)S(1)}) custom-call(s32[1]{0:T(128)} %bitcast.half_ref, s32[2144]{0:T(1024)S(1)} %get-tuple-element.15.list_ref, s32[4]{0:T(128)S(1)} %get-tuple-element.16.count_ref, f32[27,8,128]{2,1,0:T(8,128)S(1)} %copy-done.5, ...), custom_call_target="tpu_custom_call" | custom-call | flops 878182400 | bytes 1048576 | tf_op jit(solution)/shard_map/pallas_call | solution.py:391
  63.1 13.5 %all_to_all.14 = f32[32,1,128]{2,1,0:T(1,128)S(1)} all-to-all(f32[32,1,128]{2,1,0:T(1,128)S(1)} %broadcast_in_dim.24), channel_id=1, replica_groups=mesh['gx'=8,'gy_0'=4,'gy_1'=2,'gz_0'=4,'gz_1'=2] {'gz_0','gy_0','gy_1'}, dimensions={0} | all-to-all | bytes 32768 | tf_op jit(solution)/shard_map/all_to_all | solution.py:451
  76.7 18.2 %all_to_all.15 = f32[16,1,128]{2,1,0:T(1,128)S(1)} all-to-all(f32[16,1,128]{2,1,0:T(1,128)S(1)} %broadcast_in_dim.25), channel_id=1, replica_groups=mesh['gx'=8,'gy_0'=4,'gy_1'=2,'gz_0'=4,'gz_1'=2] {'gx','gz_1'}, dimensions={0} | all-to-all | bytes 16384 | tf_op jit(solution)/shard_map/all_to_all | solution.py:451
  94.9 1.2 %shard_map.127 = (f32[8,4,1,128]{3,2,1,0:T(1,128)}, f32[8,4,3,1,128]{4,3,2,1,0:T(1,128)}) custom-call(f32[16,128]{1,0:T(8,128)S(1)} %bitcast.30, f32[8,4,1,128]{3,2,1,0:T(1,128)S(1)} %get-tuple-element.24.sq_ref, f32[8,4,3,1,128]{4,3,2,1,0:T(1,128)S(1)} %get-tuple-element.25.drift_ref), custom_call_target="tpu_custom_call" | custom-call | tf_op jit(solution)/shard_map/pallas_call | solution.py:454
  (13 shorter events, 0.1 us)
Async XLA Ops:
  0.6 18.8 %copy-start.3 = (s32[8,4,1,2,128]{4,3,2,1,0:T(2,128)S(1)}, s32[8,4,1,2,128]{4,3,2,1,0:T(2,128)}, u32[]{:S(2)}) copy-start(s32[8,4,1,2,128]{4,3,2,1,0:T(2,128)} %desc_ref.1) | copy-start | bytes 98308
  0.6 18.8 %copy-start.5 = (f32[27,8,128]{2,1,0:T(8,128)S(1)}, f32[27,8,128]{2,1,0:T(8,128)}, u32[]{:S(2)}) copy-start(f32[27,8,128]{2,1,0:T(8,128)} %constant.15.clone.off_ref) | copy-start | bytes 331780
  2.3 17.2 %copy-start.2 = (f32[8,4,1,3,128]{4,2,3,1,0:T(1,128)S(1)}, f32[8,4,1,3,128]{4,2,3,1,0:T(1,128)}, u32[]{:S(2)}) copy-start(f32[8,4,1,3,128]{4,2,3,1,0:T(1,128)} %param.12) | copy-start | bytes 147460
  2.3 17.2 %copy-start.4 = (s32[8,4,1,14]{3,2,1,0:T(1,128)S(1)}, s32[8,4,1,14]{3,2,1,0:T(1,128)}, u32[]{:S(2)}) copy-start(s32[8,4,1,14]{3,2,1,0:T(1,128)} %nbr_ref.1) | copy-start | bytes 5380
  2.3 26.7 %collective-permute-start = (f32[32,8,128]{2,1,0:T(8,128)}, f32[32,8,128]{2,1,0:T(8,128)S(1)}, u32[]{:S(2)}, u32[]{:S(2)}) collective-permute-start(f32[32,8,128]{2,1,0:T(8,128)} %shard_map.122.own_ref), channel_id=1, source_target_pairs={{0,1},{1,0},{2,3},{3,2},{4,5},{5,4},{6,7},{7,6},{8,9},{9,8},{10,11... | collective-permute-start | bytes 393224 | tf_op jit(solution)/shard_map/ppermute | solution.py:423
  19.4 0.7 copy-start.6
  19.4 0.7 copy-start.1
  20.1 0.9 copy-start
  29.0 7.5 %collective-permute-start.2 = (f32[2,4,8,128]{3,2,1,0:T(8,128)S(1)}, f32[2,4,8,128]{3,2,1,0:T(8,128)S(1)}, u32[]{:S(2)}, u32[]{:S(2)}) collective-permute-start(f32[2,4,8,128]{3,2,1,0:T(8,128)S(1)} %maximum_select_fusion.1), channel_id=1, source_target_pairs={{0,449},{64,0},{128,64},{192,128},{256,192},{320,256},{384,320},{4... | collective-permute-start | bytes 98312 | tf_op jit(solution)/shard_map/ppermute | solution.py:431
  34.6 7.4 %collective-permute-start.1 = (f32[2,4,8,128]{3,2,1,0:T(8,128)S(1)}, f32[2,4,8,128]{3,2,1,0:T(8,128)S(1)}, u32[]{:S(2)}, u32[]{:S(2)}) collective-permute-start(f32[2,4,8,128]{3,2,1,0:T(8,128)S(1)} %maximum_select_fusion), channel_id=1, source_target_pairs={{0,64},{64,128},{128,192},{192,256},{256,320},{320,384},{384,448},... | collective-permute-start | bytes 98312 | tf_op jit(solution)/shard_map/ppermute | solution.py:430
  42.0 7.7 %collective-permute-start.3 = (f32[40,8,128]{2,1,0:T(8,128)S(1)}, f32[40,8,128]{2,1,0:T(8,128)S(1)}, u32[]{:S(2)}, u32[]{:S(2)}) collective-permute-start(f32[40,8,128]{2,1,0:T(8,128)S(1)} %pad_maximum_fusion.1.other_ref), channel_id=1, source_target_pairs={{0,2},{1,7},{2,4},{3,1},{4,6},{5,3},{6,0},{7,5},{8,10},{9,15},{10,... | collective-permute-start | bytes 491528 | tf_op jit(solution)/shard_map/ppermute | solution.py:439
  49.8 8.7 %collective-permute-start.4 = (f32[3,10,8,128]{3,2,1,0:T(8,128)S(1)}, f32[3,10,8,128]{3,2,1,0:T(8,128)S(1)}, u32[]{:S(2)}, u32[]{:S(2)}) collective-permute-start(f32[3,10,8,128]{3,2,1,0:T(8,128)S(1)} %pad_maximum_fusion.2), channel_id=1, source_target_pairs={{0,8},{8,16},{16,24},{24,32},{32,40},{40,48},{48,56},{56,0},{1,9},... | collective-permute-start | bytes 368648 | tf_op jit(solution)/shard_map/ppermute | solution.py:442
  54.3 4.3 %collective-permute-start.5 = (f32[3,10,8,128]{3,2,1,0:T(8,128)S(1)}, f32[3,10,8,128]{3,2,1,0:T(8,128)S(1)}, u32[]{:S(2)}, u32[]{:S(2)}) collective-permute-start(f32[3,10,8,128]{3,2,1,0:T(8,128)S(1)} %pad_maximum_fusion.3), channel_id=1, source_target_pairs={{0,56},{8,0},{16,8},{24,16},{32,24},{40,32},{48,40},{56,48},{1,57}... | collective-permute-start | bytes 368648 | tf_op jit(solution)/shard_map/ppermute | solution.py:443

commit v7 on v6

--- a/solution.py
+++ b/solution.py
@@ -48,7 +48,19 @@
     return high, mid, rest - mid
 
 
-def assemble(cnt_ref, now_ref, next_ref, own_ref):
+def carried(cx, cy):
+    assert 7 * cy <= cx * cy - cy
+    return cx // 2 * cy - cy
+
+
+def unpacked(sent, cx, cy):
+    first = carried(cx, cy)
+    rows = sent[: 7 * cy, 7].reshape(cy, 7, sent.shape[2])
+    cells = jnp.pad(rows, ((0, 0), (0, 1), (0, 0)))
+    return jnp.concatenate([sent[:first], cells, sent[first:]])
+
+
+def assemble(cnt_ref, now_ref, next_ref, own_ref, sent_ref):
     lane = lax.broadcasted_iota(jnp.int32, (1, 128), 1)
     cx, cy = now_ref.shape[:2]
     for x in range(cx):
@@ -58,6 +70,12 @@
             own_ref[cell, 3:4] = jnp.where(lane < cnt_ref[y, 0, x], now_ref[x, y, 0, 3:4], 0.0)
             own_ref[cell, 4:7] = next_ref[x, y, :, 0]
             own_ref[cell, 7:] = jnp.zeros((1, 128), jnp.float32)
+    first = carried(cx, cy)
+    for t in range(cx * cy - cy):
+        sent_ref[t] = own_ref[t if t < first else t + cy]
+    for k in range(cy):
+        for r in range(7):
+            sent_ref[7 * k + r, 7:] = own_ref[first + k, r : r + 1]
 
 
 CLASSES = 4
@@ -414,17 +432,22 @@
     nxt = jnp.transpose(positions_next, (0, 1, 3, 2, 4))
     vel = jnp.transpose(velocities, (0, 1, 3, 2, 4))
     cnt = jnp.transpose(halo_counts, (1, 2, 0))
-    own = pl.pallas_call(
+    own, sent = pl.pallas_call(
         assemble,
         in_specs=[SMEM, VMEM, VMEM],
-        out_specs=VMEM,
-        out_shape=jax.ShapeDtypeStruct((cx * cy, 8, slots), F32),
+        out_specs=[VMEM, VMEM],
+        out_shape=[
+            jax.ShapeDtypeStruct((cx * cy, 8, slots), F32),
+            jax.ShapeDtypeStruct((cx * cy - cy, 8, slots), F32),
+        ],
     )(cnt, positions_now, nxt)
-    other = lax.ppermute(own, "gz_1", [(0, 1), (1, 0)])
+    sent = lax.ppermute(sent, "gz_1", [(0, 1), (1, 0)])
+    other = unpacked(sent, cx, cy)
     lists, counts, acc0, base, links = first_forces(half[None], neighbour_lists, cnt, own, vel, descendants)
 
     def both(start):
-        ends = own[start : start + cy], other[start : start + cy]
+        place = start if start == 0 else start - cy
+        ends = own[start : start + cy], sent[place : place + cy]
         return jnp.where(half == 0, jnp.stack(ends), jnp.stack(ends[::-1]))
 
     below = lax.ppermute(both(cx * cy - cy), ZRING, zring_pairs(zs, 1))

time: 96.6 us -> 95.4 us (0.988)
  local copies, waits for them, and re-layouts: 2.39 us -> 4.19 us
  starting transfers between devices: 31.6 us -> 29.9 us
    unnamed x14 -> x21, local copies, waits for them, and re-layouts: 1.58 us -> 3.37 us
    ppermute x1, starting transfers between devices: 5.59 us -> 4.27 us  [shards(): above = lax.ppermute(both(0), ZRING, zring_pairs(zs, -1))]
where the time goes in v7:
time: 95.4 us; the launch traced here: 94.9 us
  blocking collectives  31.2 us (33%)
  starting transfers between devices  29.9 us (31%)
  Pallas kernels  23.9 us (25%)
  waiting for transfers between devices  4.65 us (5%)
  local copies, waits for them, and re-layouts  4.19 us (4%)
    all_to_all x2, blocking collectives, gathered(): lax.all_to_all(jnp.broadcast_to(row, (count, slots)), axes, 0, 0, tiled=T...  31.2 us
    ppermute x1, starting transfers between devices, shards(): sent = lax.ppermute(sent, 'gz_1', [(0, 1), (1, 0)])  16.4 us
    pallas_call x1, Pallas kernels, first_forces(): pl.pallas_call(functools.partial(own_pass, cap=cap), in_specs=[SMEM] * 4...  7.88 us
    pallas_call x1, Pallas kernels, finish(): pl.pallas_call(functools.partial(last_pass, cap=cap), in_specs=[SMEM] * 3...  4.53 us
    ppermute x1, waiting for transfers between devices, shards(): below = lax.ppermute(both(cx * cy - cy), ZRING, zring_pairs(zs, 1))  4.53 us
    pallas_call x1, Pallas kernels, other_forces(): pl.pallas_call(functools.partial(other_pass, cap=cap), in_specs=[SMEM, SM...  4.49 us
    ppermute x1, starting transfers between devices, shards(): above = lax.ppermute(both(0), ZRING, zring_pairs(zs, -1))  4.27 us
    pallas_call x1, Pallas kernels, far_forces(): pl.pallas_call(functools.partial(far_pass, cap=cap), in_specs=[SMEM, SMEM...  4.17 us
  transfers between devices with their start and end apart: 6, of which 2 were waited for; matrix products, arithmetic and copies ran while one was open for 1% of the time, Pallas kernels for 17%

profile of v7, /device:TPU:1, one launch (start us, length us, event | category | flops | bytes accessed | tf_op | source)
XLA Modules:
  0.0 94.9 jit_solution(12036358350305701907)
XLA Ops:
  0.6 0.0 copy-start.5
  0.6 0.0 copy-start.8
  0.7 1.6 %shard_map.122 = (f32[32,8,128]{2,1,0:T(8,128)}, f32[28,8,128]{2,1,0:T(8,128)}) custom-call(s32[4,1,8]{2,1,0:T(1,128)} %bitcast.31, f32[8,4,1,4,128]{4,3,2,1,0:T(4,128)} %now_ref.1, f32[8,4,3,1,128]{4,3,2,1,0:T(1,128)} %bitcast.36), custom_call_target="tpu_custom_call" | custom-call | tf_op jit(solution)/shard_map/pallas_call | solution.py:435
  2.3 0.0 copy-start.3
  2.3 16.4 %collective-permute-start = (f32[28,8,128]{2,1,0:T(8,128)}, f32[28,8,128]{2,1,0:T(8,128)S(1)}, u32[]{:S(2)}, u32[]{:S(2)}) collective-permute-start(f32[28,8,128]{2,1,0:T(8,128)} %get-tuple-element.20), channel_id=1, source_target_pairs={{0,1},{1,0},{2,3},{3,2},{4,5},{5,4},{6,7},{7,6},{8,9},{9,8},{10,11... | collective-permute-start | bytes 344072 | tf_op jit(solution)/shard_map/ppermute | solution.py:444
  18.7 0.0 copy-start.4
  18.7 0.7 slice_bitcast_fusion.5
  19.4 0.0 copy-start.2
  19.4 0.0 copy-done.5
  19.4 0.0 copy-done.8
  19.5 0.0 copy-done.3
  19.5 0.0 copy-done.4
  19.5 0.7 copy-done.2
  20.1 0.0 copy-start
  20.1 0.9 copy-done
  21.0 0.0 copy-start.6
  21.0 0.9 copy-done.6
  21.9 7.9 %shard_map.123 = (s32[2144]{0:T(1024)S(1)}, s32[4]{0:T(128)S(1)}, f32[32,8,128]{2,1,0:T(8,128)S(1)}, f32[32,8,128]{2,1,0:T(8,128)S(1)}, s32[32,8,128]{2,1,0:T(8,128)S(1)}) custom-call(s32[1]{0:T(128)} %bitcast.half_ref, s32[486]{0:T(512)S(1)} %copy-done.8, s32[8,4,1,14]{3,2,1,0:T(1,128)S(1)} %copy-done.5, s32[4,1,8]{2,1,0:T(1,128)S(1)} %bitcast.32, ...), custom_call_target="tpu_custom_call" | custom-call | flops 734003200 | bytes 1048576 | tf_op jit(solution)/shard_map/pallas_call | solution.py:362
  29.8 0.0 collective-permute-done
  29.9 4.3 %collective-permute-start.2 = (f32[2,4,8,128]{3,2,1,0:T(8,128)S(1)}, f32[2,4,8,128]{3,2,1,0:T(8,128)S(1)}, u32[]{:S(2)}, u32[]{:S(2)}) collective-permute-start(f32[2,4,8,128]{3,2,1,0:T(8,128)S(1)} %maximum_select_fusion.1), channel_id=1, source_target_pairs={{0,449},{64,0},{128,64},{192,128},{256,192},{320,256},{384,320},{4... | collective-permute-start | bytes 98312 | tf_op jit(solution)/shard_map/ppermute | solution.py:454
  34.1 1.9 %collective-permute-start.1 = (f32[2,4,8,128]{3,2,1,0:T(8,128)S(1)}, f32[2,4,8,128]{3,2,1,0:T(8,128)S(1)}, u32[]{:S(2)}, u32[]{:S(2)}) collective-permute-start(f32[2,4,8,128]{3,2,1,0:T(8,128)S(1)} %maximum_select_fusion), channel_id=1, source_target_pairs={{0,64},{64,128},{128,192},{192,256},{256,320},{320,384},{384,448},... | collective-permute-start | bytes 98312 | tf_op jit(solution)/shard_map/ppermute | solution.py:453
  36.1 4.5 %collective-permute-done.1 = f32[2,4,8,128]{3,2,1,0:T(8,128)S(1)} collective-permute-done((f32[2,4,8,128]{3,2,1,0:T(8,128)S(1)}, f32[2,4,8,128]{3,2,1,0:T(8,128)S(1)}, u32[]{:S(2)}, u32[]{:S(2)}) %collective-permute-start.1) | collective-permute-done | bytes 32800 | tf_op jit(solution)/shard_map/ppermute | solution.py:453
  40.7 0.0 copy-start.1
  40.7 0.0 collective-permute-done.2
  40.7 3.3 %collective-permute-start.3 = (f32[40,8,128]{2,1,0:T(8,128)S(1)}, f32[40,8,128]{2,1,0:T(8,128)S(1)}, u32[]{:S(2)}, u32[]{:S(2)}) collective-permute-start(f32[40,8,128]{2,1,0:T(8,128)S(1)} %bitcast_dynamic-update-slice_fusion.other_ref), channel_id=1, source_target_pairs={{0,2},{1,7},{2,4},{3,1},{4,6},{5,3},{6,0},{7,5},{8,10},{9,15},{10,... | collective-permute-start | bytes 491528 | tf_op jit(solution)/shard_map/ppermute | solution.py:462
  44.0 0.0 copy-done.1
  44.0 0.0 copy-start.7
  44.1 0.9 copy-done.7
  44.9 4.5 %shard_map.124 = (f32[32,8,128]{2,1,0:T(8,128)S(1)}, f32[2,10,8,128]{3,2,1,0:T(8,128)S(1)}, f32[2,10,8,128]{3,2,1,0:T(8,128)S(1)}) custom-call(s32[2144]{0:T(1024)S(1)} %get-tuple-element.18.list_ref, s32[4]{0:T(128)S(1)} %get-tuple-element.19.count_ref, f32[27,8,128]{2,1,0:T(8,128)S(1)} %copy-done.7, f32[40,8,128]{2,1,0:T(8,128)S(1)} %pad_maximum_fusion.own_ref, ...), custom_call_target="tpu_custom_call" | custom-call | flops 878182400 | bytes 1048576 | tf_op jit(solution)/shard_map/pallas_call | solution.py:382
  49.4 0.0 collective-permute-done.3.far_ref
  49.5 4.0 %collective-permute-start.4 = (f32[3,10,8,128]{3,2,1,0:T(8,128)S(1)}, f32[3,10,8,128]{3,2,1,0:T(8,128)S(1)}, u32[]{:S(2)}, u32[]{:S(2)}) collective-permute-start(f32[3,10,8,128]{3,2,1,0:T(8,128)S(1)} %pad_maximum_fusion.1), channel_id=1, source_target_pairs={{0,8},{8,16},{16,24},{24,32},{32,40},{40,48},{48,56},{56,0},{1,9},... | collective-permute-start | bytes 368648 | tf_op jit(solution)/shard_map/ppermute | solution.py:465
  53.5 0.0 collective-permute-start.5
  53.5 4.2 %shard_map.125.acc2_ref = f32[32,8,128]{2,1,0:T(8,128)S(1)} custom-call(s32[2144]{0:T(1024)S(1)} %get-tuple-element.18.list_ref, s32[4]{0:T(128)S(1)} %get-tuple-element.19.count_ref, f32[27,8,128]{2,1,0:T(8,128)S(1)} %copy-done.7, f32[40,8,128]{2,1,0:T(8,128)S(1)} %pad_maximum_fusion.own_ref, f32[40,8,128]{2,1,0:T(8,128)S(1)} %collective-permute-done.3.far_ref), custom_call_target="tpu_custom_call" | custom-call | flops 878182400 | bytes 1048576 | tf_op jit(solution)/shard_map/pallas_call | solution.py:395
  57.7 0.0 collective-permute-done.4.low_ref
  57.7 0.1 collective-permute-done.5.high_ref
  57.8 4.5 %shard_map.126 = (f32[8,4,3,1,128]{4,3,2,1,0:T(1,128)S(1)}, f32[8,4,1,128]{3,2,1,0:T(1,128)S(1)}, f32[1,128]{1,0:T(1,128)S(1)}) custom-call(s32[1]{0:T(128)} %bitcast.half_ref, s32[2144]{0:T(1024)S(1)} %get-tuple-element.18.list_ref, s32[4]{0:T(128)S(1)} %get-tuple-element.19.count_ref, f32[27,8,128]{2,1,0:T(8,128)S(1)} %copy-done.7, ...), custom_call_target="tpu_custom_call" | custom-call | flops 878182400 | bytes 1048576 | tf_op jit(solution)/shard_map/pallas_call | solution.py:409
  62.4 14.0 %all_to_all.14 = f32[32,1,128]{2,1,0:T(1,128)S(1)} all-to-all(f32[32,1,128]{2,1,0:T(1,128)S(1)} %broadcast_in_dim.24), channel_id=1, replica_groups=mesh['gx'=8,'gy_0'=4,'gy_1'=2,'gz_0'=4,'gz_1'=2] {'gz_0','gy_0','gy_1'}, dimensions={0} | all-to-all | bytes 32768 | tf_op jit(solution)/shard_map/all_to_all | solution.py:474
  76.4 17.2 %all_to_all.15 = f32[16,1,128]{2,1,0:T(1,128)S(1)} all-to-all(f32[16,1,128]{2,1,0:T(1,128)S(1)} %broadcast_in_dim.25), channel_id=1, replica_groups=mesh['gx'=8,'gy_0'=4,'gy_1'=2,'gz_0'=4,'gz_1'=2] {'gx','gz_1'}, dimensions={0} | all-to-all | bytes 16384 | tf_op jit(solution)/shard_map/all_to_all | solution.py:474
  93.6 1.2 %shard_map.127 = (f32[8,4,1,128]{3,2,1,0:T(1,128)}, f32[8,4,3,1,128]{4,3,2,1,0:T(1,128)}) custom-call(f32[16,128]{1,0:T(8,128)S(1)} %bitcast.30, f32[8,4,1,128]{3,2,1,0:T(1,128)S(1)} %get-tuple-element.28.sq_ref, f32[8,4,3,1,128]{4,3,2,1,0:T(1,128)S(1)} %get-tuple-element.29.drift_ref), custom_call_target="tpu_custom_call" | custom-call | tf_op jit(solution)/shard_map/pallas_call | solution.py:477
  (19 shorter events, 0.2 us)
Async XLA Ops:
  0.6 18.8 %copy-start.5 = (s32[8,4,1,14]{3,2,1,0:T(1,128)S(1)}, s32[8,4,1,14]{3,2,1,0:T(1,128)}, u32[]{:S(2)}) copy-start(s32[8,4,1,14]{3,2,1,0:T(1,128)} %nbr_ref.1) | copy-start | bytes 5380
  0.6 18.8 %copy-start.8 = (s32[486]{0:T(512)S(1)}, s32[486]{0:T(512)}, u32[]{:S(2)}) copy-start(s32[486]{0:T(512)} %constant.15.clone.table_ref) | copy-start | bytes 5836
  2.3 17.2 %copy-start.3 = (f32[8,4,1,3,128]{4,2,3,1,0:T(1,128)S(1)}, f32[8,4,1,3,128]{4,2,3,1,0:T(1,128)}, u32[]{:S(2)}) copy-start(f32[8,4,1,3,128]{4,2,3,1,0:T(1,128)} %param.12) | copy-start | bytes 147460
  2.3 27.5 %collective-permute-start = (f32[28,8,128]{2,1,0:T(8,128)}, f32[28,8,128]{2,1,0:T(8,128)S(1)}, u32[]{:S(2)}, u32[]{:S(2)}) collective-permute-start(f32[28,8,128]{2,1,0:T(8,128)} %get-tuple-element.20), channel_id=1, source_target_pairs={{0,1},{1,0},{2,3},{3,2},{4,5},{5,4},{6,7},{7,6},{8,9},{9,8},{10,11... | collective-permute-start | bytes 344072 | tf_op jit(solution)/shard_map/ppermute | solution.py:444
  18.7 0.8 copy-start.4
  19.4 0.7 copy-start.2
  20.1 0.9 copy-start
  21.0 0.9 copy-start.6
  29.9 10.9 %collective-permute-start.2 = (f32[2,4,8,128]{3,2,1,0:T(8,128)S(1)}, f32[2,4,8,128]{3,2,1,0:T(8,128)S(1)}, u32[]{:S(2)}, u32[]{:S(2)}) collective-permute-start(f32[2,4,8,128]{3,2,1,0:T(8,128)S(1)} %maximum_select_fusion.1), channel_id=1, source_target_pairs={{0,449},{64,0},{128,64},{192,128},{256,192},{320,256},{384,320},{4... | collective-permute-start | bytes 98312 | tf_op jit(solution)/shard_map/ppermute | solution.py:454
  34.1 6.5 %collective-permute-start.1 = (f32[2,4,8,128]{3,2,1,0:T(8,128)S(1)}, f32[2,4,8,128]{3,2,1,0:T(8,128)S(1)}, u32[]{:S(2)}, u32[]{:S(2)}) collective-permute-start(f32[2,4,8,128]{3,2,1,0:T(8,128)S(1)} %maximum_select_fusion), channel_id=1, source_target_pairs={{0,64},{64,128},{128,192},{192,256},{256,320},{320,384},{384,448},... | collective-permute-start | bytes 98312 | tf_op jit(solution)/shard_map/ppermute | solution.py:453
  40.7 3.3 %copy-start.1 = (f32[32,8,128]{2,1,0:T(8,128)S(1)}, f32[32,8,128]{2,1,0:T(8,128)}, u32[]{:S(2)}) copy-start(f32[32,8,128]{2,1,0:T(8,128)} %get-tuple-element.17.own_ref) | copy-start | bytes 393220
  40.7 8.7 %collective-permute-start.3 = (f32[40,8,128]{2,1,0:T(8,128)S(1)}, f32[40,8,128]{2,1,0:T(8,128)S(1)}, u32[]{:S(2)}, u32[]{:S(2)}) collective-permute-start(f32[40,8,128]{2,1,0:T(8,128)S(1)} %bitcast_dynamic-update-slice_fusion.other_ref), channel_id=1, source_target_pairs={{0,2},{1,7},{2,4},{3,1},{4,6},{5,3},{6,0},{7,5},{8,10},{9,15},{10,... | collective-permute-start | bytes 491528 | tf_op jit(solution)/shard_map/ppermute | solution.py:462
  44.0 0.9 copy-start.7
  49.5 8.2 %collective-permute-start.4 = (f32[3,10,8,128]{3,2,1,0:T(8,128)S(1)}, f32[3,10,8,128]{3,2,1,0:T(8,128)S(1)}, u32[]{:S(2)}, u32[]{:S(2)}) collective-permute-start(f32[3,10,8,128]{3,2,1,0:T(8,128)S(1)} %pad_maximum_fusion.1), channel_id=1, source_target_pairs={{0,8},{8,16},{16,24},{24,32},{32,40},{40,48},{48,56},{56,0},{1,9},... | collective-permute-start | bytes 368648 | tf_op jit(solution)/shard_map/ppermute | solution.py:465
  53.5 4.3 %collective-permute-start.5 = (f32[3,10,8,128]{3,2,1,0:T(8,128)S(1)}, f32[3,10,8,128]{3,2,1,0:T(8,128)S(1)}, u32[]{:S(2)}, u32[]{:S(2)}) collective-permute-start(f32[3,10,8,128]{3,2,1,0:T(8,128)S(1)} %pad_maximum_fusion.2), channel_id=1, source_target_pairs={{0,56},{8,0},{16,8},{24,16},{32,24},{40,32},{48,40},{56,48},{1,57}... | collective-permute-start | bytes 368648 | tf_op jit(solution)/shard_map/ppermute | solution.py:466

commit v8 on v7

--- a/solution.py
+++ b/solution.py
@@ -167,9 +167,11 @@
 
 def own_pass(
     half_ref, table_ref, nbr_ref, cnt_ref, off_ref, own_ref, vel_ref, desc_ref,
-    list_ref, count_ref, acc_ref, base_ref, link_ref, st_ref, mc_ref, *, cap
+    list_ref, count_ref, acc_ref, base_ref, link_ref, kept_ref, table_out_ref, st_ref, mc_ref, *, cap
 ):
     cx, cy = nbr_ref.shape[:2]
+    kept_ref[...] = own_ref[...]
+    table_out_ref[...] = off_ref[...]
     width = nbr_ref.shape[3]
     half = half_ref[0]
     lane = lax.broadcasted_iota(I32, (1, 128), 1)
@@ -285,16 +287,27 @@
         fill(0, other_ref, 1)
         fill(2, far_ref, 2)
 
+    sub = sublanes()
+    for x in range(px):
+        for y in range(cy + 2):
+            cube_ref[0, x, y] = jnp.where(sub < 4, pltpu.roll(cube_ref[0, x, y], 4, 0), cube_ref[2, x, y])
+
     def one_cell(x, y):
         cell = x * cy + y
         dcode = link_ref[cell, 0:1]
         dslot = jnp.broadcast_to(link_ref[cell, 1:2], (8, 128))
-        found = jnp.zeros((8, 128), F32)
-        for code in range(27):
-            dx, dy, dz = code // 9, code // 3 % 3, code % 3
-            got = jnp.take_along_axis(cube_ref[dz, x + dx, y + dy], dslot, axis=1)
-            found = jnp.where(dcode == code, got, found)
-        error = base_ref[cell, :3] + found[4:7] - HALF_KICK * acc_ref[cell, :3]
+        key = jnp.where(sub < 4, dcode, dcode - 2)
+        level = jnp.zeros((8, 128), F32)
+        sides = jnp.zeros((8, 128), F32)
+        for dx in range(3):
+            for dy in range(3):
+                code = 9 * dx + 3 * dy
+                got = jnp.take_along_axis(cube_ref[1, x + dx, y + dy], dslot, axis=1)
+                level = jnp.where(dcode == code + 1, got, level)
+                got = jnp.take_along_axis(cube_ref[0, x + dx, y + dy], dslot, axis=1)
+                sides = jnp.where(key == code, got, sides)
+        found = (level[4:7] + sides[4:7]) + sides[:3]
+        error = base_ref[cell, :3] + found - HALF_KICK * acc_ref[cell, :3]
         alive = base_ref[cell, 3:4]
         drift_ref[x, y, :, 0] = jnp.where(alive > 0.0, error, 0.0)
         squared = jnp.where(alive > 0.0, jnp.sum(error * error, axis=0, keepdims=True), 0.0)
@@ -362,13 +375,15 @@
     return pl.pallas_call(
         functools.partial(own_pass, cap=cap),
         in_specs=[SMEM] * 4 + [VMEM] * 4,
-        out_specs=[SMEM, SMEM, VMEM, VMEM, VMEM],
+        out_specs=[SMEM, SMEM] + [VMEM] * 5,
         out_shape=[
             jax.ShapeDtypeStruct((CLASSES * cap,), I32),
             jax.ShapeDtypeStruct((CLASSES,), I32),
             rows,
             rows,
             jax.ShapeDtypeStruct((cells, 8, 128), I32),
+            rows,
+            jax.ShapeDtypeStruct((27, 8, 128), F32),
         ],
         scratch_shapes=features_of(cells),
         cost_estimate=cost(items // 4),
@@ -376,7 +391,7 @@
     )(half, item_table(cx, cy), neighbour_lists, cnt, offset_table(), own, vel, descendants)
 
 
-def other_forces(lists, counts, own, other, cells, px):
+def other_forces(lists, counts, offsets, own, other, cells, px):
     cap = lists.shape[0] // CLASSES
     strip = jax.ShapeDtypeStruct((2, px, 8, 128), F32)
     return pl.pallas_call(
@@ -387,10 +402,10 @@
         scratch_shapes=features_of(2 * own.shape[0] - cells),
         cost_estimate=cost(cap // 4),
         compiler_params=params(),
-    )(lists, counts, offset_table(), own, other)
-
-
-def far_forces(lists, counts, own, far, cells):
+    )(lists, counts, offsets, own, other)
+
+
+def far_forces(lists, counts, offsets, own, far, cells):
     cap = lists.shape[0] // CLASSES
     return pl.pallas_call(
         functools.partial(far_pass, cap=cap),
@@ -400,10 +415,10 @@
         scratch_shapes=features_of(far.shape[0]),
         cost_estimate=cost(cap // 4),
         compiler_params=params(),
-    )(lists, counts, offset_table(), own, far)
-
-
-def finish(half, lists, counts, planes, low, high, sums, base, links, cx, cy):
+    )(lists, counts, offsets, own, far)
+
+
+def finish(half, lists, counts, offsets, planes, low, high, sums, base, links, cx, cy):
     px = cx + 2
     cap = lists.shape[0] // CLASSES
     return pl.pallas_call(
@@ -420,7 +435,7 @@
         + [pltpu.VMEM((3, px, cy + 2, 8, 128), F32)],
         cost_estimate=cost(cap // 4),
         compiler_params=params(),
-    )(half, lists, counts, offset_table(), *planes, low, high, *sums, base, links)
+    )(half, lists, counts, offsets, *planes, low, high, *sums, base, links)
 
 
 def shards(positions_now, velocities, positions_next, halo_counts, neighbour_lists, descendants):
@@ -443,7 +458,9 @@
     )(cnt, positions_now, nxt)
     sent = lax.ppermute(sent, "gz_1", [(0, 1), (1, 0)])
     other = unpacked(sent, cx, cy)
-    lists, counts, acc0, base, links = first_forces(half[None], neighbour_lists, cnt, own, vel, descendants)
+    lists, counts, acc0, base, links, own, offsets = first_forces(
+        half[None], neighbour_lists, cnt, own, vel, descendants
+    )
 
     def both(start):
         place = start if start == 0 else start - cy
@@ -460,13 +477,13 @@
     own = widened(own, half)
     other = widened(other, 1 - half)
     far = lax.ppermute(other, GZ, xhop_pairs(xs))
-    acc1, top, bottom = other_forces(lists, counts, own, other, cx * cy, cx + 2)
+    acc1, top, bottom = other_forces(lists, counts, offsets, own, other, cx * cy, cx + 2)
     rows = far.reshape(cx + 2, cy * 8, slots)
     low = lax.ppermute(jnp.concatenate([top, rows[None, :, 8 * cy - 8 :]]), GY, ring(ny, 1))
     high = lax.ppermute(jnp.concatenate([bottom, rows[None, :, :8]]), GY, ring(ny, -1))
-    acc2 = far_forces(lists, counts, own, far, cx * cy)
+    acc2 = far_forces(lists, counts, offsets, own, far, cx * cy)
     drift, squared, part = finish(
-        half[None], lists, counts, (own, other, far), low, high, (acc0, acc1, acc2), base, links, cx, cy
+        half[None], lists, counts, offsets, (own, other, far), low, high, (acc0, acc1, acc2), base, links, cx, cy
     )
 
     def gathered(row, axes):

time: 95.4 us -> 94.9 us (level)
  starting transfers between devices: 29.9 us -> 31.9 us
  local copies, waits for them, and re-layouts: 4.19 us -> 2.56 us
  Pallas kernels: 23.9 us -> 22.7 us
    ppermute x1, starting transfers between devices: 4.27 us -> 5.96 us  [shards(): above = lax.ppermute(both(0), ZRING, zring_pairs(zs, -1))]
    unnamed x21 -> x17, local copies, waits for them, and re-layouts: 3.37 us -> 2.47 us
  transfers between devices with their start and end apart: 6 -> 6, of which waited for: 2 -> 2; matrix products, arithmetic and copies ran while one was open for 1% -> 0% of each run, Pallas kernels for 17% -> 16%
where the time goes in v8:
time: 94.9 us; the launch traced here: 94.5 us
  starting transfers between devices  31.9 us (34%)
  blocking collectives  31.7 us (33%)
  Pallas kernels  22.7 us (24%)
  waiting for transfers between devices  4.65 us (5%)
  local copies, waits for them, and re-layouts  2.56 us (3%)
    all_to_all x2, blocking collectives, gathered(): lax.all_to_all(jnp.broadcast_to(row, (count, slots)), axes, 0, 0, tiled=T...  31.7 us
    ppermute x1, starting transfers between devices, shards(): sent = lax.ppermute(sent, 'gz_1', [(0, 1), (1, 0)])  16.4 us
    pallas_call x1, Pallas kernels, first_forces(): pl.pallas_call(functools.partial(own_pass, cap=cap), in_specs=[SMEM] * 4...  6.93 us
    ppermute x1, starting transfers between devices, shards(): above = lax.ppermute(both(0), ZRING, zring_pairs(zs, -1))  5.96 us
    ppermute x1, waiting for transfers between devices, shards(): below = lax.ppermute(both(cx * cy - cy), ZRING, zring_pairs(zs, 1))  4.53 us
    pallas_call x1, Pallas kernels, other_forces(): pl.pallas_call(functools.partial(other_pass, cap=cap), in_specs=[SMEM, SM...  4.49 us
    ppermute x1, starting transfers between devices, shards(): lax.ppermute(jnp.concatenate([top, rows[None, :, 8 * cy - 8:]]), GY, ring...  4.47 us
    pallas_call x1, Pallas kernels, finish(): pl.pallas_call(functools.partial(last_pass, cap=cap), in_specs=[SMEM] * 3...  4.28 us
  transfers between devices with their start and end apart: 6, of which 2 were waited for; matrix products, arithmetic and copies ran while one was open for 0% of the time, Pallas kernels for 16%

profile of v8, /device:TPU:1, one launch (start us, length us, event | category | flops | bytes accessed | tf_op | source)
XLA Modules:
  0.0 94.5 jit_solution(4869345855683047315)
XLA Ops:
  0.6 0.0 copy-start.2
  0.6 0.0 copy-start.3
  0.7 0.0 copy-start.6
  0.7 1.7 %shard_map.95 = (f32[32,8,128]{2,1,0:T(8,128)}, f32[28,8,128]{2,1,0:T(8,128)}) custom-call(s32[4,1,8]{2,1,0:T(1,128)} %bitcast.31, f32[8,4,1,4,128]{4,3,2,1,0:T(4,128)} %now_ref.1, f32[8,4,3,1,128]{4,3,2,1,0:T(1,128)} %bitcast.36), custom_call_target="tpu_custom_call" | custom-call | tf_op jit(solution)/shard_map/pallas_call | solution.py:450
  2.3 0.0 copy-start.4
  2.3 16.4 %collective-permute-start = (f32[28,8,128]{2,1,0:T(8,128)}, f32[28,8,128]{2,1,0:T(8,128)S(1)}, u32[]{:S(2)}, u32[]{:S(2)}) collective-permute-start(f32[28,8,128]{2,1,0:T(8,128)} %get-tuple-element.24), channel_id=1, source_target_pairs={{0,1},{1,0},{2,3},{3,2},{4,5},{5,4},{6,7},{7,6},{8,9},{9,8},{10,11... | collective-permute-start | bytes 344072 | tf_op jit(solution)/shard_map/ppermute | solution.py:459
  18.7 0.0 copy-start
  18.7 0.0 copy-done.2
  18.7 0.0 copy-done.3
  18.8 0.0 copy-done.6
  18.8 0.0 copy-done.4
  18.8 0.6 copy-done
  19.4 0.0 copy-start.1
  19.4 0.9 copy-done.1
  20.3 0.0 copy-start.5
  20.3 0.9 copy-done.5
  21.2 6.9 %shard_map.96 = (s32[2144]{0:T(1024)S(1)}, s32[4]{0:T(128)S(1)}, f32[32,8,128]{2,1,0:T(8,128)S(1)}, f32[32,8,128]{2,1,0:T(8,128)S(1)}, s32[32,8,128]{2,1,0:T(8,1...) custom-call(s32[1]{0:T(128)} %bitcast.half_ref, s32[486]{0:T(512)S(1)} %copy-done.6, ...), custom_call_target="tpu_custom_call" | custom-call | flops 734003200 | bytes 1048576 | tf_op jit(solution)/shard_map/pallas_call | solution.py:375
  28.2 0.0 collective-permute-done
  28.2 6.0 %collective-permute-start.2 = (f32[2,4,8,128]{3,2,1,0:T(8,128)S(1)}, f32[2,4,8,128]{3,2,1,0:T(8,128)S(1)}, u32[]{:S(2)}, u32[]{:S(2)}) collective-permute-start(f32[2,4,8,128]{3,2,1,0:T(8,128)S(1)} %maximum_select_fusion.1), channel_id=1, source_target_pairs={{0,449},{64,0},{128,64},{192,128},{256,192},{320,256},{384,320},{4... | collective-permute-start | bytes 98312 | tf_op jit(solution)/shard_map/ppermute | solution.py:471
  34.2 1.9 %collective-permute-start.1 = (f32[2,4,8,128]{3,2,1,0:T(8,128)S(1)}, f32[2,4,8,128]{3,2,1,0:T(8,128)S(1)}, u32[]{:S(2)}, u32[]{:S(2)}) collective-permute-start(f32[2,4,8,128]{3,2,1,0:T(8,128)S(1)} %maximum_select_fusion), channel_id=1, source_target_pairs={{0,64},{64,128},{128,192},{192,256},{256,320},{320,384},{384,448},... | collective-permute-start | bytes 98312 | tf_op jit(solution)/shard_map/ppermute | solution.py:470
  36.2 4.5 %collective-permute-done.1 = f32[2,4,8,128]{3,2,1,0:T(8,128)S(1)} collective-permute-done((f32[2,4,8,128]{3,2,1,0:T(8,128)S(1)}, f32[2,4,8,128]{3,2,1,0:T(8,128)S(1)}, u32[]{:S(2)}, u32[]{:S(2)}) %collective-permute-start.1) | collective-permute-done | bytes 32800 | tf_op jit(solution)/shard_map/ppermute | solution.py:470
  40.7 0.0 collective-permute-done.2
  40.8 3.1 %collective-permute-start.3 = (f32[40,8,128]{2,1,0:T(8,128)S(1)}, f32[40,8,128]{2,1,0:T(8,128)S(1)}, u32[]{:S(2)}, u32[]{:S(2)}) collective-permute-start(f32[40,8,128]{2,1,0:T(8,128)S(1)} %bitcast_dynamic-update-slice_fusion.other_ref), channel_id=1, source_target_pairs={{0,2},{1,7},{2,4},{3,1},{4,6},{5,3},{6,0},{7,5},{8,10},{9,15},{10,... | collective-permute-start | bytes 491528 | tf_op jit(solution)/shard_map/ppermute | solution.py:479
  43.9 4.5 %shard_map.97 = (f32[32,8,128]{2,1,0:T(8,128)S(1)}, f32[2,10,8,128]{3,2,1,0:T(8,128)S(1)}, f32[2,10,8,128]{3,2,1,0:T(8,128)S(1)}) custom-call(s32[2144]{0:T(1024)S(1)} %get-tuple-element.20.list_ref, s32[4]{0:T(128)S(1)} %get-tuple-element.21.count_ref, f32[27,8,128]{2,1,0:T(8,128)S(1)} %get-tuple-element.22.off_ref, ...), custom_call_target="tpu_custom_call" | custom-call | flops 878182400 | bytes 1048576 | tf_op jit(solution)/shard_map/pallas_call | solution.py:397
  48.4 0.0 collective-permute-done.3.far_ref
  48.5 4.5 %collective-permute-start.4 = (f32[3,10,8,128]{3,2,1,0:T(8,128)S(1)}, f32[3,10,8,128]{3,2,1,0:T(8,128)S(1)}, u32[]{:S(2)}, u32[]{:S(2)}) collective-permute-start(f32[3,10,8,128]{3,2,1,0:T(8,128)S(1)} %pad_maximum_fusion.1), channel_id=1, source_target_pairs={{0,8},{8,16},{16,24},{24,32},{32,40},{40,48},{48,56},{56,0},{1,9},... | collective-permute-start | bytes 368648 | tf_op jit(solution)/shard_map/ppermute | solution.py:482
  53.0 0.0 collective-permute-start.5
  53.0 4.2 %shard_map.98.acc2_ref = f32[32,8,128]{2,1,0:T(8,128)S(1)} custom-call(s32[2144]{0:T(1024)S(1)} %get-tuple-element.20.list_ref, s32[4]{0:T(128)S(1)} %get-tuple-element.21.count_ref, f32[27,8,128]{2,1,0:T(8,128)S(1)} %get-tuple-element.22.off_ref, f32[40,8,128]{2,1,0:T(8,128)S(1)} %pad_maximum_fusion.own_ref, f32[40,8,128]{2,1,0:T(8,128)S(1)} %collective-permute-done.3.far_ref), custom_call_target="tpu_custom_call" | custom-call | flops 878182400 | bytes 1048576 | tf_op jit(solution)/shard_map/pallas_call | solution.py:410
  57.2 0.0 collective-permute-done.4.low_ref
  57.2 0.1 collective-permute-done.5.high_ref
  57.3 4.3 %shard_map.99 = (f32[8,4,3,1,128]{4,3,2,1,0:T(1,128)S(1)}, f32[8,4,1,128]{3,2,1,0:T(1,128)S(1)}, f32[1,128]{1,0:T(1,128)S(1)}) custom-call(s32[1]{0:T(128)} %bitcast.half_ref, s32[2144]{0:T(1024)S(1)} %get-tuple-element.20.list_ref, s32[4]{0:T(128)S(1)} %get-tuple-element.21.count_ref, f32[27,8,128]{2,1,0:T(8,128)S(1)} %get-tuple-element.22.off_ref, ...), custom_call_target="tpu_custom_call" | custom-call | flops 878182400 | bytes 1048576 | tf_op jit(solution)/shard_map/pallas_call | solution.py:424
  61.6 13.5 %all_to_all.14 = f32[32,1,128]{2,1,0:T(1,128)S(1)} all-to-all(f32[32,1,128]{2,1,0:T(1,128)S(1)} %broadcast_in_dim.24), channel_id=1, replica_groups=mesh['gx'=8,'gy_0'=4,'gy_1'=2,'gz_0'=4,'gz_1'=2] {'gz_0','gy_0','gy_1'}, dimensions={0} | all-to-all | bytes 32768 | tf_op jit(solution)/shard_map/all_to_all | solution.py:491
  75.2 18.1 %all_to_all.15 = f32[16,1,128]{2,1,0:T(1,128)S(1)} all-to-all(f32[16,1,128]{2,1,0:T(1,128)S(1)} %broadcast_in_dim.25), channel_id=1, replica_groups=mesh['gx'=8,'gy_0'=4,'gy_1'=2,'gz_0'=4,'gz_1'=2] {'gx','gz_1'}, dimensions={0} | all-to-all | bytes 16384 | tf_op jit(solution)/shard_map/all_to_all | solution.py:491
  93.3 1.2 %shard_map.100 = (f32[8,4,1,128]{3,2,1,0:T(1,128)}, f32[8,4,3,1,128]{4,3,2,1,0:T(1,128)}) custom-call(f32[16,128]{1,0:T(8,128)S(1)} %bitcast.30, f32[8,4,1,128]{3,2,1,0:T(1,128)S(1)} %get-tuple-element.32.sq_ref, f32[8,4,3,1,128]{4,3,2,1,0:T(1,128)S(1)} %get-tuple-element.33.drift_ref), custom_call_target="tpu_custom_call" | custom-call | tf_op jit(solution)/shard_map/pallas_call | solution.py:494
  (20 shorter events, 0.2 us)
Async XLA Ops:
  0.6 18.1 %copy-start.2 = (f32[8,4,1,3,128]{4,2,3,1,0:T(1,128)S(1)}, f32[8,4,1,3,128]{4,2,3,1,0:T(1,128)}, u32[]{:S(2)}) copy-start(f32[8,4,1,3,128]{4,2,3,1,0:T(1,128)} %param.9) | copy-start | bytes 147460
  0.6 18.1 %copy-start.3 = (s32[8,4,1,2,128]{4,3,2,1,0:T(2,128)S(1)}, s32[8,4,1,2,128]{4,3,2,1,0:T(2,128)}, u32[]{:S(2)}) copy-start(s32[8,4,1,2,128]{4,3,2,1,0:T(2,128)} %desc_ref.1) | copy-start | bytes 98308
  0.7 18.1 %copy-start.6 = (s32[486]{0:T(512)S(1)}, s32[486]{0:T(512)}, u32[]{:S(2)}) copy-start(s32[486]{0:T(512)} %constant.15.clone.table_ref) | copy-start | bytes 5836
  2.3 16.5 %copy-start.4 = (s32[8,4,1,14]{3,2,1,0:T(1,128)S(1)}, s32[8,4,1,14]{3,2,1,0:T(1,128)}, u32[]{:S(2)}) copy-start(s32[8,4,1,14]{3,2,1,0:T(1,128)} %nbr_ref.1) | copy-start | bytes 5380
  2.3 25.8 %collective-permute-start = (f32[28,8,128]{2,1,0:T(8,128)}, f32[28,8,128]{2,1,0:T(8,128)S(1)}, u32[]{:S(2)}, u32[]{:S(2)}) collective-permute-start(f32[28,8,128]{2,1,0:T(8,128)} %get-tuple-element.24), channel_id=1, source_target_pairs={{0,1},{1,0},{2,3},{3,2},{4,5},{5,4},{6,7},{7,6},{8,9},{9,8},{10,11... | collective-permute-start | bytes 344072 | tf_op jit(solution)/shard_map/ppermute | solution.py:459
  18.7 0.7 copy-start
  19.4 0.9 copy-start.1
  20.3 0.9 copy-start.5
  28.2 12.5 %collective-permute-start.2 = (f32[2,4,8,128]{3,2,1,0:T(8,128)S(1)}, f32[2,4,8,128]{3,2,1,0:T(8,128)S(1)}, u32[]{:S(2)}, u32[]{:S(2)}) collective-permute-start(f32[2,4,8,128]{3,2,1,0:T(8,128)S(1)} %maximum_select_fusion.1), channel_id=1, source_target_pairs={{0,449},{64,0},{128,64},{192,128},{256,192},{320,256},{384,320},{4... | collective-permute-start | bytes 98312 | tf_op jit(solution)/shard_map/ppermute | solution.py:471
  34.2 6.5 %collective-permute-start.1 = (f32[2,4,8,128]{3,2,1,0:T(8,128)S(1)}, f32[2,4,8,128]{3,2,1,0:T(8,128)S(1)}, u32[]{:S(2)}, u32[]{:S(2)}) collective-permute-start(f32[2,4,8,128]{3,2,1,0:T(8,128)S(1)} %maximum_select_fusion), channel_id=1, source_target_pairs={{0,64},{64,128},{128,192},{192,256},{256,320},{320,384},{384,448},... | collective-permute-start | bytes 98312 | tf_op jit(solution)/shard_map/ppermute | solution.py:470
  40.8 7.7 %collective-permute-start.3 = (f32[40,8,128]{2,1,0:T(8,128)S(1)}, f32[40,8,128]{2,1,0:T(8,128)S(1)}, u32[]{:S(2)}, u32[]{:S(2)}) collective-permute-start(f32[40,8,128]{2,1,0:T(8,128)S(1)} %bitcast_dynamic-update-slice_fusion.other_ref), channel_id=1, source_target_pairs={{0,2},{1,7},{2,4},{3,1},{4,6},{5,3},{6,0},{7,5},{8,10},{9,15},{10,... | collective-permute-start | bytes 491528 | tf_op jit(solution)/shard_map/ppermute | solution.py:479
  48.5 8.7 %collective-permute-start.4 = (f32[3,10,8,128]{3,2,1,0:T(8,128)S(1)}, f32[3,10,8,128]{3,2,1,0:T(8,128)S(1)}, u32[]{:S(2)}, u32[]{:S(2)}) collective-permute-start(f32[3,10,8,128]{3,2,1,0:T(8,128)S(1)} %pad_maximum_fusion.1), channel_id=1, source_target_pairs={{0,8},{8,16},{16,24},{24,32},{32,40},{40,48},{48,56},{56,0},{1,9},... | collective-permute-start | bytes 368648 | tf_op jit(solution)/shard_map/ppermute | solution.py:482
  53.0 4.3 %collective-permute-start.5 = (f32[3,10,8,128]{3,2,1,0:T(8,128)S(1)}, f32[3,10,8,128]{3,2,1,0:T(8,128)S(1)}, u32[]{:S(2)}, u32[]{:S(2)}) collective-permute-start(f32[3,10,8,128]{3,2,1,0:T(8,128)S(1)} %pad_maximum_fusion.2), channel_id=1, source_target_pairs={{0,56},{8,0},{16,8},{24,16},{32,24},{40,32},{48,40},{56,48},{1,57}... | collective-permute-start | bytes 368648 | tf_op jit(solution)/shard_map/ppermute | solution.py:483

commit v9 on v8

--- a/solution.py
+++ b/solution.py
@@ -456,26 +456,22 @@
             jax.ShapeDtypeStruct((cx * cy - cy, 8, slots), F32),
         ],
     )(cnt, positions_now, nxt)
-    sent = lax.ppermute(sent, "gz_1", [(0, 1), (1, 0)])
-    other = unpacked(sent, cx, cy)
+    swap = [(0, 1), (1, 0)]
+    sent = lax.ppermute(sent, "gz_1", swap)
+    last = cx * cy - cy
+    below = lax.ppermute(own[last:], ZRING, zring_pairs(zs, 1))
+    above = lax.ppermute(own[:cy], ZRING, zring_pairs(zs, -1))
+    edges = jnp.concatenate([below, above])
+    traded = lax.ppermute(edges, "gz_1", swap)
     lists, counts, acc0, base, links, own, offsets = first_forces(
         half[None], neighbour_lists, cnt, own, vel, descendants
     )
-
-    def both(start):
-        place = start if start == 0 else start - cy
-        ends = own[start : start + cy], sent[place : place + cy]
-        return jnp.where(half == 0, jnp.stack(ends), jnp.stack(ends[::-1]))
-
-    below = lax.ppermute(both(cx * cy - cy), ZRING, zring_pairs(zs, 1))
-    above = lax.ppermute(both(0), ZRING, zring_pairs(zs, -1))
-
-    def widened(block, plane):
-        ends = [jnp.where(plane == 0, v[0], v[1]) for v in (below, above)]
-        return jnp.concatenate([ends[0], block, ends[1]], axis=0)
-
-    own = widened(own, half)
-    other = widened(other, 1 - half)
+    place = lax.axis_index("gx")
+    ends = ((slice(0, cy), place == 0), (slice(cy, 2 * cy), place == zs - 1))
+    own_ends = [jnp.where(crossing, traded[part], edges[part]) for part, crossing in ends]
+    other_ends = [jnp.where(crossing, edges[part], traded[part]) for part, crossing in ends]
+    own = jnp.concatenate([own_ends[0], own, own_ends[1]])
+    other = jnp.concatenate([other_ends[0], unpacked(sent, cx, cy), other_ends[1]])
     far = lax.ppermute(other, GZ, xhop_pairs(xs))
     acc1, top, bottom = other_forces(lists, counts, offsets, own, other, cx * cy, cx + 2)
     rows = far.reshape(cx + 2, cy * 8, slots)

time: 94.9 us -> 95.5 us (level)
  starting transfers between devices: 31.9 us -> 34 us
  waiting for transfers between devices: 4.65 us -> 2.63 us
  blocking collectives: 31.7 us -> 33 us
    ppermute x3 -> x4, starting transfers between devices: 24.3 us -> 27.9 us  [the longest x1 9.5 us: shards(): above = lax.ppermute(own[:cy], ZRING, zring_pairs(zs, -1))]
    ppermute x3 -> x4, waiting for transfers between devices: 4.53 us -> 2.24 us  [the longest x1 2.23 us: shards(): traded = lax.ppermute(edges, 'gz_1', swap)]
    unnamed x17, local copies, waits for them, and re-layouts: 2.47 us -> 0.94 us
    ppermute x1, starting transfers between devices: 4.47 us -> 2.99 us  [shards(): lax.ppermute(jnp.concatenate([top, rows[None, :, 8 * cy - 8:]]), GY, ring...]
    all_to_all x2, blocking collectives: 31.7 us -> 33 us  [gathered(): lax.all_to_all(jnp.broadcast_to(row, (count, slots)), axes, 0, 0, tiled=T...]
  transfers between devices with their start and end apart: 6 -> 7, of which waited for: 2 -> 3; matrix products, arithmetic and copies ran while one was open for 0% -> 0% of each run, Pallas kernels for 16% -> 16%
where the time goes in v9:
time: 95.5 us; the launch traced here: 95.1 us
  starting transfers between devices  34 us (36%)
  blocking collectives  33 us (35%)
  Pallas kernels  22.7 us (24%)
  waiting for transfers between devices  2.63 us (3%)
  local copies, waits for them, and re-layouts  1.81 us (2%)
    all_to_all x2, blocking collectives, gathered(): lax.all_to_all(jnp.broadcast_to(row, (count, slots)), axes, 0, 0, tiled=T...  33 us
    ppermute x1, starting transfers between devices, shards(): above = lax.ppermute(own[:cy], ZRING, zring_pairs(zs, -1))  9.5 us
    ppermute x1, starting transfers between devices, shards(): sent = lax.ppermute(sent, 'gz_1', swap)  8.89 us
    pallas_call x1, Pallas kernels, first_forces(): pl.pallas_call(functools.partial(own_pass, cap=cap), in_specs=[SMEM] * 4...  6.93 us
    ppermute x1, starting transfers between devices, shards(): traded = lax.ppermute(edges, 'gz_1', swap)  5.1 us
    pallas_call x1, Pallas kernels, other_forces(): pl.pallas_call(functools.partial(other_pass, cap=cap), in_specs=[SMEM, SM...  4.49 us
    ppermute x1, starting transfers between devices, shards(): below = lax.ppermute(own[last:], ZRING, zring_pairs(zs, 1))  4.36 us
    pallas_call x1, Pallas kernels, finish(): pl.pallas_call(functools.partial(last_pass, cap=cap), in_specs=[SMEM] * 3...  4.27 us
  transfers between devices with their start and end apart: 7, of which 3 were waited for; matrix products, arithmetic and copies ran while one was open for 0% of the time, Pallas kernels for 16%

profile of v9, /device:TPU:1, one launch (start us, length us, event | category | flops | bytes accessed | tf_op | source)
XLA Modules:
  0.0 95.1 jit_solution(17703839257265453294)
XLA Ops:
  0.6 0.0 copy-start.2
  0.6 0.0 copy-start.3
  0.7 0.0 copy-start.4
  0.7 1.6 %shard_map.95 = (f32[32,8,128]{2,1,0:T(8,128)}, f32[28,8,128]{2,1,0:T(8,128)}) custom-call(s32[4,1,8]{2,1,0:T(1,128)} %bitcast.15, f32[8,4,1,4,128]{4,3,2,1,0:T(4,128)} %now_ref.1, f32[8,4,3,1,128]{4,3,2,1,0:T(1,128)} %bitcast.20), custom_call_target="tpu_custom_call" | custom-call | tf_op jit(solution)/shard_map/pallas_call | solution.py:450
  2.3 0.0 copy-start
  2.3 0.8 fusion
  3.1 4.4 %collective-permute-start = (f32[4,8,128]{2,1,0:T(8,128)S(1)}, f32[4,8,128]{2,1,0:T(8,128)S(1)}, u32[]{:S(2)}, u32[]{:S(2)}) collective-permute-start(f32[4,8,128]{2,1,0:T(8,128)S(1)} %get-tuple-element.38), channel_id=1, source_target_pairs={{0,64},{64,128},{128,192},{192,256},{256,320},{320,384},{384,448},... | collective-permute-start | bytes 49160 | tf_op jit(solution)/shard_map/ppermute | solution.py:462
  7.5 9.5 %collective-permute-start.1 = (f32[4,8,128]{2,1,0:T(8,128)S(1)}, f32[4,8,128]{2,1,0:T(8,128)S(1)}, u32[]{:S(2)}, u32[]{:S(2)}) collective-permute-start(f32[4,8,128]{2,1,0:T(8,128)S(1)} %get-tuple-element.39), channel_id=1, source_target_pairs={{0,449},{64,0},{128,64},{192,128},{256,192},{320,256},{384,320},{4... | collective-permute-start | bytes 49160 | tf_op jit(solution)/shard_map/ppermute | solution.py:463
  17.0 8.9 %collective-permute-start.3 = (f32[28,8,128]{2,1,0:T(8,128)}, f32[28,8,128]{2,1,0:T(8,128)S(1)}, u32[]{:S(2)}, u32[]{:S(2)}) collective-permute-start(f32[28,8,128]{2,1,0:T(8,128)} %get-tuple-element.24), channel_id=1, source_target_pairs={{0,1},{1,0},{2,3},{3,2},{4,5},{5,4},{6,7},{7,6},{8,9},{9,8},{10,11... | collective-permute-start | bytes 344072 | tf_op jit(solution)/shard_map/ppermute | solution.py:460
  25.9 0.0 collective-permute-done
  25.9 0.0 collective-permute-done.1
  25.9 0.0 copy-start.6
  25.9 0.0 copy-start.1
  25.9 5.1 %collective-permute-start.2 = (f32[8,8,128]{2,1,0:T(8,128)S(1)}, f32[8,8,128]{2,1,0:T(8,128)S(1)}, u32[]{:S(2)}, u32[]{:S(2)}) collective-permute-start(f32[8,8,128]{2,1,0:T(8,128)S(1)} %pad_maximum_fusion.3), channel_id=1, source_target_pairs={{0,1},{1,0},{2,3},{3,2},{4,5},{5,4},{6,7},{7,6},{8,9},{9,8},{10,11... | collective-permute-start | bytes 98312 | tf_op jit(solution)/shard_map/ppermute | solution.py:465
  31.1 0.0 copy-done.2
  31.1 0.0 copy-done.3
  31.1 0.0 copy-done.4
  31.1 0.0 copy-done
  31.1 0.0 copy-done.6
  31.1 0.0 copy-done.1
  31.1 0.0 copy-start.5
  31.1 0.9 copy-done.5
  32.0 6.9 %shard_map.96 = (s32[2144]{0:T(1024)S(1)}, s32[4]{0:T(128)S(1)}, f32[32,8,128]{2,1,0:T(8,128)S(1)}, f32[32,8,128]{2,1,0:T(8,128)S(1)}, s32[32,8,128]{2,1,0:T(8,1...) custom-call(s32[1]{0:T(128)} %bitcast.half_ref, s32[486]{0:T(512)S(1)} %copy-done.6, ...), custom_call_target="tpu_custom_call" | custom-call | flops 734003200 | bytes 1048576 | tf_op jit(solution)/shard_map/pallas_call | solution.py:375
  39.0 2.2 %collective-permute-done.2 = f32[8,8,128]{2,1,0:T(8,128)S(1)} collective-permute-done((f32[8,8,128]{2,1,0:T(8,128)S(1)}, f32[8,8,128]{2,1,0:T(8,128)S(1)}, u32[]{:S(2)}, u32[]{:S(2)}) %collective-permute-start.2) | collective-permute-done | bytes 32800 | tf_op jit(solution)/shard_map/ppermute | solution.py:465
  41.2 0.0 collective-permute-done.3
  41.3 3.1 %collective-permute-start.4 = (f32[40,8,128]{2,1,0:T(8,128)S(1)}, f32[40,8,128]{2,1,0:T(8,128)S(1)}, u32[]{:S(2)}, u32[]{:S(2)}) collective-permute-start(f32[40,8,128]{2,1,0:T(8,128)S(1)} %get-tuple-element.40.other_ref), channel_id=1, source_target_pairs={{0,2},{1,7},{2,4},{3,1},{4,6},{5,3},{6,0},{7,5},{8,10},{9,15},{10,... | collective-permute-start | bytes 491528 | tf_op jit(solution)/shard_map/ppermute | solution.py:475
  44.5 4.5 %shard_map.97 = (f32[32,8,128]{2,1,0:T(8,128)S(1)}, f32[2,10,8,128]{3,2,1,0:T(8,128)S(1)}, f32[2,10,8,128]{3,2,1,0:T(8,128)S(1)}) custom-call(s32[2144]{0:T(1024)S(1)} %get-tuple-element.20.list_ref, s32[4]{0:T(128)S(1)} %get-tuple-element.21.count_ref, f32[27,8,128]{2,1,0:T(8,128)S(1)} %get-tuple-element.22.off_ref, ...), custom_call_target="tpu_custom_call" | custom-call | flops 878182400 | bytes 1048576 | tf_op jit(solution)/shard_map/pallas_call | solution.py:397
  49.0 0.3 collective-permute-done.4.far_ref
  49.3 3.0 %collective-permute-start.5 = (f32[3,10,8,128]{3,2,1,0:T(8,128)S(1)}, f32[3,10,8,128]{3,2,1,0:T(8,128)S(1)}, u32[]{:S(2)}, u32[]{:S(2)}) collective-permute-start(f32[3,10,8,128]{3,2,1,0:T(8,128)S(1)} %pad_maximum_fusion.1), channel_id=1, source_target_pairs={{0,8},{8,16},{16,24},{24,32},{32,40},{40,48},{48,56},{56,0},{1,9},... | collective-permute-start | bytes 368648 | tf_op jit(solution)/shard_map/ppermute | solution.py:478
  52.3 0.0 collective-permute-start.6
  52.3 4.2 %shard_map.98.acc2_ref = f32[32,8,128]{2,1,0:T(8,128)S(1)} custom-call(s32[2144]{0:T(1024)S(1)} %get-tuple-element.20.list_ref, s32[4]{0:T(128)S(1)} %get-tuple-element.21.count_ref, f32[27,8,128]{2,1,0:T(8,128)S(1)} %get-tuple-element.22.off_ref, f32[40,8,128]{2,1,0:T(8,128)S(1)} %pad_maximum_fusion.own_ref, f32[40,8,128]{2,1,0:T(8,128)S(1)} %collective-permute-done.4.far_ref), custom_call_target="tpu_custom_call" | custom-call | flops 878182400 | bytes 1048576 | tf_op jit(solution)/shard_map/pallas_call | solution.py:410
  56.5 0.0 collective-permute-done.5.low_ref
  56.5 0.1 collective-permute-done.6.high_ref
  56.6 4.3 %shard_map.99 = (f32[8,4,3,1,128]{4,3,2,1,0:T(1,128)S(1)}, f32[8,4,1,128]{3,2,1,0:T(1,128)S(1)}, f32[1,128]{1,0:T(1,128)S(1)}) custom-call(s32[1]{0:T(128)} %bitcast.half_ref, s32[2144]{0:T(1024)S(1)} %get-tuple-element.20.list_ref, s32[4]{0:T(128)S(1)} %get-tuple-element.21.count_ref, f32[27,8,128]{2,1,0:T(8,128)S(1)} %get-tuple-element.22.off_ref, ...), custom_call_target="tpu_custom_call" | custom-call | flops 878182400 | bytes 1048576 | tf_op jit(solution)/shard_map/pallas_call | solution.py:424
  60.9 13.1 %all_to_all.14 = f32[32,1,128]{2,1,0:T(1,128)S(1)} all-to-all(f32[32,1,128]{2,1,0:T(1,128)S(1)} %broadcast_in_dim.24), channel_id=1, replica_groups=mesh['gx'=8,'gy_0'=4,'gy_1'=2,'gz_0'=4,'gz_1'=2] {'gz_0','gy_0','gy_1'}, dimensions={0} | all-to-all | bytes 32768 | tf_op jit(solution)/shard_map/all_to_all | solution.py:487
  74.0 19.9 %all_to_all.15 = f32[16,1,128]{2,1,0:T(1,128)S(1)} all-to-all(f32[16,1,128]{2,1,0:T(1,128)S(1)} %broadcast_in_dim.25), channel_id=1, replica_groups=mesh['gx'=8,'gy_0'=4,'gy_1'=2,'gz_0'=4,'gz_1'=2] {'gx','gz_1'}, dimensions={0} | all-to-all | bytes 16384 | tf_op jit(solution)/shard_map/all_to_all | solution.py:487
  93.9 1.2 %shard_map.100 = (f32[8,4,1,128]{3,2,1,0:T(1,128)}, f32[8,4,3,1,128]{4,3,2,1,0:T(1,128)}) custom-call(f32[16,128]{1,0:T(8,128)S(1)} %bitcast.14, f32[8,4,1,128]{3,2,1,0:T(1,128)S(1)} %get-tuple-element.32.sq_ref, f32[8,4,3,1,128]{4,3,2,1,0:T(1,128)S(1)} %get-tuple-element.33.drift_ref), custom_call_target="tpu_custom_call" | custom-call | tf_op jit(solution)/shard_map/pallas_call | solution.py:490
  (15 shorter events, 0.2 us)
Async XLA Ops:
  0.6 30.4 %copy-start.2 = (f32[8,4,1,3,128]{4,2,3,1,0:T(1,128)S(1)}, f32[8,4,1,3,128]{4,2,3,1,0:T(1,128)}, u32[]{:S(2)}) copy-start(f32[8,4,1,3,128]{4,2,3,1,0:T(1,128)} %param.9) | copy-start | bytes 147460
  0.6 30.4 %copy-start.3 = (s32[8,4,1,2,128]{4,3,2,1,0:T(2,128)S(1)}, s32[8,4,1,2,128]{4,3,2,1,0:T(2,128)}, u32[]{:S(2)}) copy-start(s32[8,4,1,2,128]{4,3,2,1,0:T(2,128)} %desc_ref.1) | copy-start | bytes 98308
  0.7 30.4 %copy-start.4 = (s32[8,4,1,14]{3,2,1,0:T(1,128)S(1)}, s32[8,4,1,14]{3,2,1,0:T(1,128)}, u32[]{:S(2)}) copy-start(s32[8,4,1,14]{3,2,1,0:T(1,128)} %nbr_ref.1) | copy-start | bytes 5380
  2.3 28.8 %copy-start = (f32[32,8,128]{2,1,0:T(8,128)S(1)}, f32[32,8,128]{2,1,0:T(8,128)}, u32[]{:S(2)}) copy-start(f32[32,8,128]{2,1,0:T(8,128)} %get-tuple-element.19.own_ref) | copy-start | bytes 393220
  3.1 22.8 %collective-permute-start = (f32[4,8,128]{2,1,0:T(8,128)S(1)}, f32[4,8,128]{2,1,0:T(8,128)S(1)}, u32[]{:S(2)}, u32[]{:S(2)}) collective-permute-start(f32[4,8,128]{2,1,0:T(8,128)S(1)} %get-tuple-element.38), channel_id=1, source_target_pairs={{0,64},{64,128},{128,192},{192,256},{256,320},{320,384},{384,448},... | collective-permute-start | bytes 49160 | tf_op jit(solution)/shard_map/ppermute | solution.py:462
  7.5 18.4 %collective-permute-start.1 = (f32[4,8,128]{2,1,0:T(8,128)S(1)}, f32[4,8,128]{2,1,0:T(8,128)S(1)}, u32[]{:S(2)}, u32[]{:S(2)}) collective-permute-start(f32[4,8,128]{2,1,0:T(8,128)S(1)} %get-tuple-element.39), channel_id=1, source_target_pairs={{0,449},{64,0},{128,64},{192,128},{256,192},{320,256},{384,320},{4... | collective-permute-start | bytes 49160 | tf_op jit(solution)/shard_map/ppermute | solution.py:463
  17.0 24.2 %collective-permute-start.3 = (f32[28,8,128]{2,1,0:T(8,128)}, f32[28,8,128]{2,1,0:T(8,128)S(1)}, u32[]{:S(2)}, u32[]{:S(2)}) collective-permute-start(f32[28,8,128]{2,1,0:T(8,128)} %get-tuple-element.24), channel_id=1, source_target_pairs={{0,1},{1,0},{2,3},{3,2},{4,5},{5,4},{6,7},{7,6},{8,9},{9,8},{10,11... | collective-permute-start | bytes 344072 | tf_op jit(solution)/shard_map/ppermute | solution.py:460
  25.9 5.2 %copy-start.6 = (s32[486]{0:T(512)S(1)}, s32[486]{0:T(512)}, u32[]{:S(2)}) copy-start(s32[486]{0:T(512)} %constant.21.clone.table_ref) | copy-start | bytes 5836
  25.9 5.2 %copy-start.1 = (s32[8,4,1]{0,2,1:T(1,128)S(1)}, s32[8,4,1]{0,2,1:T(1,128)}, u32[]{:S(2)}) copy-start(s32[8,4,1]{0,2,1:T(1,128)} %param.11) | copy-start | bytes 388
  25.9 15.2 %collective-permute-start.2 = (f32[8,8,128]{2,1,0:T(8,128)S(1)}, f32[8,8,128]{2,1,0:T(8,128)S(1)}, u32[]{:S(2)}, u32[]{:S(2)}) collective-permute-start(f32[8,8,128]{2,1,0:T(8,128)S(1)} %pad_maximum_fusion.3), channel_id=1, source_target_pairs={{0,1},{1,0},{2,3},{3,2},{4,5},{5,4},{6,7},{7,6},{8,9},{9,8},{10,11... | collective-permute-start | bytes 98312 | tf_op jit(solution)/shard_map/ppermute | solution.py:465
  31.1 0.9 copy-start.5
  41.3 7.9 %collective-permute-start.4 = (f32[40,8,128]{2,1,0:T(8,128)S(1)}, f32[40,8,128]{2,1,0:T(8,128)S(1)}, u32[]{:S(2)}, u32[]{:S(2)}) collective-permute-start(f32[40,8,128]{2,1,0:T(8,128)S(1)} %get-tuple-element.40.other_ref), channel_id=1, source_target_pairs={{0,2},{1,7},{2,4},{3,1},{4,6},{5,3},{6,0},{7,5},{8,10},{9,15},{10,... | collective-permute-start | bytes 491528 | tf_op jit(solution)/shard_map/ppermute | solution.py:475
  49.3 7.2 %collective-permute-start.5 = (f32[3,10,8,128]{3,2,1,0:T(8,128)S(1)}, f32[3,10,8,128]{3,2,1,0:T(8,128)S(1)}, u32[]{:S(2)}, u32[]{:S(2)}) collective-permute-start(f32[3,10,8,128]{3,2,1,0:T(8,128)S(1)} %pad_maximum_fusion.1), channel_id=1, source_target_pairs={{0,8},{8,16},{16,24},{24,32},{32,40},{40,48},{48,56},{56,0},{1,9},... | collective-permute-start | bytes 368648 | tf_op jit(solution)/shard_map/ppermute | solution.py:478
  52.3 4.3 %collective-permute-start.6 = (f32[3,10,8,128]{3,2,1,0:T(8,128)S(1)}, f32[3,10,8,128]{3,2,1,0:T(8,128)S(1)}, u32[]{:S(2)}, u32[]{:S(2)}) collective-permute-start(f32[3,10,8,128]{3,2,1,0:T(8,128)S(1)} %pad_maximum_fusion.2), channel_id=1, source_target_pairs={{0,56},{8,0},{16,8},{24,16},{32,24},{40,32},{48,40},{56,48},{1,57}... | collective-permute-start | bytes 368648 | tf_op jit(solution)/shard_map/ppermute | solution.py:479

commit v10 on v8

--- a/solution.py
+++ b/solution.py
@@ -249,9 +249,9 @@
     half_ref, list_ref, count_ref, off_ref, own_ref, other_ref, far_ref, low_ref, high_ref,
     acc0_ref, acc1_ref, acc2_ref, base_ref, link_ref,
     drift_ref, sq_ref, part_ref,
-    acc_ref, st_ref, mc_ref, cube_ref, *, cap
+    acc_ref, st_ref, mc_ref, cube_ref, out_ref, sems, *, cap
 ):
-    cx, cy = drift_ref.shape[:2]
+    cx, cy = out_ref.shape[:2]
     px = cx + 2
     half = half_ref[0]
     lane = lax.broadcasted_iota(I32, (1, 128), 1)
@@ -309,7 +309,7 @@
         found = (level[4:7] + sides[4:7]) + sides[:3]
         error = base_ref[cell, :3] + found - HALF_KICK * acc_ref[cell, :3]
         alive = base_ref[cell, 3:4]
-        drift_ref[x, y, :, 0] = jnp.where(alive > 0.0, error, 0.0)
+        out_ref[x, y, :, 0] = jnp.where(alive > 0.0, error, 0.0)
         squared = jnp.where(alive > 0.0, jnp.sum(error * error, axis=0, keepdims=True), 0.0)
         sq_ref[x, y] = squared
         return squared, alive
@@ -320,6 +320,7 @@
             squared, alive = one_cell(x, y)
             total = total + squared
             live = live + alive
+        pltpu.make_async_copy(out_ref.at[x], drift_ref.at[x], sems.at[x]).start()
         return total, live
 
     zero = jnp.zeros((1, 128), F32)
@@ -329,11 +330,11 @@
         return v + pltpu.roll(jnp.broadcast_to(v, (8, 128)), 64, 1)[:1]
 
     part_ref[...] = jnp.where(lane < 64, folded(total), folded(live))
-
-
-def scaled(rows_ref, sq_ref, drift_ref, tension_ref, out_ref, sem):
-    copy = pltpu.make_async_copy(drift_ref, out_ref, sem)
-    copy.start()
+    for x in range(cx):
+        pltpu.make_async_copy(out_ref.at[x], drift_ref.at[x], sems.at[x]).wait()
+
+
+def scaled(rows_ref, sq_ref, tension_ref):
     lane = lax.broadcasted_iota(I32, (1, 128), 1)
     sums = jnp.sum(rows_ref[...], axis=0, keepdims=True)
     total = jnp.sum(jnp.where(lane < 64, sums, 0.0), axis=1, keepdims=True)
@@ -342,7 +343,6 @@
     for x in range(sq_ref.shape[0]):
         for y in range(sq_ref.shape[1]):
             tension_ref[x, y] = sq_ref[x, y] / bound
-    copy.wait()
 
 
 SMEM = pl.BlockSpec(memory_space=pltpu.SMEM)
@@ -424,7 +424,7 @@
     return pl.pallas_call(
         functools.partial(last_pass, cap=cap),
         in_specs=[SMEM] * 3 + [VMEM] * 11,
-        out_specs=[VMEM, VMEM, VMEM],
+        out_specs=[pl.BlockSpec(memory_space=pl.ANY), VMEM, VMEM],
         out_shape=[
             jax.ShapeDtypeStruct((cx, cy, 3, 1, 128), F32),
             jax.ShapeDtypeStruct((cx, cy, 1, 128), F32),
@@ -432,7 +432,11 @@
         ],
         scratch_shapes=[pltpu.VMEM((cx * cy, 8, 128), F32)]
         + features_of(6 * px)
-        + [pltpu.VMEM((3, px, cy + 2, 8, 128), F32)],
+        + [
+            pltpu.VMEM((3, px, cy + 2, 8, 128), F32),
+            pltpu.VMEM((cx, cy, 3, 1, 128), F32),
+            pltpu.SemaphoreType.DMA((cx,)),
+        ],
         cost_estimate=cost(cap // 4),
         compiler_params=params(),
     )(half, lists, counts, offsets, *planes, low, high, *sums, base, links)
@@ -491,17 +495,13 @@
         return lax.all_to_all(jnp.broadcast_to(row, (count, slots)), axes, 0, 0, tiled=True)
 
     sums = jnp.sum(gathered(part, XYC), axis=0, keepdims=True)
-    tension, drift = pl.pallas_call(
+    tension = pl.pallas_call(
         scaled,
-        in_specs=[VMEM, VMEM, VMEM],
-        out_specs=[VMEM, pl.BlockSpec(memory_space=pl.ANY)],
-        out_shape=[
-            jax.ShapeDtypeStruct((cx, cy, cz, slots), F32),
-            jax.ShapeDtypeStruct(drift.shape, F32),
-        ],
-        scratch_shapes=[pltpu.SemaphoreType.DMA],
+        in_specs=[VMEM, VMEM],
+        out_specs=VMEM,
+        out_shape=jax.ShapeDtypeStruct((cx, cy, cz, slots), F32),
         compiler_params=small_params(),
-    )(gathered(sums, ZRING), squared, drift)
+    )(gathered(sums, ZRING), squared)
     return jnp.transpose(drift, (0, 1, 3, 2, 4)), tension
 
 

time: 94.9 us -> 95 us (level)
  Pallas kernels: 22.7 us -> 23.8 us
  starting transfers between devices: 31.9 us -> 30.9 us
    ppermute x1, starting transfers between devices: 5.96 us -> 4.99 us  [shards(): above = lax.ppermute(both(0), ZRING, zring_pairs(zs, -1))]
    pallas_call x1, Pallas kernels: 6.93 us -> 7.89 us  [first_forces(): pl.pallas_call(functools.partial(own_pass, cap=cap), in_specs=[SMEM] * 4...]
  transfers between devices with their start and end apart: 6 -> 6, of which waited for: 2 -> 2; matrix products, arithmetic and copies ran while one was open for 0% -> 0% of each run, Pallas kernels for 16% -> 17%
where the time goes in v10:
time: 95 us; the launch traced here: 94.6 us
  blocking collectives  31.7 us (33%)
  starting transfers between devices  30.9 us (33%)
  Pallas kernels  23.8 us (25%)
  waiting for transfers between devices  4.65 us (5%)
  local copies, waits for them, and re-layouts  2.56 us (3%)
    all_to_all x2, blocking collectives, gathered(): lax.all_to_all(jnp.broadcast_to(row, (count, slots)), axes, 0, 0, tiled=T...  31.7 us
    ppermute x1, starting transfers between devices, shards(): sent = lax.ppermute(sent, 'gz_1', [(0, 1), (1, 0)])  16.4 us
    pallas_call x1, Pallas kernels, first_forces(): pl.pallas_call(functools.partial(own_pass, cap=cap), in_specs=[SMEM] * 4...  7.89 us
    ppermute x1, starting transfers between devices, shards(): above = lax.ppermute(both(0), ZRING, zring_pairs(zs, -1))  4.99 us
    pallas_call x1, Pallas kernels, finish(): pl.pallas_call(functools.partial(last_pass, cap=cap), in_specs=[SMEM] * 3...  4.86 us
    ppermute x1, waiting for transfers between devices, shards(): below = lax.ppermute(both(cx * cy - cy), ZRING, zring_pairs(zs, 1))  4.53 us
    pallas_call x1, Pallas kernels, other_forces(): pl.pallas_call(functools.partial(other_pass, cap=cap), in_specs=[SMEM, SM...  4.49 us
    ppermute x1, starting transfers between devices, shards(): lax.ppermute(jnp.concatenate([top, rows[None, :, 8 * cy - 8:]]), GY, ring...  4.47 us
  transfers between devices with their start and end apart: 6, of which 2 were waited for; matrix products, arithmetic and copies ran while one was open for 0% of the time, Pallas kernels for 17%

profile of v10, /device:TPU:1, one launch (start us, length us, event | category | flops | bytes accessed | tf_op | source)
XLA Modules:
  0.0 94.6 jit_solution(13355260666784097853)
XLA Ops:
  0.6 0.0 copy-start.2
  0.6 0.0 copy-start.3
  0.7 0.0 copy-start.6
  0.7 1.6 %shard_map.95 = (f32[32,8,128]{2,1,0:T(8,128)}, f32[28,8,128]{2,1,0:T(8,128)}) custom-call(s32[4,1,8]{2,1,0:T(1,128)} %bitcast.31, f32[8,4,1,4,128]{4,3,2,1,0:T(4,128)} %now_ref.1, f32[8,4,3,1,128]{4,3,2,1,0:T(1,128)} %bitcast.36), custom_call_target="tpu_custom_call" | custom-call | tf_op jit(solution)/shard_map/pallas_call | solution.py:454
  2.3 0.0 copy-start.4
  2.3 16.4 %collective-permute-start = (f32[28,8,128]{2,1,0:T(8,128)}, f32[28,8,128]{2,1,0:T(8,128)S(1)}, u32[]{:S(2)}, u32[]{:S(2)}) collective-permute-start(f32[28,8,128]{2,1,0:T(8,128)} %get-tuple-element.22), channel_id=1, source_target_pairs={{0,1},{1,0},{2,3},{3,2},{4,5},{5,4},{6,7},{7,6},{8,9},{9,8},{10,11... | collective-permute-start | bytes 344072 | tf_op jit(solution)/shard_map/ppermute | solution.py:463
  18.7 0.0 copy-start
  18.7 0.0 copy-done.2
  18.7 0.0 copy-done.3
  18.7 0.0 copy-done.6
  18.8 0.0 copy-done.4
  18.8 0.6 copy-done
  19.4 0.0 copy-start.1
  19.4 0.9 copy-done.1
  20.3 0.0 copy-start.5
  20.3 0.9 copy-done.5
  21.2 7.9 %shard_map.96 = (s32[2144]{0:T(1024)S(1)}, s32[4]{0:T(128)S(1)}, f32[32,8,128]{2,1,0:T(8,128)S(1)}, f32[32,8,128]{2,1,0:T(8,128)S(1)}, s32[32,8,128]{2,1,0:T(8,1...) custom-call(s32[1]{0:T(128)} %bitcast.half_ref, s32[486]{0:T(512)S(1)} %copy-done.6, ...), custom_call_target="tpu_custom_call" | custom-call | flops 734003200 | bytes 1048576 | tf_op jit(solution)/shard_map/pallas_call | solution.py:375
  29.1 0.0 collective-permute-done
  29.2 5.0 %collective-permute-start.2 = (f32[2,4,8,128]{3,2,1,0:T(8,128)S(1)}, f32[2,4,8,128]{3,2,1,0:T(8,128)S(1)}, u32[]{:S(2)}, u32[]{:S(2)}) collective-permute-start(f32[2,4,8,128]{3,2,1,0:T(8,128)S(1)} %maximum_select_fusion.1), channel_id=1, source_target_pairs={{0,449},{64,0},{128,64},{192,128},{256,192},{320,256},{384,320},{4... | collective-permute-start | bytes 98312 | tf_op jit(solution)/shard_map/ppermute | solution.py:475
  34.2 1.9 %collective-permute-start.1 = (f32[2,4,8,128]{3,2,1,0:T(8,128)S(1)}, f32[2,4,8,128]{3,2,1,0:T(8,128)S(1)}, u32[]{:S(2)}, u32[]{:S(2)}) collective-permute-start(f32[2,4,8,128]{3,2,1,0:T(8,128)S(1)} %maximum_select_fusion), channel_id=1, source_target_pairs={{0,64},{64,128},{128,192},{192,256},{256,320},{320,384},{384,448},... | collective-permute-start | bytes 98312 | tf_op jit(solution)/shard_map/ppermute | solution.py:474
  36.2 4.5 %collective-permute-done.1 = f32[2,4,8,128]{3,2,1,0:T(8,128)S(1)} collective-permute-done((f32[2,4,8,128]{3,2,1,0:T(8,128)S(1)}, f32[2,4,8,128]{3,2,1,0:T(8,128)S(1)}, u32[]{:S(2)}, u32[]{:S(2)}) %collective-permute-start.1) | collective-permute-done | bytes 32800 | tf_op jit(solution)/shard_map/ppermute | solution.py:474
  40.7 0.0 collective-permute-done.2
  40.8 3.1 %collective-permute-start.3 = (f32[40,8,128]{2,1,0:T(8,128)S(1)}, f32[40,8,128]{2,1,0:T(8,128)S(1)}, u32[]{:S(2)}, u32[]{:S(2)}) collective-permute-start(f32[40,8,128]{2,1,0:T(8,128)S(1)} %bitcast_dynamic-update-slice_fusion.other_ref), channel_id=1, source_target_pairs={{0,2},{1,7},{2,4},{3,1},{4,6},{5,3},{6,0},{7,5},{8,10},{9,15},{10,... | collective-permute-start | bytes 491528 | tf_op jit(solution)/shard_map/ppermute | solution.py:483
  43.9 4.5 %shard_map.97 = (f32[32,8,128]{2,1,0:T(8,128)S(1)}, f32[2,10,8,128]{3,2,1,0:T(8,128)S(1)}, f32[2,10,8,128]{3,2,1,0:T(8,128)S(1)}) custom-call(s32[2144]{0:T(1024)S(1)} %get-tuple-element.18.list_ref, s32[4]{0:T(128)S(1)} %get-tuple-element.19.count_ref, f32[27,8,128]{2,1,0:T(8,128)S(1)} %get-tuple-element.20.off_ref, ...), custom_call_target="tpu_custom_call" | custom-call | flops 878182400 | bytes 1048576 | tf_op jit(solution)/shard_map/pallas_call | solution.py:397
  48.4 0.0 collective-permute-done.3.far_ref
  48.5 4.5 %collective-permute-start.4 = (f32[3,10,8,128]{3,2,1,0:T(8,128)S(1)}, f32[3,10,8,128]{3,2,1,0:T(8,128)S(1)}, u32[]{:S(2)}, u32[]{:S(2)}) collective-permute-start(f32[3,10,8,128]{3,2,1,0:T(8,128)S(1)} %pad_maximum_fusion.1), channel_id=1, source_target_pairs={{0,8},{8,16},{16,24},{24,32},{32,40},{40,48},{48,56},{56,0},{1,9},... | collective-permute-start | bytes 368648 | tf_op jit(solution)/shard_map/ppermute | solution.py:486
  53.0 0.0 collective-permute-start.5
  53.0 4.2 %shard_map.98.acc2_ref = f32[32,8,128]{2,1,0:T(8,128)S(1)} custom-call(s32[2144]{0:T(1024)S(1)} %get-tuple-element.18.list_ref, s32[4]{0:T(128)S(1)} %get-tuple-element.19.count_ref, f32[27,8,128]{2,1,0:T(8,128)S(1)} %get-tuple-element.20.off_ref, f32[40,8,128]{2,1,0:T(8,128)S(1)} %pad_maximum_fusion.own_ref, f32[40,8,128]{2,1,0:T(8,128)S(1)} %collective-permute-done.3.far_ref), custom_call_target="tpu_custom_call" | custom-call | flops 878182400 | bytes 1048576 | tf_op jit(solution)/shard_map/pallas_call | solution.py:410
  57.1 0.0 collective-permute-done.4.low_ref
  57.2 0.1 collective-permute-done.5.high_ref
  57.3 4.9 %shard_map.99 = (f32[8,4,3,1,128]{4,3,2,1,0:T(1,128)}, f32[8,4,1,128]{3,2,1,0:T(1,128)S(1)}, f32[1,128]{1,0:T(1,128)S(1)}) custom-call(s32[1]{0:T(128)} %bitcast.half_ref, s32[2144]{0:T(1024)S(1)} %get-tuple-element.18.list_ref, s32[4]{0:T(128)S(1)} %get-tuple-element.19.count_ref, f32[27,8,128]{2,1,0:T(8,128)S(1)} %get-tuple-element.20.off_ref, ...), custom_call_target="tpu_custom_call" | custom-call | flops 878182400 | bytes 1048576 | tf_op jit(solution)/shard_map/pallas_call | solution.py:424
  62.2 13.5 %all_to_all.14 = f32[32,1,128]{2,1,0:T(1,128)S(1)} all-to-all(f32[32,1,128]{2,1,0:T(1,128)S(1)} %broadcast_in_dim.24), channel_id=1, replica_groups=mesh['gx'=8,'gy_0'=4,'gy_1'=2,'gz_0'=4,'gz_1'=2] {'gz_0','gy_0','gy_1'}, dimensions={0} | all-to-all | bytes 32768 | tf_op jit(solution)/shard_map/all_to_all | solution.py:495
  75.7 18.1 %all_to_all.15 = f32[16,1,128]{2,1,0:T(1,128)S(1)} all-to-all(f32[16,1,128]{2,1,0:T(1,128)S(1)} %broadcast_in_dim.25), channel_id=1, replica_groups=mesh['gx'=8,'gy_0'=4,'gy_1'=2,'gz_0'=4,'gz_1'=2] {'gx','gz_1'}, dimensions={0} | all-to-all | bytes 16384 | tf_op jit(solution)/shard_map/all_to_all | solution.py:495
  93.9 0.7 shard_map.100
  (20 shorter events, 0.2 us)
Async XLA Ops:
  0.6 18.1 %copy-start.2 = (f32[8,4,1,3,128]{4,2,3,1,0:T(1,128)S(1)}, f32[8,4,1,3,128]{4,2,3,1,0:T(1,128)}, u32[]{:S(2)}) copy-start(f32[8,4,1,3,128]{4,2,3,1,0:T(1,128)} %param.9) | copy-start | bytes 147460
  0.6 18.1 %copy-start.3 = (s32[8,4,1,2,128]{4,3,2,1,0:T(2,128)S(1)}, s32[8,4,1,2,128]{4,3,2,1,0:T(2,128)}, u32[]{:S(2)}) copy-start(s32[8,4,1,2,128]{4,3,2,1,0:T(2,128)} %desc_ref.1) | copy-start | bytes 98308
  0.7 18.1 %copy-start.6 = (s32[486]{0:T(512)S(1)}, s32[486]{0:T(512)}, u32[]{:S(2)}) copy-start(s32[486]{0:T(512)} %constant.15.clone.table_ref) | copy-start | bytes 5836
  2.3 16.5 %copy-start.4 = (s32[8,4,1,14]{3,2,1,0:T(1,128)S(1)}, s32[8,4,1,14]{3,2,1,0:T(1,128)}, u32[]{:S(2)}) copy-start(s32[8,4,1,14]{3,2,1,0:T(1,128)} %nbr_ref.1) | copy-start | bytes 5380
  2.3 26.8 %collective-permute-start = (f32[28,8,128]{2,1,0:T(8,128)}, f32[28,8,128]{2,1,0:T(8,128)S(1)}, u32[]{:S(2)}, u32[]{:S(2)}) collective-permute-start(f32[28,8,128]{2,1,0:T(8,128)} %get-tuple-element.22), channel_id=1, source_target_pairs={{0,1},{1,0},{2,3},{3,2},{4,5},{5,4},{6,7},{7,6},{8,9},{9,8},{10,11... | collective-permute-start | bytes 344072 | tf_op jit(solution)/shard_map/ppermute | solution.py:463
  18.7 0.7 copy-start
  19.4 0.9 copy-start.1
  20.3 0.9 copy-start.5
  29.2 11.6 %collective-permute-start.2 = (f32[2,4,8,128]{3,2,1,0:T(8,128)S(1)}, f32[2,4,8,128]{3,2,1,0:T(8,128)S(1)}, u32[]{:S(2)}, u32[]{:S(2)}) collective-permute-start(f32[2,4,8,128]{3,2,1,0:T(8,128)S(1)} %maximum_select_fusion.1), channel_id=1, source_target_pairs={{0,449},{64,0},{128,64},{192,128},{256,192},{320,256},{384,320},{4... | collective-permute-start | bytes 98312 | tf_op jit(solution)/shard_map/ppermute | solution.py:475
  34.2 6.5 %collective-permute-start.1 = (f32[2,4,8,128]{3,2,1,0:T(8,128)S(1)}, f32[2,4,8,128]{3,2,1,0:T(8,128)S(1)}, u32[]{:S(2)}, u32[]{:S(2)}) collective-permute-start(f32[2,4,8,128]{3,2,1,0:T(8,128)S(1)} %maximum_select_fusion), channel_id=1, source_target_pairs={{0,64},{64,128},{128,192},{192,256},{256,320},{320,384},{384,448},... | collective-permute-start | bytes 98312 | tf_op jit(solution)/shard_map/ppermute | solution.py:474
  40.8 7.7 %collective-permute-start.3 = (f32[40,8,128]{2,1,0:T(8,128)S(1)}, f32[40,8,128]{2,1,0:T(8,128)S(1)}, u32[]{:S(2)}, u32[]{:S(2)}) collective-permute-start(f32[40,8,128]{2,1,0:T(8,128)S(1)} %bitcast_dynamic-update-slice_fusion.other_ref), channel_id=1, source_target_pairs={{0,2},{1,7},{2,4},{3,1},{4,6},{5,3},{6,0},{7,5},{8,10},{9,15},{10,... | collective-permute-start | bytes 491528 | tf_op jit(solution)/shard_map/ppermute | solution.py:483
  48.5 8.7 %collective-permute-start.4 = (f32[3,10,8,128]{3,2,1,0:T(8,128)S(1)}, f32[3,10,8,128]{3,2,1,0:T(8,128)S(1)}, u32[]{:S(2)}, u32[]{:S(2)}) collective-permute-start(f32[3,10,8,128]{3,2,1,0:T(8,128)S(1)} %pad_maximum_fusion.1), channel_id=1, source_target_pairs={{0,8},{8,16},{16,24},{24,32},{32,40},{40,48},{48,56},{56,0},{1,9},... | collective-permute-start | bytes 368648 | tf_op jit(solution)/shard_map/ppermute | solution.py:486
  53.0 4.3 %collective-permute-start.5 = (f32[3,10,8,128]{3,2,1,0:T(8,128)S(1)}, f32[3,10,8,128]{3,2,1,0:T(8,128)S(1)}, u32[]{:S(2)}, u32[]{:S(2)}) collective-permute-start(f32[3,10,8,128]{3,2,1,0:T(8,128)S(1)} %pad_maximum_fusion.2), channel_id=1, source_target_pairs={{0,56},{8,0},{16,8},{24,16},{32,24},{40,32},{48,40},{56,48},{1,57}... | collective-permute-start | bytes 368648 | tf_op jit(solution)/shard_map/ppermute | solution.py:487

commit v11 on v10

--- a/solution.py
+++ b/solution.py
@@ -13,7 +13,8 @@
 GY = ("gy_0", "gy_1")
 GZ = ("gz_0", "gz_1")
 ZRING = ("gx", "gz_1")
-XYC = ("gz_0", "gy_0", "gy_1")
+XY = ("gz_0", "gy_0")
+ZC = ("gx", "gz_1", "gy_1")
 
 EPS_SQ = 0.01
 STEP_DT = 0.3
@@ -494,14 +495,14 @@
         count = lax.axis_size(axes)
         return lax.all_to_all(jnp.broadcast_to(row, (count, slots)), axes, 0, 0, tiled=True)
 
-    sums = jnp.sum(gathered(part, XYC), axis=0, keepdims=True)
+    sums = jnp.sum(gathered(part, XY), axis=0, keepdims=True)
     tension = pl.pallas_call(
         scaled,
         in_specs=[VMEM, VMEM],
         out_specs=VMEM,
         out_shape=jax.ShapeDtypeStruct((cx, cy, cz, slots), F32),
         compiler_params=small_params(),
-    )(gathered(sums, ZRING), squared)
+    )(gathered(sums, ZC), squared)
     return jnp.transpose(drift, (0, 1, 3, 2, 4)), tension
 
 

time: 95 us -> 96.4 us (1.015)
  blocking collectives: 31.7 us -> 33.1 us
    all_to_all x2, blocking collectives: 31.7 us -> 33.1 us  [gathered(): lax.all_to_all(jnp.broadcast_to(row, (count, slots)), axes, 0, 0, tiled=T...]
where the time goes in v11:
time: 96.4 us; the launch traced here: 96 us
  blocking collectives  33.1 us (34%)
  starting transfers between devices  30.9 us (32%)
  Pallas kernels  23.8 us (25%)
  waiting for transfers between devices  4.65 us (5%)
  local copies, waits for them, and re-layouts  2.56 us (3%)
    all_to_all x2, blocking collectives, gathered(): lax.all_to_all(jnp.broadcast_to(row, (count, slots)), axes, 0, 0, tiled=T...  33.1 us
    ppermute x1, starting transfers between devices, shards(): sent = lax.ppermute(sent, 'gz_1', [(0, 1), (1, 0)])  16.4 us
    pallas_call x1, Pallas kernels, first_forces(): pl.pallas_call(functools.partial(own_pass, cap=cap), in_specs=[SMEM] * 4...  7.9 us
    ppermute x1, starting transfers between devices, shards(): above = lax.ppermute(both(0), ZRING, zring_pairs(zs, -1))  4.99 us
    pallas_call x1, Pallas kernels, finish(): pl.pallas_call(functools.partial(last_pass, cap=cap), in_specs=[SMEM] * 3...  4.86 us
    ppermute x1, waiting for transfers between devices, shards(): below = lax.ppermute(both(cx * cy - cy), ZRING, zring_pairs(zs, 1))  4.53 us
    pallas_call x1, Pallas kernels, other_forces(): pl.pallas_call(functools.partial(other_pass, cap=cap), in_specs=[SMEM, SM...  4.49 us
    ppermute x1, starting transfers between devices, shards(): lax.ppermute(jnp.concatenate([top, rows[None, :, 8 * cy - 8:]]), GY, ring...  4.47 us
  transfers between devices with their start and end apart: 6, of which 2 were waited for; matrix products, arithmetic and copies ran while one was open for 0% of the time, Pallas kernels for 17%

profile of v11, /device:TPU:1, one launch (start us, length us, event | category | flops | bytes accessed | tf_op | source)
XLA Modules:
  0.0 96.0 jit_solution(11648357637924779339)
XLA Ops:
  0.6 0.0 copy-start.2
  0.6 0.0 copy-start.3
  0.7 0.0 copy-start.6
  0.7 1.6 %shard_map.95 = (f32[32,8,128]{2,1,0:T(8,128)}, f32[28,8,128]{2,1,0:T(8,128)}) custom-call(s32[4,1,8]{2,1,0:T(1,128)} %bitcast.31, f32[8,4,1,4,128]{4,3,2,1,0:T(4,128)} %now_ref.1, f32[8,4,3,1,128]{4,3,2,1,0:T(1,128)} %bitcast.35), custom_call_target="tpu_custom_call" | custom-call | tf_op jit(solution)/shard_map/pallas_call | solution.py:455
  2.3 0.0 copy-start.4
  2.3 16.4 %collective-permute-start = (f32[28,8,128]{2,1,0:T(8,128)}, f32[28,8,128]{2,1,0:T(8,128)S(1)}, u32[]{:S(2)}, u32[]{:S(2)}) collective-permute-start(f32[28,8,128]{2,1,0:T(8,128)} %get-tuple-element.22), channel_id=1, source_target_pairs={{0,1},{1,0},{2,3},{3,2},{4,5},{5,4},{6,7},{7,6},{8,9},{9,8},{10,11... | collective-permute-start | bytes 344072 | tf_op jit(solution)/shard_map/ppermute | solution.py:464
  18.7 0.0 copy-start
  18.7 0.0 copy-done.2
  18.7 0.0 copy-done.3
  18.7 0.0 copy-done.6
  18.8 0.0 copy-done.4
  18.8 0.6 copy-done
  19.4 0.0 copy-start.1
  19.4 0.9 copy-done.1
  20.3 0.0 copy-start.5
  20.3 0.9 copy-done.5
  21.2 7.9 %shard_map.96 = (s32[2144]{0:T(1024)S(1)}, s32[4]{0:T(128)S(1)}, f32[32,8,128]{2,1,0:T(8,128)S(1)}, f32[32,8,128]{2,1,0:T(8,128)S(1)}, s32[32,8,128]{2,1,0:T(8,1...) custom-call(s32[1]{0:T(128)} %bitcast.half_ref, s32[486]{0:T(512)S(1)} %copy-done.6, ...), custom_call_target="tpu_custom_call" | custom-call | flops 734003200 | bytes 1048576 | tf_op jit(solution)/shard_map/pallas_call | solution.py:376
  29.1 0.0 collective-permute-done
  29.2 5.0 %collective-permute-start.2 = (f32[2,4,8,128]{3,2,1,0:T(8,128)S(1)}, f32[2,4,8,128]{3,2,1,0:T(8,128)S(1)}, u32[]{:S(2)}, u32[]{:S(2)}) collective-permute-start(f32[2,4,8,128]{3,2,1,0:T(8,128)S(1)} %maximum_select_fusion.1), channel_id=1, source_target_pairs={{0,449},{64,0},{128,64},{192,128},{256,192},{320,256},{384,320},{4... | collective-permute-start | bytes 98312 | tf_op jit(solution)/shard_map/ppermute | solution.py:476
  34.2 1.9 %collective-permute-start.1 = (f32[2,4,8,128]{3,2,1,0:T(8,128)S(1)}, f32[2,4,8,128]{3,2,1,0:T(8,128)S(1)}, u32[]{:S(2)}, u32[]{:S(2)}) collective-permute-start(f32[2,4,8,128]{3,2,1,0:T(8,128)S(1)} %maximum_select_fusion), channel_id=1, source_target_pairs={{0,64},{64,128},{128,192},{192,256},{256,320},{320,384},{384,448},... | collective-permute-start | bytes 98312 | tf_op jit(solution)/shard_map/ppermute | solution.py:475
  36.2 4.5 %collective-permute-done.1 = f32[2,4,8,128]{3,2,1,0:T(8,128)S(1)} collective-permute-done((f32[2,4,8,128]{3,2,1,0:T(8,128)S(1)}, f32[2,4,8,128]{3,2,1,0:T(8,128)S(1)}, u32[]{:S(2)}, u32[]{:S(2)}) %collective-permute-start.1) | collective-permute-done | bytes 32800 | tf_op jit(solution)/shard_map/ppermute | solution.py:475
  40.7 0.0 collective-permute-done.2
  40.8 3.1 %collective-permute-start.3 = (f32[40,8,128]{2,1,0:T(8,128)S(1)}, f32[40,8,128]{2,1,0:T(8,128)S(1)}, u32[]{:S(2)}, u32[]{:S(2)}) collective-permute-start(f32[40,8,128]{2,1,0:T(8,128)S(1)} %bitcast_dynamic-update-slice_fusion.other_ref), channel_id=1, source_target_pairs={{0,2},{1,7},{2,4},{3,1},{4,6},{5,3},{6,0},{7,5},{8,10},{9,15},{10,... | collective-permute-start | bytes 491528 | tf_op jit(solution)/shard_map/ppermute | solution.py:484
  43.9 4.5 %shard_map.97 = (f32[32,8,128]{2,1,0:T(8,128)S(1)}, f32[2,10,8,128]{3,2,1,0:T(8,128)S(1)}, f32[2,10,8,128]{3,2,1,0:T(8,128)S(1)}) custom-call(s32[2144]{0:T(1024)S(1)} %get-tuple-element.18.list_ref, s32[4]{0:T(128)S(1)} %get-tuple-element.19.count_ref, f32[27,8,128]{2,1,0:T(8,128)S(1)} %get-tuple-element.20.off_ref, ...), custom_call_target="tpu_custom_call" | custom-call | flops 878182400 | bytes 1048576 | tf_op jit(solution)/shard_map/pallas_call | solution.py:398
  48.4 0.0 collective-permute-done.3.far_ref
  48.5 4.5 %collective-permute-start.4 = (f32[3,10,8,128]{3,2,1,0:T(8,128)S(1)}, f32[3,10,8,128]{3,2,1,0:T(8,128)S(1)}, u32[]{:S(2)}, u32[]{:S(2)}) collective-permute-start(f32[3,10,8,128]{3,2,1,0:T(8,128)S(1)} %pad_maximum_fusion.1), channel_id=1, source_target_pairs={{0,8},{8,16},{16,24},{24,32},{32,40},{40,48},{48,56},{56,0},{1,9},... | collective-permute-start | bytes 368648 | tf_op jit(solution)/shard_map/ppermute | solution.py:487
  53.0 0.0 collective-permute-start.5
  53.0 4.2 %shard_map.98.acc2_ref = f32[32,8,128]{2,1,0:T(8,128)S(1)} custom-call(s32[2144]{0:T(1024)S(1)} %get-tuple-element.18.list_ref, s32[4]{0:T(128)S(1)} %get-tuple-element.19.count_ref, f32[27,8,128]{2,1,0:T(8,128)S(1)} %get-tuple-element.20.off_ref, f32[40,8,128]{2,1,0:T(8,128)S(1)} %pad_maximum_fusion.own_ref, f32[40,8,128]{2,1,0:T(8,128)S(1)} %collective-permute-done.3.far_ref), custom_call_target="tpu_custom_call" | custom-call | flops 878182400 | bytes 1048576 | tf_op jit(solution)/shard_map/pallas_call | solution.py:411
  57.1 0.0 collective-permute-done.4.low_ref
  57.2 0.1 collective-permute-done.5.high_ref
  57.3 4.9 %shard_map.99 = (f32[8,4,3,1,128]{4,3,2,1,0:T(1,128)}, f32[8,4,1,128]{3,2,1,0:T(1,128)S(1)}, f32[1,128]{1,0:T(1,128)S(1)}) custom-call(s32[1]{0:T(128)} %bitcast.half_ref, s32[2144]{0:T(1024)S(1)} %get-tuple-element.18.list_ref, s32[4]{0:T(128)S(1)} %get-tuple-element.19.count_ref, f32[27,8,128]{2,1,0:T(8,128)S(1)} %get-tuple-element.20.off_ref, ...), custom_call_target="tpu_custom_call" | custom-call | flops 878182400 | bytes 1048576 | tf_op jit(solution)/shard_map/pallas_call | solution.py:425
  62.2 11.9 %all_to_all.14 = f32[16,1,128]{2,1,0:T(1,128)S(1)} all-to-all(f32[16,1,128]{2,1,0:T(1,128)S(1)} %broadcast_in_dim.24), channel_id=1, replica_groups=mesh['gx'=8,'gy_0'=4,'gy_1'=2,'gz_0'=4,'gz_1'=2] {'gz_0','gy_0'}, dimensions={0} | all-to-all | bytes 16384 | tf_op jit(solution)/shard_map/all_to_all | solution.py:496
  74.1 21.2 %all_to_all.15 = f32[32,1,128]{2,1,0:T(1,128)S(1)} all-to-all(f32[32,1,128]{2,1,0:T(1,128)S(1)} %broadcast_in_dim.25), channel_id=1, replica_groups=mesh['gx'=8,'gy_0'=4,'gy_1'=2,'gz_0'=4,'gz_1'=2] {'gx','gz_1','gy_1'}, dimensions={0} | all-to-all | bytes 32768 | tf_op jit(solution)/shard_map/all_to_all | solution.py:496
  95.3 0.7 shard_map.100
  (20 shorter events, 0.2 us)
Async XLA Ops:
  0.6 18.1 %copy-start.2 = (f32[8,4,1,3,128]{4,2,3,1,0:T(1,128)S(1)}, f32[8,4,1,3,128]{4,2,3,1,0:T(1,128)}, u32[]{:S(2)}) copy-start(f32[8,4,1,3,128]{4,2,3,1,0:T(1,128)} %param.9) | copy-start | bytes 147460
  0.6 18.1 %copy-start.3 = (s32[8,4,1,2,128]{4,3,2,1,0:T(2,128)S(1)}, s32[8,4,1,2,128]{4,3,2,1,0:T(2,128)}, u32[]{:S(2)}) copy-start(s32[8,4,1,2,128]{4,3,2,1,0:T(2,128)} %desc_ref.1) | copy-start | bytes 98308
  0.7 18.1 %copy-start.6 = (s32[486]{0:T(512)S(1)}, s32[486]{0:T(512)}, u32[]{:S(2)}) copy-start(s32[486]{0:T(512)} %constant.15.clone.table_ref) | copy-start | bytes 5836
  2.3 16.5 %copy-start.4 = (s32[8,4,1,14]{3,2,1,0:T(1,128)S(1)}, s32[8,4,1,14]{3,2,1,0:T(1,128)}, u32[]{:S(2)}) copy-start(s32[8,4,1,14]{3,2,1,0:T(1,128)} %nbr_ref.1) | copy-start | bytes 5380
  2.3 26.8 %collective-permute-start = (f32[28,8,128]{2,1,0:T(8,128)}, f32[28,8,128]{2,1,0:T(8,128)S(1)}, u32[]{:S(2)}, u32[]{:S(2)}) collective-permute-start(f32[28,8,128]{2,1,0:T(8,128)} %get-tuple-element.22), channel_id=1, source_target_pairs={{0,1},{1,0},{2,3},{3,2},{4,5},{5,4},{6,7},{7,6},{8,9},{9,8},{10,11... | collective-permute-start | bytes 344072 | tf_op jit(solution)/shard_map/ppermute | solution.py:464
  18.7 0.7 copy-start
  19.4 0.9 copy-start.1
  20.3 0.9 copy-start.5
  29.2 11.6 %collective-permute-start.2 = (f32[2,4,8,128]{3,2,1,0:T(8,128)S(1)}, f32[2,4,8,128]{3,2,1,0:T(8,128)S(1)}, u32[]{:S(2)}, u32[]{:S(2)}) collective-permute-start(f32[2,4,8,128]{3,2,1,0:T(8,128)S(1)} %maximum_select_fusion.1), channel_id=1, source_target_pairs={{0,449},{64,0},{128,64},{192,128},{256,192},{320,256},{384,320},{4... | collective-permute-start | bytes 98312 | tf_op jit(solution)/shard_map/ppermute | solution.py:476
  34.2 6.5 %collective-permute-start.1 = (f32[2,4,8,128]{3,2,1,0:T(8,128)S(1)}, f32[2,4,8,128]{3,2,1,0:T(8,128)S(1)}, u32[]{:S(2)}, u32[]{:S(2)}) collective-permute-start(f32[2,4,8,128]{3,2,1,0:T(8,128)S(1)} %maximum_select_fusion), channel_id=1, source_target_pairs={{0,64},{64,128},{128,192},{192,256},{256,320},{320,384},{384,448},... | collective-permute-start | bytes 98312 | tf_op jit(solution)/shard_map/ppermute | solution.py:475
  40.8 7.7 %collective-permute-start.3 = (f32[40,8,128]{2,1,0:T(8,128)S(1)}, f32[40,8,128]{2,1,0:T(8,128)S(1)}, u32[]{:S(2)}, u32[]{:S(2)}) collective-permute-start(f32[40,8,128]{2,1,0:T(8,128)S(1)} %bitcast_dynamic-update-slice_fusion.other_ref), channel_id=1, source_target_pairs={{0,2},{1,7},{2,4},{3,1},{4,6},{5,3},{6,0},{7,5},{8,10},{9,15},{10,... | collective-permute-start | bytes 491528 | tf_op jit(solution)/shard_map/ppermute | solution.py:484
  48.5 8.7 %collective-permute-start.4 = (f32[3,10,8,128]{3,2,1,0:T(8,128)S(1)}, f32[3,10,8,128]{3,2,1,0:T(8,128)S(1)}, u32[]{:S(2)}, u32[]{:S(2)}) collective-permute-start(f32[3,10,8,128]{3,2,1,0:T(8,128)S(1)} %pad_maximum_fusion.1), channel_id=1, source_target_pairs={{0,8},{8,16},{16,24},{24,32},{32,40},{40,48},{48,56},{56,0},{1,9},... | collective-permute-start | bytes 368648 | tf_op jit(solution)/shard_map/ppermute | solution.py:487
  53.0 4.3 %collective-permute-start.5 = (f32[3,10,8,128]{3,2,1,0:T(8,128)S(1)}, f32[3,10,8,128]{3,2,1,0:T(8,128)S(1)}, u32[]{:S(2)}, u32[]{:S(2)}) collective-permute-start(f32[3,10,8,128]{3,2,1,0:T(8,128)S(1)} %pad_maximum_fusion.2), channel_id=1, source_target_pairs={{0,56},{8,0},{16,8},{24,16},{32,24},{40,32},{48,40},{56,48},{1,57}... | collective-permute-start | bytes 368648 | tf_op jit(solution)/shard_map/ppermute | solution.py:488
